TPU v7x, 32 devices: a whole 2x2x4 slice. The times are simulated.
32 devices in a mesh: tile: 16 (over z, y, x), depth: 2 (over core).
Axes of the slice: x: 2, y: 2, z: 4, core: 2. Of those that a mesh axis runs over, the one named last changes fastest.
Arguments:
- density: float32 [64, 256, 256], P('depth', 'tile'), may hold values from -6 to 6
- absorption: float32 [256, 256], P('tile'), may hold values from 0.25 to 32
- view_dir: int32 [256], P('tile'), may hold values 0 or 1
- target_ids: int32 [256, 256], P('tile'), may hold values from 0 to 127
- palette: float32 [3, 128], replicated, may hold values from -3 to 3
- emission_coef: float32 [3, 4], replicated, may hold values from -3 to 3
- light: float32 [3], replicated, may hold values from -4 to 4
Outputs:
- image: float32 [3, 256, 256], P(None, ('tile', 'depth'))
- density_grad: float32 [64, 256, 256], P('depth', 'tile')
All inputs are finite; a program needn't handle non-finite values. No bound on the sum of `view_dir` on one device may be relied on, other than what follows from the above.
Results may differ from a plain program's by a relative error of at most 0.00023.
Values sent between devices are 32-bit elements; how exact they have to be, the bound alone decides.
No kernel may reach another device: no remote copies, remote signals or barrier semaphores. Data moves between devices by JAX's collectives and lax.ppermute only.
A program may use at most 64 MiB of HBM per device.

v0:
```python
import jax
import jax.numpy as jnp
from jax import lax
from jax.sharding import PartitionSpec as P


def extended(cells, sides, width):
    for axis, dim in sides:
        count = lax.axis_size(axis)
        ends = count - 1
        head = lax.slice_in_dim(cells, 0, width, axis=dim)
        tail = lax.slice_in_dim(cells, cells.shape[dim] - width, cells.shape[dim], axis=dim)
        cells = jnp.concatenate(
            [
                lax.ppermute(tail, axis, [(i, (i + 1) % count) for i in range(ends)]),
                cells,
                lax.ppermute(head, axis, [((i + 1) % count, i) for i in range(ends)]),
            ],
            axis=dim,
        )
    return cells


def smooth_field(ext):
    core = ext[1:-1, 1:-1]
    total = 2.0 * core + ext[2:, 1:-1] + ext[:-2, 1:-1] + ext[1:-1, 2:] + ext[1:-1, :-2]
    total = total + jnp.roll(core, -1, 2) + jnp.roll(core, 1, 2)
    return total / 8.0


def shade_parts(padded, absorption, emission_coef, light, depth_count):
    smoothed = smooth_field(padded)
    centre = smoothed[1:-1, 1:-1]
    grad_z = 0.5 * (smoothed[2:, 1:-1] - smoothed[:-2, 1:-1])
    grad_y = 0.5 * (smoothed[1:-1, 2:] - smoothed[1:-1, :-2])
    grad_x = 0.5 * (jnp.roll(centre, -1, 2) - jnp.roll(centre, 1, 2))
    facing = grad_z * light[0] + grad_y * light[1] + grad_x * light[2]
    shade = 0.5 + 0.5 * facing / jnp.sqrt(1.0 + grad_z * grad_z + grad_y * grad_y + grad_x * grad_x)
    value = (
        emission_coef[:, 3][:, None, None, None] * centre[None]
        + emission_coef[:, 2][:, None, None, None]
    )
    value = value * centre[None] + emission_coef[:, 1][:, None, None, None]
    value = value * centre[None] + emission_coef[:, 0][:, None, None, None]
    emission = value * shade[None]
    sigma = absorption[None] * jax.nn.softplus(centre) / depth_count
    return (emission, sigma)


def lookup_target(target_ids, palette):
    rows, cols = target_ids.shape
    entries = palette.shape[1]
    onehot = (
        target_ids.reshape(1, rows * cols) == jnp.arange(entries, dtype=jnp.int32)[:, None]
    ).astype(jnp.float32)
    return jnp.dot(palette, onehot, precision=lax.Precision.HIGHEST).reshape(3, rows, cols)


def shards(density, absorption, view_dir, target_ids, palette, emission_coef, light):
    slab, rows, cols = density.shape
    depth_count = slab * lax.axis_size("depth")
    position = lax.axis_index("depth")
    share = rows // lax.axis_size("depth")
    columns = lax.all_to_all(density, "depth", split_axis=1, concat_axis=0, tiled=True)
    ext = extended(columns, ((("tile", "depth"), 1),), 2)
    start = position * share
    absorb_rows = lax.dynamic_slice_in_dim(absorption, start, share, 0)
    view_rows = lax.dynamic_slice_in_dim(view_dir, start, share, 0)
    target_rows = lax.dynamic_slice_in_dim(target_ids, start, share, 0)
    flipped_rows = (view_rows == 1)[None, :, None]

    def column_render(field):
        padded = jnp.pad(field, ((2, 2), (0, 0), (0, 0)))
        emission, sigma = shade_parts(padded, absorb_rows, emission_coef, light, depth_count)
        ascending = jnp.cumsum(sigma, 0) - sigma
        total = jnp.sum(sigma, 0)
        descending = total[None] - ascending - sigma
        depth_before = jnp.where(flipped_rows, descending, ascending)
        weight = jnp.exp(-depth_before) * (1.0 - jnp.exp(-sigma))
        return jnp.sum(emission * weight[None], 1)

    image_rows, pullback = jax.vjp(column_render, ext)
    target = lookup_target(target_rows, palette)
    (grad_ext,) = pullback((image_rows - target) * depth_count)
    edges = jnp.concatenate([grad_ext[:, :2], grad_ext[:, -2:]], 1)
    arrived = extended(edges, ((("tile", "depth"), 1),), 2)
    inner = grad_ext[:, 2:-2]
    inner = jnp.concatenate(
        [inner[:, :2] + arrived[:, :2], inner[:, 2:-2], inner[:, -2:] + arrived[:, -2:]], 1
    )
    density_grad = lax.all_to_all(inner, "depth", split_axis=0, concat_axis=1, tiled=True)
    return (image_rows, density_grad)


def solution(mesh):
    placed = (P("depth", "tile", None), P("tile", None), P("tile"), P("tile", None), P(), P(), P())
    return jax.shard_map(
        shards,
        mesh=mesh,
        in_specs=placed,
        out_specs=(P(None, ("tile", "depth"), None), P("depth", "tile", None)),
        check_vma=False,
    )
```

profile of v0, /device:TPU:7, one launch (start us, length us, event | category | flops | bytes accessed | tf_op | source)
XLA Modules:
  0.0 49.1 jit_solution(7746812675933893874)
XLA Ops:
  0.6 1.4 %copy.14 = f32[32,16,256]{2,0,1:T(8,128)S(1)} copy(f32[32,16,256]{2,1,0:T(8,128)} %param.7) | data formatting | bytes 1048576 | tf_op args[0]
  2.0 4.5 %all_to_all.36 = f32[32,16,256]{2,0,1:T(8,128)S(1)} all-to-all(f32[32,16,256]{2,0,1:T(8,128)S(1)} %copy.14), channel_id=1, replica_groups=mesh['tile'=16,'depth'=2] {'depth'}, dimensions={1} | all-to-all | bytes 1048576 | tf_op jit(solution)/shard_map/all_to_all | solution.py:64
  6.5 0.3 copy.15
  6.9 3.4 %collective-permute-start = (f32[64,2,256]{2,1,0:T(2,128)S(1)}, f32[64,2,256]{2,1,0:T(2,128)S(1)}, u32[]{:S(2)}, u32[]{:S(2)}) collective-permute-start(f32[64,2,256]{2,1,0:T(2,128)S(1)} %get-tuple-element.49), channel_id=1, source_target_pairs={{0,1},{1,2},{2,3},{3,4},{4,5},{5,6},{6,7},{7,8},{8,9},{9,10},{10,1... | collective-permute-start | bytes 393224 | tf_op jit(solution)/shard_map/ppermute | solution.py:15
  10.3 1.9 %collective-permute-start.1 = (f32[64,2,256]{2,1,0:T(2,128)S(1)}, f32[64,2,256]{2,1,0:T(2,128)S(1)}, u32[]{:S(2)}, u32[]{:S(2)}) collective-permute-start(f32[64,2,256]{2,1,0:T(2,128)S(1)} %get-tuple-element.50), channel_id=1, source_target_pairs={{1,0},{2,1},{3,2},{4,3},{5,4},{6,5},{7,6},{8,7},{9,8},{10,9},{11,1... | collective-permute-start | bytes 393224 | tf_op jit(solution)/shard_map/ppermute | solution.py:17
  12.2 0.6 %fusion.48 = (f32[1]{0:T(128)}, f32[1]{0:T(128)}, f32[1]{0:T(128)}) fusion(f32[3]{0:T(128)S(1)} %copy-done.3), kind=kLoop, calls=%fused_computation.104 | loop fusion | bytes 24 | tf_op jit(solution)/shard_map/jvp()/slice | solution.py:37
  12.8 0.2 slice_reduce_fusion.3
  13.1 0.4 fusion.14
  15.5 2.9 %collective-permute-done.1 = f32[64,2,256]{2,1,0:T(2,128)S(1)} collective-permute-done((f32[64,2,256]{2,1,0:T(2,128)S(1)}, f32[64,2,256]{2,1,0:T(2,128)S(1)}, u32[]{:S(2)}, u32[]{:S(2)}) %collective-permute-start.1) | collective-permute-done | bytes 131104 | tf_op jit(solution)/shard_map/ppermute | solution.py:17
  18.8 0.4 fusion.41
  19.2 0.7 %fusion.13 = f32[66,10,256]{2,1,0:T(8,128)S(1)} fusion(f32[68,12,256]{2,1,0:T(8,128)S(1)} %select_maximum_fusion, f32[66,10,1]{2,1,0:T(8,128)S(1)} %get-tuple-element.31, f32[66,10,255]{2,1,0:T(8,128)S(1)} %get-tuple-element.33, f32[66,10,255]{2,1,0:T(8,128)S(1)} %get-tuple-element.32, f32[66,10,1]{2,1,0:T(8,128)S(1)} %get-tuple-element.30), kind=kLoop, calls=%fused_computation.28 | loop fusion | flops 1689600 | bytes 5406720 | tf_op jit(solution)/shard_map/jvp()/div | solution.py:28
  19.9 0.4 fusion.33
  20.2 0.4 fusion.32
  21.0 1.2 %fusion.44 = (f32[64,8,256]{2,1,0:T(8,128)S(1)}, f32[64,8,256]{2,1,0:T(8,128)S(1)}, f32[64,8,256]{2,1,0:T(8,128)S(1)}, f32[64,8,256]{2,1,0:T(8,128)S(1)}, f32[64...) fusion(f32[66,10,256]{2,1,0:T(8,128)S(1)} %fusion.13, f32[64,8,256]{2,1,0:T(8,128)S(1)} %fusion.32, ...), kind=kLoop, calls=%fused_computation.100 | loop fusion | flops 4980736 | bytes 7356436 | tf_op jit(solution)/shard_map/jvp()/slice | solution.py:33
  22.2 0.5 %multiply_reduce_fusion.1 = f32[3,8,256]{2,1,0:T(8,128)S(1)} fusion(f32[64,8,256]{2,1,0:T(8,128)S(1)} %get-tuple-element.40, f32[64,8,256]{2,1,0:T(8,128)S(1)} %get-tuple-element.41, f32[3]{0:T(128)S(1)} %get-tuple-element.9, f32[3]{0:T(128)S(1)} %get-tuple-element.10, f32[3]{0:T(128)S(1)} %get-tuple-element.8, f32[64,8,256]{2,1,0:T(8,128)S(1)} %get-tuple-element.39, ...), kind=kLoop, calls=%fused_computation.14 | loop fusion | flops 3532800 | bytes 1597488 | tf_op jit(solution)/shard_map/jvp()/reduce_sum | solution.py:80
  22.8 1.2 %fusion.7 = (f32[64,8,256]{2,1,0:T(8,128)S(1)}, f32[64,8,256]{2,1,0:T(8,128)S(1)}, f32[64,8,256]{2,1,0:T(8,128)S(1)}, f32[64,8,256]{2,1,0:T(8,128)S(1)}, f32[64,8,256]{2,1,0:T(8,128)S(1)}) fusion(f32[3,8,256]{2,1,0:T(8,128)S(1)} %fusion.30, f32[64,8,256]{2,1,0:T(8,128)S(1)} %get-tuple-element.40, f32[64,8,256]{2,1,0:T(8,128)S(1)} %get-tuple-element.41, ...), kind=kLoop, calls=%fused_computation.11 | loop fusion | flops 7602176 | bytes 4218928 | tf_op jit(solution)/shard_map/transpose(jvp())/reduce_sum | solution.py:44
  24.0 0.3 fusion.34
  24.4 0.9 %fusion.36 = (f32[64,8,256]{2,1,0:T(8,128)S(1)}, f32[64,8,256]{2,1,0:T(8,128)S(1)}, f32[64,8,256]{2,1,0:T(8,128)S(1)}, f32[64,8,256]{2,1,0:T(8,128)S(1)}, f32[8,256]{1,0:T(8,128)S(1)}) fusion(f32[]{:T(128)} %bitcast.4, f32[64,8,256]{2,1,0:T(8,128)S(1)} %get-tuple-element.6, f32[64,8,256]{2,1,0:T(8,128)S(1)} %get-tuple-element.42, ...), kind=kLoop, calls=%fused_computation.94 | loop fusion | flops 4716544 | bytes 6840336 | tf_op jit(solution)/shard_map/transpose(jvp())/neg | solution.py:34
  25.6 2.3 %fusion.22 = f32[64,8,256]{2,1,0:T(8,128)S(1)} fusion(f32[64,8,256]{2,1,0:T(8,128)S(1)} %get-tuple-element.4, f32[64,8,256]{2,1,0:T(8,128)S(1)} %get-tuple-element.3, f32[64,8,256]{2,1,0:T(8,128)S(1)} %get-tuple-element.2, f32[64,8,255]{2,1,0:T(8,128)S(1)} %bitcast.24, f32[64,8,1]{2,1,0:T(8,128)S(1)} %split.42, f32[64,8,1]{2,1,0:T(8,128)S(1)} %split.41, ...), kind=kOutput, calls=%fused_computation.45 | output fusion | flops 17039360 | bytes 6865920 | tf_op jit(solution)/shard_map/transpose(jvp(jit(cumsum)))/reduce_window_sum | solution.py:75
  28.0 0.5 %broadcast_multiply_fusion = f32[66,10,256]{2,1,0:T(8,128)S(1)} fusion(f32[64,8,256]{2,1,0:T(8,128)S(1)} %fusion.22, f32[64,8,256]{2,1,0:T(8,128)S(1)} %get-tuple-element.19, f32[64,8,256]{2,1,0:T(8,128)S(1)} %get-tuple-element.18, f32[64,8,256]{2,1,0:T(8,128)S(1)} %get-tuple-element.16, f32[64,8,256]{2,1,0:T(8,128)S(1)} %get-tuple-element.15), kind=kLoop, calls=%fused_computation.37 | loop fusion | flops 844800 | bytes 3297280 | tf_op jit(solution)/shard_map/transpose(jvp())/div | solution.py:28
  28.7 0.4 fusion.42
  29.1 0.9 %multiply_add_fusion.3 = f32[66,10,256]{2,1,0:T(8,128)S(1)} fusion(f32[66,10,255]{2,1,0:T(8,128)S(1)} %get-tuple-element.35, f32[66,10,1]{2,1,0:T(8,128)S(1)} %get-tuple-element.37, f32[66,10,1]{2,1,0:T(8,128)S(1)} %get-tuple-element.36, f32[66,10,255]{2,1,0:T(8,128)S(1)} %get-tuple-element.34, f32[64,8,256]{2,1,0:T(8,128)S(1)} %fusion.22, ...), kind=kLoop, calls=%fused_computation.33 | loop fusion | flops 1520640 | bytes 4648960 | tf_op jit(solution)/shard_map/transpose(jvp())/add_any | solution.py:26
  30.0 0.2 pad_add_fusion.6
  30.2 2.6 %collective-permute-start.2 = (f32[64,2,256]{2,1,0:T(2,128)S(1)}, f32[64,2,256]{2,1,0:T(2,128)S(1)}, u32[]{:S(2)}, u32[]{:S(2)}) collective-permute-start(f32[64,2,256]{2,1,0:T(2,128)S(1)} %get-tuple-element.13), channel_id=1, source_target_pairs={{0,1},{1,2},{2,3},{3,4},{4,5},{5,6},{6,7},{7,8},{8,9},{9,10},{10,1... | collective-permute-start | bytes 393224 | tf_op jit(solution)/shard_map/ppermute | solution.py:15
  32.8 1.9 %collective-permute-done.2 = f32[64,2,256]{2,1,0:T(2,128)S(1)} collective-permute-done((f32[64,2,256]{2,1,0:T(2,128)S(1)}, f32[64,2,256]{2,1,0:T(2,128)S(1)}, u32[]{:S(2)}, u32[]{:S(2)}) %collective-permute-start.2) | collective-permute-done | bytes 131104 | tf_op jit(solution)/shard_map/ppermute | solution.py:15
  34.8 0.2 add_add_fusion.1
  35.2 1.9 %collective-permute-start.3 = (f32[64,2,256]{2,1,0:T(2,128)S(1)}, f32[64,2,256]{2,1,0:T(2,128)S(1)}, u32[]{:S(2)}, u32[]{:S(2)}) collective-permute-start(f32[64,2,256]{2,1,0:T(2,128)S(1)} %pad_add_fusion.2), channel_id=1, source_target_pairs={{1,0},{2,1},{3,2},{4,3},{5,4},{6,5},{7,6},{8,7},{9,8},{10,9},{11,1... | collective-permute-start | bytes 393224 | tf_op jit(solution)/shard_map/ppermute | solution.py:17
  37.1 0.2 pad_add_fusion.1
  37.4 6.6 %collective-permute-done.3 = f32[64,2,256]{2,1,0:T(2,128)S(1)} collective-permute-done((f32[64,2,256]{2,1,0:T(2,128)S(1)}, f32[64,2,256]{2,1,0:T(2,128)S(1)}, u32[]{:S(2)}, u32[]{:S(2)}) %collective-permute-start.3) | collective-permute-done | bytes 131104 | tf_op jit(solution)/shard_map/ppermute | solution.py:17
  44.0 0.3 add_add_fusion
  44.4 3.8 %all_to_all.37 = f32[64,8,256]{2,1,0:T(8,128)S(1)} all-to-all(f32[64,8,256]{2,1,0:T(8,128)S(1)} %pad_maximum_fusion), channel_id=1, replica_groups=mesh['tile'=16,'depth'=2] {'depth'}, dimensions={0} | all-to-all | bytes 1048576 | tf_op jit(solution)/shard_map/all_to_all | solution.py:91
  48.2 0.9 %copy.21 = f32[32,2,8,256]{3,2,1,0:T(8,128)} copy(f32[32,2,8,256]{3,2,0,1:T(8,128)S(1)} %bitcast.28) | data formatting | bytes 1048576 | tf_op jit(solution)/shard_map/all_to_all | solution.py:91
  (31 shorter events, 1.9 us)
Async XLA Ops:
  0.6 12.4 %copy-start = (s32[16,256]{1,0:T(8,128)S(1)}, s32[16,256]{1,0:T(8,128)}, u32[]{:S(2)}) copy-start(s32[16,256]{1,0:T(8,128)} %param.10) | copy-start | bytes 49156
  2.0 10.2 %copy-start.3 = (f32[3]{0:T(128)S(1)}, f32[3]{0:T(128)}, u32[]{:S(2)}) copy-start(f32[3]{0:T(128)} %param.13) | copy-start | bytes 40
  2.0 10.8 %copy-start.2 = (f32[3,4]{1,0:T(4,128)S(1)}, f32[3,4]{1,0:T(4,128)}, u32[]{:S(2)}) copy-start(f32[3,4]{1,0:T(4,128)} %param.12) | copy-start | bytes 148
  6.5 6.6 %copy-start.5 = (f32[3,128]{1,0:T(4,128)S(1)}, f32[3,128]{1,0:T(4,128)}, u32[]{:S(2)}) copy-start(f32[3,128]{1,0:T(4,128)} %param.11) | copy-start | bytes 4612
  6.5 7.0 %copy-start.6 = (s32[16]{0:T(128)S(1)}, s32[16]{0:T(128)}, u32[]{:S(2)}) copy-start(s32[16]{0:T(128)} %param.9) | copy-start | bytes 196
  6.5 9.0 %copy-start.4 = (f32[16,256]{1,0:T(8,128)S(1)}, f32[16,256]{1,0:T(8,128)}, u32[]{:S(2)}) copy-start(f32[16,256]{1,0:T(8,128)} %param.8) | copy-start | bytes 49156
  6.9 8.6 %collective-permute-start = (f32[64,2,256]{2,1,0:T(2,128)S(1)}, f32[64,2,256]{2,1,0:T(2,128)S(1)}, u32[]{:S(2)}, u32[]{:S(2)}) collective-permute-start(f32[64,2,256]{2,1,0:T(2,128)S(1)} %get-tuple-element.49), channel_id=1, source_target_pairs={{0,1},{1,2},{2,3},{3,4},{4,5},{5,6},{6,7},{7,8},{8,9},{9,10},{10,1... | collective-permute-start | bytes 393224 | tf_op jit(solution)/shard_map/ppermute | solution.py:15
  10.3 8.1 %collective-permute-start.1 = (f32[64,2,256]{2,1,0:T(2,128)S(1)}, f32[64,2,256]{2,1,0:T(2,128)S(1)}, u32[]{:S(2)}, u32[]{:S(2)}) collective-permute-start(f32[64,2,256]{2,1,0:T(2,128)S(1)} %get-tuple-element.50), channel_id=1, source_target_pairs={{1,0},{2,1},{3,2},{4,3},{5,4},{6,5},{7,6},{8,7},{9,8},{10,9},{11,1... | collective-permute-start | bytes 393224 | tf_op jit(solution)/shard_map/ppermute | solution.py:17
  22.8 1.3 %copy-start.1 = (f32[3,8,256]{2,1,0:T(8,128)}, f32[3,8,256]{2,1,0:T(8,128)S(1)}, u32[]{:S(2)}) copy-start(f32[3,8,256]{2,1,0:T(8,128)S(1)} %multiply_reduce_fusion.1) | copy-start | bytes 73732
  30.2 4.5 %collective-permute-start.2 = (f32[64,2,256]{2,1,0:T(2,128)S(1)}, f32[64,2,256]{2,1,0:T(2,128)S(1)}, u32[]{:S(2)}, u32[]{:S(2)}) collective-permute-start(f32[64,2,256]{2,1,0:T(2,128)S(1)} %get-tuple-element.13), channel_id=1, source_target_pairs={{0,1},{1,2},{2,3},{3,4},{4,5},{5,6},{6,7},{7,8},{8,9},{9,10},{10,1... | collective-permute-start | bytes 393224 | tf_op jit(solution)/shard_map/ppermute | solution.py:15
  35.2 8.8 %collective-permute-start.3 = (f32[64,2,256]{2,1,0:T(2,128)S(1)}, f32[64,2,256]{2,1,0:T(2,128)S(1)}, u32[]{:S(2)}, u32[]{:S(2)}) collective-permute-start(f32[64,2,256]{2,1,0:T(2,128)S(1)} %pad_add_fusion.2), channel_id=1, source_target_pairs={{1,0},{2,1},{3,2},{4,3},{5,4},{6,5},{7,6},{8,7},{9,8},{10,9},{11,1... | collective-permute-start | bytes 393224 | tf_op jit(solution)/shard_map/ppermute | solution.py:17
where the time goes:
time: 49.4 us; the launch traced here: 49.1 us
  waiting for transfers between devices  11.4 us (23%)
  other arithmetic  11.1 us (22%)
  starting transfers between devices  9.8 us (20%)
  blocking collectives  8.25 us (17%)
  local copies, waits for them, and re-layouts  5.34 us (11%)
  between operations  2.8 us (6%)
    ppermute x2, waiting for transfers between devices, extended(): lax.ppermute(head, axis, [((i + 1) % count, i) for i in range(ends)])  9.49 us
    ppermute x2, starting transfers between devices, extended(): lax.ppermute(tail, axis, [(i, (i + 1) % count) for i in range(ends)])  5.96 us
    all_to_all x1, blocking collectives, shards(): lax.all_to_all(density, 'depth', split_axis=1, concat_axis=0, tiled=True)  4.46 us
    ppermute x2, starting transfers between devices, extended(): lax.ppermute(head, axis, [((i + 1) % count, i) for i in range(ends)])  3.84 us
    all_to_all x1, blocking collectives, shards(): lax.all_to_all(inner, 'depth', split_axis=0, concat_axis=1, tiled=True)  3.79 us
    another operation x2, other arithmetic, column_render(): ascending = jnp.cumsum(sigma, 0) - sigma  2.77 us
    ppermute x2, waiting for transfers between devices, extended(): lax.ppermute(tail, axis, [(i, (i + 1) % count) for i in range(ends)])  1.93 us
    unnamed x17, local copies, waits for them, and re-layouts  1.41 us
  transfers between devices with their start and end apart: 4, of which 3 were waited for; matrix products, arithmetic and copies ran while one was open for 3% of the time, Pallas kernels for 0%

commit v1 on v0

v1 whole, which is shorter than its diff:
```python
import functools

import jax
import jax.numpy as jnp
from jax import lax
from jax.experimental import pallas as pl
from jax.experimental.pallas import tpu as pltpu
from jax.sharding import PartitionSpec as P

F32 = jnp.float32
HALO = 4
PIX = 3
VMEM = pl.BlockSpec(memory_space=pltpu.VMEM)
SMEM = pl.BlockSpec(memory_space=pltpu.SMEM)


def call(kernel, outs, args, specs, scratch=(), cost=None):
    args = [pltpu.with_memory_space_constraint(a, pltpu.VMEM) if s is VMEM else a for a, s in zip(args, specs)]
    return pl.pallas_call(
        kernel,
        out_shape=outs,
        in_specs=specs,
        out_specs=jax.tree.map(lambda _: VMEM, outs),
        scratch_shapes=scratch,
        cost_estimate=cost,
        compiler_params=pltpu.CompilerParams(vmem_limit_bytes=8 << 20),
    )(*args)


def resident(*shape):
    return pltpu.VMEM(shape, F32)


def where_am_i():
    return lax.axis_index("depth"), lax.rem(lax.axis_index("tile"), 2)


def local_plane(core, nz, z):
    return jnp.where(core == 0, z, nz - 1 - z)


def prep_kernel(dens, absorb, ids, view, zmsg, xmsg, lmsg, pix):
    nz, rows, cols = dens.shape
    core, odd = where_am_i()
    row = lax.broadcasted_iota(jnp.int32, (rows, cols), 0)
    seen = jnp.zeros((rows, cols), F32)
    for r in range(rows):
        seen = jnp.where(row == r, view[r].astype(F32), seen)
    pix[0] = absorb[...]
    pix[1] = ids[...].astype(F32)
    pix[2] = seen

    def edges(plane, x_to, l_to):
        head, tail = plane[:HALO], plane[rows - HALO :]
        xmsg[x_to] = jnp.where(odd == 1, head, tail)
        lmsg[l_to] = jnp.where(odd == 1, tail, head)

    for j in range(nz):
        plane = dens[local_plane(core, nz, nz - 1 - j)]
        edges(plane, j, j)
        if j < HALO:
            zmsg[j] = plane
    for j in range(PIX):
        edges(pix[j], nz + j, nz + j)


def corner_kernel(zrecv, early, lmsg):
    rows = zrecv.shape[1]
    _, odd = where_am_i()
    lmsg[HALO:] = early[...]
    for j in range(HALO):
        plane = zrecv[HALO - 1 - j]
        lmsg[j] = jnp.where(odd == 1, plane[rows - HALO :], plane[:HALO])


def lookup(palette, ids):
    rows, cols = ids.shape
    entries = palette.shape[1]
    index = ids.astype(jnp.int32)
    parts = []
    for c in range(3):
        strips = []
        for r in range(0, rows, 8):
            strip = []
            for x in range(0, cols, entries):
                table = jnp.broadcast_to(palette[c : c + 1, :], (8, entries))
                strip.append(jnp.take_along_axis(table, index[r : r + 8, x : x + entries], axis=1))
            strips.append(jnp.concatenate(strip, axis=1))
        parts.append(jnp.concatenate(strips, axis=0))
    return parts


def forward_block(band, depth, own, halo, shift, light, coef, out):
    core, _ = where_am_i()
    wide = band + 8
    smooth, dxs, dys, rnorm, phis, edge, sig, taus, mid, pixo = out

    def gather(o, h):
        return pltpu.roll(jnp.concatenate([o, h, h], axis=0), shift, axis=0)

    a, ids, view = [gather(own(-1 - j), halo(-1 - j))[:band] for j in range(PIX)]
    back = jnp.where(core == 0, view, 1.0 - view)
    sign = 1.0 - 2.0 * back
    scale = a * (1.0 / (2 * depth))
    pixo[0] = a
    pixo[1] = ids
    pixo[2] = back
    signed = scale * sign

    def smoothing(before, here, after):
        t = before + after + 2.0 * here
        t = t + pltpu.roll(here, 1, axis=0) + pltpu.roll(here, wide - 1, axis=0)
        cols = here.shape[1]
        t = t + pltpu.roll(here, 1, axis=1) + pltpu.roll(here, cols - 1, axis=1)
        return t * 0.125

    def optical(z, s):
        e = jnp.exp(s)
        soft = jnp.log(1.0 + e)
        sig[z] = 1.0 - jnp.exp(-soft)
        tau = signed * soft
        taus[z] = tau
        return tau

    first = gather(own(0), halo(0))
    zero = jnp.zeros_like(first)
    smooth[0] = first * 0.125

    def smooth_step(z, carry):
        before, here, total = carry
        after = gather(own(z + 1), halo(z + 1))
        s = smoothing(before, here, after)
        smooth[z + 1] = s
        return here, after, total + optical(z, s[:band])

    carry = (zero, first, jnp.zeros_like(a))
    carry = lax.fori_loop(0, depth - 1, smooth_step, carry)
    before, here, total = smooth_step_seam(depth - 1, carry, own, halo, gather, smoothing, smooth, optical, band)
    tot = total
    for z in range(depth, depth + 3):
        after = gather(own(z + 1), halo(z + 1))
        s = smoothing(before, here, after)
        smooth[z + 1] = s
        if z < depth + 2:
            optical(z, s[:band])
        before, here = here, after

    start = jnp.where(back == 1.0, tot, 0.0)
    lz = jnp.where(core == 0, light[0], -light[0])
    ly, lx = light[1], light[2]
    first_edge = jnp.exp(start)
    edge[0] = first_edge

    def shade_step(z, carry):
        run, seen, m0, m1, m2, m3 = carry
        wide_s = smooth[z + 1]
        cols = wide_s.shape[1]
        s = wide_s[:band]
        dz = smooth[z + 2, pl.ds(0, band)] - smooth[z, pl.ds(0, band)]
        dy = (pltpu.roll(wide_s, wide - 1, axis=0) - pltpu.roll(wide_s, 1, axis=0))[:band]
        dx = pltpu.roll(s, cols - 1, axis=1) - pltpu.roll(s, 1, axis=1)
        r = lax.rsqrt(4.0 + dz * dz + dy * dy + dx * dx)
        phi = (dz * lz + dy * ly + dx * lx) * r
        dxs[z] = dx
        dys[z] = dy
        rnorm[z] = r
        phis[z] = phi
        run = run - taus[z]
        nxt = jnp.exp(run)
        edge[z + 1] = nxt
        b = (seen - nxt) * (1.0 + phi)
        m0 = m0 + b
        b = b * s
        m1 = m1 + b
        b = b * s
        m2 = m2 + b
        b = b * s
        m3 = m3 + b
        return run, nxt, m0, m1, m2, m3

    nil = jnp.zeros_like(a)
    carry = (start, first_edge, nil, nil, nil, nil)
    carry = lax.fori_loop(0, depth, shade_step, carry)
    _, _, m0, m1, m2, m3 = carry
    half = 0.5 * sign
    mid[0] = sign * tot
    for c in range(3):
        mid[1 + c] = half * (m0 * coef[c, 0] + m1 * coef[c, 1] + m2 * coef[c, 2] + m3 * coef[c, 3])
    shade_step(depth, carry)
    shade_step(depth + 1, (carry[0] - taus[depth], *carry[1:]))


def smooth_step_seam(z, carry, own, halo, gather, smoothing, smooth, optical, band):
    before, here, total = carry
    after = gather(own(z + 1), halo(z + 1))
    s = smoothing(before, here, after)
    smooth[z + 1] = s
    return here, after, total + optical(z, s[:band])


def main_forward_kernel(dens, pix, zrecv, xrecv, xcorner, light, coef, *out):
    nz, rows, cols = dens.shape
    core, odd = where_am_i()

    def own(z):
        if isinstance(z, int):
            if z < 0:
                return pix[-1 - z]
            if z >= nz:
                return zrecv[z - nz]
        return dens[local_plane(core, nz, z)]

    def halo(z):
        if isinstance(z, int):
            if z < 0:
                return xrecv[nz - 1 - z]
            if z >= nz:
                return xcorner[z - nz]
        return xrecv[nz - 1 - z]

    shift = jnp.where(odd == 1, 2, rows + 8 - 2)
    forward_block(rows, nz, own, halo, shift, light, coef, out)


def far_forward_kernel(dens, pix, zrecv, lrecv, light, coef, *out):
    nz, rows, cols = dens.shape
    core, odd = where_am_i()
    at = pl.multiple_of(odd * (rows - 8), 8)

    def own(z):
        if isinstance(z, int):
            if z < 0:
                return pix[-1 - z, pl.ds(at, 8)]
            if z >= nz:
                return zrecv[z - nz, pl.ds(at, 8)]
        return dens[local_plane(core, nz, z), pl.ds(at, 8)]

    def halo(z):
        if isinstance(z, int) and z < 0:
            return lrecv[nz + HALO - 1 - z]
        return lrecv[nz + HALO - 1 - z]

    shift = jnp.where(odd == 1, 16 - 2, 2)
    forward_block(8, nz, own, halo, shift, light, coef, out)


def backward_block(band, depth, res, theirs, palette, light, coef, grads, image, emit):
    core, _ = where_am_i()
    smooth, dxs, dys, rnorm, phis, edge, sig, taus, mid, pixo = res
    back = pixo[2] == 1.0
    sign = jnp.where(back, -1.0, 1.0)
    mine_total, their_total = mid[0], theirs[0]
    through_me, through_them = jnp.exp(-mine_total), jnp.exp(-their_total)
    target = lookup(palette, pixo[1])
    g, flow = [], jnp.zeros_like(sign)
    for c in range(3):
        mine, other = mid[1 + c], theirs[1 + c]
        pic = jnp.where(back, other + through_them * mine, mine + through_me * other)
        image[c] = pic
        err = (pic - target[c]) * (2.0 * depth)
        g.append(err)
        flow = flow + err * pic
    kappa = jnp.where(back, 0.5 * through_them, 0.5)
    gam = [kappa * (g[0] * coef[0, k] + g[1] * coef[1, k] + g[2] * coef[2, k]) for k in range(4)]
    gam2, gam3 = 2.0 * gam[2], 3.0 * gam[3]
    queue = jnp.where(back, 0.0, -flow)
    weight = pixo[0] * (1.0 / (2 * depth))
    lz = jnp.where(core == 0, light[0], -light[0])
    ly, lx = light[1], light[2]

    def shade_back(z, carry):
        run, part, last = carry
        s = smooth[z + 1, pl.ds(0, band)]
        cols = s.shape[1]
        dz = smooth[z + 2, pl.ds(0, band)] - smooth[z, pl.ds(0, band)]
        phi, r, near, far = phis[z], rnorm[z], edge[z], edge[z + 1]
        shade = 1.0 + phi
        poly = gam[0] + s * (gam[1] + s * (gam[2] + s * gam[3]))
        slope = gam[1] + s * (gam2 + s * gam3)
        h = shade * poly
        lost = near - far
        w = sign * lost
        mine = (near * h + run) * (weight * sig[z]) + (w * shade) * slope
        run = run + lost * h
        t1 = w * poly * r
        t3 = t1 * phi * r
        az = t1 * lz - t3 * dz
        ay = t1 * ly - t3 * dys[z]
        ax = t1 * lx - t3 * dxs[z]
        grads[z] = part - az
        part = mine + last
        part = part + (pltpu.roll(ay, 1, axis=0) - pltpu.roll(ay, band - 1, axis=0))
        part = part + (pltpu.roll(ax, 1, axis=1) - pltpu.roll(ax, cols - 1, axis=1))
        return run, part, az

    nil = jnp.zeros_like(sign)
    lax.fori_loop(0, depth + 2, shade_back, (queue, nil, nil))

    def smooth_back(z, carry):
        here = grads[z + 1]
        cols = here.shape[1]
        t = grads[z] + grads[z + 2] + 2.0 * here
        t = t + pltpu.roll(here, 1, axis=0) + pltpu.roll(here, band - 1, axis=0)
        t = t + pltpu.roll(here, 1, axis=1) + pltpu.roll(here, cols - 1, axis=1)
        emit(z, t * 0.125)
        return carry

    lax.fori_loop(0, depth, smooth_back, 0)


def main_backward_kernel(*refs):
    res, (theirs, palette, light, coef, out, image, grads) = refs[:10], refs[10:]
    nz, rows, cols = out.shape
    core, odd = where_am_i()
    shift = jnp.where(odd == 1, rows - 2, 2)

    def emit(z, value):
        out[local_plane(core, nz, z)] = pltpu.roll(value, shift, axis=0)

    backward_block(rows, nz, res, theirs, palette, light, coef, grads, image, emit)


def far_backward_kernel(*refs):
    res = refs[:10]
    theirs, palette, light, coef, near_grad, near_image, picture, out, image, grads = refs[10:]
    nz, rows, cols = out.shape
    core, odd = where_am_i()
    shift = jnp.where(odd == 1, 2, rows - 2)
    unshift = jnp.where(odd == 1, rows - 2, 2)
    row = lax.broadcasted_iota(jnp.int32, (rows, cols), 0)
    low = odd * (rows - 4)
    mask = (row >= low) & (row < low + 4)

    def emit(z, value):
        at = local_plane(core, nz, z)
        both = pltpu.roll(jnp.concatenate([value, value], axis=0), shift, axis=0)
        out[at] = jnp.where(mask, both, near_grad[at])

    backward_block(8, nz, res, theirs, palette, light, coef, grads, image, emit)
    low = odd * (rows - 2)
    mask2 = (row >= low) & (row < low + 2)
    for c in range(3):
        both = pltpu.roll(jnp.concatenate([image[c], image[c]], axis=0), shift, axis=0)
        whole = jnp.where(mask2, both, pltpu.roll(near_image[c], unshift, axis=0))
        picture[c] = jnp.where(core == 0, whole[:8], whole[8:])


def shards(density, absorption, view_dir, target_ids, palette, emission_coef, light):
    nz, rows, cols = density.shape
    tiles = lax.axis_size("tile")

    sds = resident

    zmsg, xmsg, lmsg, pix = call(
        prep_kernel,
        (sds(HALO, rows, cols), sds(nz + PIX, HALO, cols), sds(nz + PIX, HALO, cols), sds(PIX, rows, cols)),
        (density, absorption, target_ids, view_dir),
        [VMEM, VMEM, VMEM, SMEM],
    )
    swap = [(0, 1), (1, 0)]
    near = [(i, i ^ 1) for i in range(tiles)]
    far = [(i, i + 1 if i % 2 else i - 1) for i in range(1, tiles - 1)]
    zrecv = lax.ppermute(zmsg, "depth", swap)
    xrecv = lax.ppermute(xmsg, "tile", near)
    lmsg = call(corner_kernel, sds(HALO + nz + PIX, HALO, cols), (zrecv, lmsg), [VMEM, VMEM])
    lrecv = lax.ppermute(lmsg, "tile", far)
    xcorner = lax.ppermute(xrecv[:HALO], "depth", swap)

    def residuals(band):
        planes = nz + 2
        return (
            sds(nz + 4, band + 8, cols),
            sds(planes, band, cols),
            sds(planes, band, cols),
            sds(planes, band, cols),
            sds(planes, band, cols),
            sds(planes + 1, band, cols),
            sds(planes, band, cols),
            sds(planes, band, cols),
            sds(4, band, cols),
            sds(PIX, band, cols),
        )

    main = call(
        main_forward_kernel,
        residuals(rows),
        (density, pix, zrecv, xrecv, xcorner, light, emission_coef),
        [VMEM] * 5 + [SMEM] * 2,
    )
    theirs = lax.ppermute(main[8], "depth", swap)
    near_grad, near_image = call(
        main_backward_kernel,
        (sds(nz, rows, cols), sds(3, rows, cols)),
        (*main, theirs, palette, light, emission_coef),
        [VMEM] * 12 + [SMEM] * 2,
        scratch=[pltpu.VMEM((nz + 2, rows, cols), F32)],
    )
    edge = call(
        far_forward_kernel,
        residuals(8),
        (density, pix, zrecv, lrecv, light, emission_coef),
        [VMEM] * 4 + [SMEM] * 2,
    )
    theirs = lax.ppermute(edge[8], "depth", swap)
    picture, grad = call(
        far_backward_kernel,
        (jax.ShapeDtypeStruct((3, 8, cols), F32), jax.ShapeDtypeStruct((nz, rows, cols), F32)),
        (*edge, theirs, palette, light, emission_coef, near_grad, near_image),
        [VMEM] * 12 + [SMEM] * 2 + [VMEM] * 2,
        scratch=[pltpu.VMEM((3, 8, cols), F32), pltpu.VMEM((nz + 2, 8, cols), F32)],
    )
    return picture, grad


def solution(mesh):
    placed = (P("depth", "tile", None), P("tile", None), P("tile"), P("tile", None), P(), P(), P())
    return jax.shard_map(
        shards,
        mesh=mesh,
        in_specs=placed,
        out_specs=(P(None, ("tile", "depth"), None), P("depth", "tile", None)),
        check_vma=False,
    )
```

time: 49.4 us -> 42.1 us (0.85)
  the two profiles are of different devices: /device:TPU:7 before, /device:TPU:0 now
where the time goes in v1:
time: 42.1 us; the launch traced here: 41.7 us
  Pallas kernels  28 us (67%)
  waiting for transfers between devices  4.83 us (11%)
  starting transfers between devices  4.42 us (10%)
  local copies, waits for them, and re-layouts  3.82 us (9%)
  between operations  0.7 us (2%)
    pallas_call x6, Pallas kernels, call(): pl.pallas_call(kernel, out_shape=outs, in_specs=specs, out_specs=jax.tree...  28 us
    unnamed x16, local copies, waits for them, and re-layouts  3.82 us
    ppermute x1, waiting for transfers between devices, shards(): xrecv = lax.ppermute(xmsg, 'tile', near)  3.65 us
    ppermute x1, starting transfers between devices, shards(): xrecv = lax.ppermute(xmsg, 'tile', near)  2.55 us
    ppermute x1, waiting for transfers between devices, shards(): xcorner = lax.ppermute(xrecv[:HALO], 'depth', swap)  1.17 us
  transfers between devices with their start and end apart: 6, of which 2 were waited for; matrix products, arithmetic and copies ran while one was open for 0% of the time, Pallas kernels for 49%

profile of v1, /device:TPU:0, one launch (start us, length us, event | category | flops | bytes accessed | tf_op | source)
XLA Modules:
  0.0 41.7 jit_solution(11504814831431589006)
XLA Ops:
  0.6 0.0 copy-start
  0.6 1.0 %copy-done = f32[32,16,256]{2,1,0:T(8,128)S(1)} copy-done((f32[32,16,256]{2,1,0:T(8,128)S(1)}, f32[32,16,256]{2,1,0:T(8,128)}, u32[]{:S(2)}) %copy-start) | copy-done | bytes 524312
  1.7 0.0 copy-start.3
  1.7 0.7 %copy-done.3 = f32[16,256]{1,0:T(8,128)S(1)} copy-done((f32[16,256]{1,0:T(8,128)S(1)}, f32[16,256]{1,0:T(8,128)}, u32[]{:S(2)}) %copy-start.3) | copy-done | bytes 16408
  2.4 0.0 copy-start.4
  2.4 0.7 %copy-done.4 = s32[16,256]{1,0:T(8,128)S(1)} copy-done((s32[16,256]{1,0:T(8,128)S(1)}, s32[16,256]{1,0:T(8,128)}, u32[]{:S(2)}) %copy-start.4) | copy-done | bytes 16408
  3.1 0.0 copy-start.7
  3.1 0.7 %copy-done.7 = s32[16]{0:T(128)S(1)} copy-done((s32[16]{0:T(128)S(1)}, s32[16]{0:T(128)}, u32[]{:S(2)}) %copy-start.7) | copy-done | bytes 88
  3.8 0.0 copy-start.1
  3.8 0.6 %shard_map.86 = (f32[4,16,256]{2,1,0:T(8,128)S(1)}, f32[35,4,256]{2,1,0:T(4,128)S(1)}, f32[35,4,256]{2,1,0:T(4,128)S(1)}, f32[3,16,256]{2,1,0:T(8,128)S(1)}) custom-call(f32[32,16,256]{2,1,0:T(8,128)S(1)} %copy-done, f32[16,256]{1,0:T(8,128)S(1)} %copy-done.3, s32[16,256]{1,0:T(8,128)S(1)} %copy-done.4, s32[16]{0:T(128)S(1)} %copy-done.7), custom_call_target="tpu_custom_call" | custom-call | tf_op jit(solution)/shard_map/pallas_call | solution.py:19
  4.4 0.6 %collective-permute-start = (f32[4,16,256]{2,1,0:T(8,128)S(1)}, f32[4,16,256]{2,1,0:T(8,128)S(1)}, u32[]{:S(2)}, u32[]{:S(2)}) collective-permute-start(f32[4,16,256]{2,1,0:T(8,128)S(1)} %get-tuple-element.29), channel_id=1, source_target_pairs={{0,1},{1,0},{2,3},{3,2},{4,5},{5,4},{6,7},{7,6},{8,9},{9,8},{10,11... | collective-permute-start | bytes 196616 | tf_op jit(solution)/shard_map/ppermute | solution.py:363
  5.0 2.6 %collective-permute-start.3 = (f32[35,4,256]{2,1,0:T(4,128)S(1)}, f32[35,4,256]{2,1,0:T(4,128)S(1)}, u32[]{:S(2)}, u32[]{:S(2)}) collective-permute-start(f32[35,4,256]{2,1,0:T(4,128)S(1)} %get-tuple-element.41), channel_id=1, source_target_pairs={{0,2},{2,0},{4,6},{6,4},{8,10},{10,8},{12,14},{14,12},{16,18},{18,... | collective-permute-start | bytes 430088 | tf_op jit(solution)/shard_map/ppermute | solution.py:364
  7.5 0.0 collective-permute-done.zrecv
  7.5 0.7 %collective-permute-start.1 = (f32[39,4,256]{2,1,0:T(4,128)S(1)}, f32[39,4,256]{2,1,0:T(4,128)S(1)}, u32[]{:S(2)}, u32[]{:S(2)}) collective-permute-start(f32[39,4,256]{2,1,0:T(4,128)S(1)} %shard_map.87), channel_id=1, source_target_pairs={{2,4},{4,2},{6,8},{8,6},{10,12},{12,10},{14,16},{16,14},{18,20},{2... | collective-permute-start | bytes 479240 | tf_op jit(solution)/shard_map/ppermute | solution.py:366
  8.2 3.6 %collective-permute-done.3.xrecv = f32[35,4,256]{2,1,0:T(4,128)S(1)} collective-permute-done((f32[35,4,256]{2,1,0:T(4,128)S(1)}, f32[35,4,256]{2,1,0:T(4,128)S(1)}, u32[]{:S(2)}, u32[]{:S(2)}) %collective-permute-start.3) | collective-permute-done | bytes 143392 | tf_op jit(solution)/shard_map/ppermute | solution.py:364
  11.9 0.0 copy-start.2
  11.9 0.0 copy-start.6
  11.9 0.0 collective-permute-start.4
  11.9 1.2 %collective-permute-done.4.xcorner = f32[4,4,256]{2,1,0:T(4,128)S(1)} collective-permute-done((f32[4,4,256]{2,1,0:T(4,128)S(1)}, f32[4,4,256]{2,1,0:T(4,128)S(1)}, u32[]{:S(2)}, u32[]{:S(2)}) %collective-permute-start.4) | collective-permute-done | bytes 16416 | tf_op jit(solution)/shard_map/ppermute | solution.py:367
  13.1 0.0 copy-done.1
  13.1 0.0 copy-done.2
  13.1 0.0 copy-done.6
  13.1 7.1 %shard_map.89 = (f32[36,24,256]{2,1,0:T(8,128)S(1)}, f32[34,16,256]{2,1,0:T(8,128)S(1)}, f32[34,16,256]{2,1,0:T(8,128)S(1)}, f32[34,16,256]{2,1,0:T(8,128)S(1)},...) custom-call(f32[32,16,256]{2,1,0:T(8,128)S(1)} %copy-done.1, ...), custom_call_target="tpu_custom_call" | custom-call | tf_op jit(solution)/shard_map/pallas_call | solution.py:19
  20.2 0.2 collective-permute-start.5
  20.4 0.0 collective-permute-done.1.lrecv
  20.4 6.7 %shard_map.88 = (f32[36,16,256]{2,1,0:T(8,128)S(1)}, f32[34,8,256]{2,1,0:T(8,128)S(1)}, f32[34,8,256]{2,1,0:T(8,128)S(1)}, f32[34,8,256]{2,1,0:T(8,128)S(1)}, f3...) custom-call(f32[32,16,256]{2,1,0:T(8,128)S(1)} %copy-done.1, ...), custom_call_target="tpu_custom_call" | custom-call | tf_op jit(solution)/shard_map/pallas_call | solution.py:19
  27.1 0.4 collective-permute-start.2
  27.5 0.0 collective-permute-done.5.refs_10_
  27.5 0.7 %copy-done.5 = f32[3,128]{1,0:T(4,128)S(1)} copy-done((f32[3,128]{1,0:T(4,128)S(1)}, f32[3,128]{1,0:T(4,128)}, u32[]{:S(2)}) %copy-start.5) | copy-done | bytes 1560
  28.2 6.6 %shard_map.90 = (f32[32,16,256]{2,1,0:T(8,128)S(1)}, f32[3,16,256]{2,1,0:T(8,128)S(1)}) custom-call(f32[36,24,256]{2,1,0:T(8,128)S(1)} %get-tuple-element.42.refs_0_, f32[34,16,256]{2,1,0:T(8,128)S(1)} %get-tuple-element.43.refs_1_, f32[34,16,256]{2,1,0:T(8,128)S(1)} %get-tuple-element.44.refs_2_, f32[34,16,256]{2,1,0:T(8,128)S(1)} %get-tuple-element.45.refs_3_, ...), custom_call_target="tpu_custom_call" | custom-call | tf_op jit(solution)/shard_map/pallas_call | solution.py:19
  34.8 0.0 collective-permute-done.2.refs_10_
  34.8 6.9 %shard_map.91 = (f32[3,8,256]{2,1,0:T(8,128)}, f32[32,16,256]{2,1,0:T(8,128)}) custom-call(f32[36,16,256]{2,1,0:T(8,128)S(1)} %get-tuple-element.31.refs_0_, f32[34,8,256]{2,1,0:T(8,128)S(1)} %get-tuple-element.32.refs_1_, f32[34,8,256]{2,1,0:T(8,128)S(1)} %get-tuple-element.33.refs_2_, f32[34,8,256]{2,1,0:T(8,128)S(1)} %get-tuple-element.34.refs_3_, ...), custom_call_target="tpu_custom_call" | custom-call | tf_op jit(solution)/shard_map/pallas_call | solution.py:19
  (3 shorter events, 0.0 us)
Async XLA Ops:
  0.6 1.0 %copy-start = (f32[32,16,256]{2,1,0:T(8,128)S(1)}, f32[32,16,256]{2,1,0:T(8,128)}, u32[]{:S(2)}) copy-start(f32[32,16,256]{2,1,0:T(8,128)} %dens.5) | copy-start | bytes 1572868
  1.7 0.7 %copy-start.3 = (f32[16,256]{1,0:T(8,128)S(1)}, f32[16,256]{1,0:T(8,128)}, u32[]{:S(2)}) copy-start(f32[16,256]{1,0:T(8,128)} %absorb.1) | copy-start | bytes 49156
  2.4 0.7 %copy-start.4 = (s32[16,256]{1,0:T(8,128)S(1)}, s32[16,256]{1,0:T(8,128)}, u32[]{:S(2)}) copy-start(s32[16,256]{1,0:T(8,128)} %ids.1) | copy-start | bytes 49156
  3.1 0.7 %copy-start.7 = (s32[16]{0:T(128)S(1)}, s32[16]{0:T(128)}, u32[]{:S(2)}) copy-start(s32[16]{0:T(128)} %view.1) | copy-start | bytes 196
  3.8 9.3 %copy-start.1 = (f32[32,16,256]{2,1,0:T(8,128)S(1)}, f32[32,16,256]{2,1,0:T(8,128)}, u32[]{:S(2)}) copy-start(f32[32,16,256]{2,1,0:T(8,128)} %dens.5) | copy-start | bytes 1572868
  4.4 3.1 %collective-permute-start = (f32[4,16,256]{2,1,0:T(8,128)S(1)}, f32[4,16,256]{2,1,0:T(8,128)S(1)}, u32[]{:S(2)}, u32[]{:S(2)}) collective-permute-start(f32[4,16,256]{2,1,0:T(8,128)S(1)} %get-tuple-element.29), channel_id=1, source_target_pairs={{0,1},{1,0},{2,3},{3,2},{4,5},{5,4},{6,7},{7,6},{8,9},{9,8},{10,11... | collective-permute-start | bytes 196616 | tf_op jit(solution)/shard_map/ppermute | solution.py:363
  5.0 6.9 %collective-permute-start.3 = (f32[35,4,256]{2,1,0:T(4,128)S(1)}, f32[35,4,256]{2,1,0:T(4,128)S(1)}, u32[]{:S(2)}, u32[]{:S(2)}) collective-permute-start(f32[35,4,256]{2,1,0:T(4,128)S(1)} %get-tuple-element.41), channel_id=1, source_target_pairs={{0,2},{2,0},{4,6},{6,4},{8,10},{10,8},{12,14},{14,12},{16,18},{18,... | collective-permute-start | bytes 430088 | tf_op jit(solution)/shard_map/ppermute | solution.py:364
  7.5 12.9 %collective-permute-start.1 = (f32[39,4,256]{2,1,0:T(4,128)S(1)}, f32[39,4,256]{2,1,0:T(4,128)S(1)}, u32[]{:S(2)}, u32[]{:S(2)}) collective-permute-start(f32[39,4,256]{2,1,0:T(4,128)S(1)} %shard_map.87), channel_id=1, source_target_pairs={{2,4},{4,2},{6,8},{8,6},{10,12},{12,10},{14,16},{16,14},{18,20},{2... | collective-permute-start | bytes 479240 | tf_op jit(solution)/shard_map/ppermute | solution.py:366
  11.9 1.2 %copy-start.2 = (f32[3,4]{1,0:T(4,128)S(1)}, f32[3,4]{1,0:T(4,128)}, u32[]{:S(2)}) copy-start(f32[3,4]{1,0:T(4,128)} %refs_13_.3) | copy-start | bytes 148
  11.9 1.2 %copy-start.6 = (f32[3]{0:T(128)S(1)}, f32[3]{0:T(128)}, u32[]{:S(2)}) copy-start(f32[3]{0:T(128)} %refs_12_.3) | copy-start | bytes 40
  11.9 1.2 %collective-permute-start.4 = (f32[4,4,256]{2,1,0:T(4,128)S(1)}, f32[4,4,256]{2,1,0:T(4,128)S(1)}, u32[]{:S(2)}, u32[]{:S(2)}) collective-permute-start(f32[4,4,256]{2,1,0:T(4,128)S(1)} %slice.4), channel_id=1, source_target_pairs={{0,1},{1,0},{2,3},{3,2},{4,5},{5,4},{6,7},{7,6},{8,9},{9,8},{10,11... | collective-permute-start | bytes 49160 | tf_op jit(solution)/shard_map/ppermute | solution.py:367
  20.2 7.3 %collective-permute-start.5 = (f32[4,16,256]{2,1,0:T(8,128)S(1)}, f32[4,16,256]{2,1,0:T(8,128)S(1)}, u32[]{:S(2)}, u32[]{:S(2)}) collective-permute-start(f32[4,16,256]{2,1,0:T(8,128)S(1)} %get-tuple-element.50.refs_8_), channel_id=1, source_target_pairs={{0,1},{1,0},{2,3},{3,2},{4,5},{5,4},{6,7},{7,6},{8,9},{9,8},{10,11... | collective-permute-start | bytes 196616 | tf_op jit(solution)/shard_map/ppermute | solution.py:390
  27.1 7.7 %collective-permute-start.2 = (f32[4,8,256]{2,1,0:T(8,128)S(1)}, f32[4,8,256]{2,1,0:T(8,128)S(1)}, u32[]{:S(2)}, u32[]{:S(2)}) collective-permute-start(f32[4,8,256]{2,1,0:T(8,128)S(1)} %get-tuple-element.39.refs_8_), channel_id=1, source_target_pairs={{0,1},{1,0},{2,3},{3,2},{4,5},{5,4},{6,7},{7,6},{8,9},{9,8},{10,11... | collective-permute-start | bytes 98312 | tf_op jit(solution)/shard_map/ppermute | solution.py:404
  27.5 0.7 %copy-start.5 = (f32[3,128]{1,0:T(4,128)S(1)}, f32[3,128]{1,0:T(4,128)}, u32[]{:S(2)}) copy-start(f32[3,128]{1,0:T(4,128)} %refs_11_.3) | copy-start | bytes 4612

commit v2 on v1

--- a/solution.py
+++ b/solution.py
@@ -9,6 +9,7 @@
 
 F32 = jnp.float32
 HALO = 4
+UNROLL = 8
 PIX = 3
 VMEM = pl.BlockSpec(memory_space=pltpu.VMEM)
 SMEM = pl.BlockSpec(memory_space=pltpu.SMEM)
@@ -134,7 +135,7 @@
         return here, after, total + optical(z, s[:band])
 
     carry = (zero, first, jnp.zeros_like(a))
-    carry = lax.fori_loop(0, depth - 1, smooth_step, carry)
+    carry = lax.fori_loop(0, depth - 1, smooth_step, carry, unroll=UNROLL)
     before, here, total = smooth_step_seam(depth - 1, carry, own, halo, gather, smoothing, smooth, optical, band)
     tot = total
     for z in range(depth, depth + 3):
@@ -180,7 +181,7 @@
 
     nil = jnp.zeros_like(a)
     carry = (start, first_edge, nil, nil, nil, nil)
-    carry = lax.fori_loop(0, depth, shade_step, carry)
+    carry = lax.fori_loop(0, depth, shade_step, carry, unroll=UNROLL)
     _, _, m0, m1, m2, m3 = carry
     half = 0.5 * sign
     mid[0] = sign * tot
@@ -294,7 +295,7 @@
         return run, part, az
 
     nil = jnp.zeros_like(sign)
-    lax.fori_loop(0, depth + 2, shade_back, (queue, nil, nil))
+    lax.fori_loop(0, depth + 2, shade_back, (queue, nil, nil), unroll=UNROLL)
 
     def smooth_back(z, carry):
         here = grads[z + 1]
@@ -305,7 +306,7 @@
         emit(z, t * 0.125)
         return carry
 
-    lax.fori_loop(0, depth, smooth_back, 0)
+    lax.fori_loop(0, depth, smooth_back, 0, unroll=UNROLL)
 
 
 def main_backward_kernel(*refs):

time: 42.1 us -> 25.2 us (0.60)
  the two profiles are of different devices: /device:TPU:0 before, /device:TPU:9 now
where the time goes in v2:
time: 25.2 us; the launch traced here: 24.8 us
  Pallas kernels  11 us (44%)
  starting transfers between devices  8.16 us (32%)
  local copies, waits for them, and re-layouts  3.82 us (15%)
  waiting for transfers between devices  1.19 us (5%)
  between operations  0.7 us (3%)
    pallas_call x6, Pallas kernels, call(): pl.pallas_call(kernel, out_shape=outs, in_specs=specs, out_specs=jax.tree...  11 us
    unnamed x16, local copies, waits for them, and re-layouts  3.82 us
    ppermute x1, starting transfers between devices, shards(): lrecv = lax.ppermute(lmsg, 'tile', far)  3.65 us
    ppermute x1, starting transfers between devices, shards(): xrecv = lax.ppermute(xmsg, 'tile', near)  1.21 us
    ppermute x1, starting transfers between devices, shards(): theirs = lax.ppermute(edge[8], 'depth', swap)  1.2 us
    ppermute x1, starting transfers between devices, shards(): xcorner = lax.ppermute(xrecv[:HALO], 'depth', swap)  0.94 us
    ppermute x1, waiting for transfers between devices, shards(): xcorner = lax.ppermute(xrecv[:HALO], 'depth', swap)  0.84 us
    ppermute x1, starting transfers between devices, shards(): zrecv = lax.ppermute(zmsg, 'depth', swap)  0.74 us
  transfers between devices with their start and end apart: 6, of which 2 were waited for; matrix products, arithmetic and copies ran while one was open for 0% of the time, Pallas kernels for 31%

profile of v2, /device:TPU:9, one launch (start us, length us, event | category | flops | bytes accessed | tf_op | source)
XLA Modules:
  0.0 24.8 jit_solution(13569717527936797824)
XLA Ops:
  0.6 0.0 copy-start
  0.6 1.0 %copy-done = f32[32,16,256]{2,1,0:T(8,128)S(1)} copy-done((f32[32,16,256]{2,1,0:T(8,128)S(1)}, f32[32,16,256]{2,1,0:T(8,128)}, u32[]{:S(2)}) %copy-start) | copy-done | bytes 524312
  1.7 0.0 copy-start.3
  1.7 0.7 %copy-done.3 = f32[16,256]{1,0:T(8,128)S(1)} copy-done((f32[16,256]{1,0:T(8,128)S(1)}, f32[16,256]{1,0:T(8,128)}, u32[]{:S(2)}) %copy-start.3) | copy-done | bytes 16408
  2.4 0.0 copy-start.4
  2.4 0.7 %copy-done.4 = s32[16,256]{1,0:T(8,128)S(1)} copy-done((s32[16,256]{1,0:T(8,128)S(1)}, s32[16,256]{1,0:T(8,128)}, u32[]{:S(2)}) %copy-start.4) | copy-done | bytes 16408
  3.1 0.0 copy-start.7
  3.1 0.7 %copy-done.7 = s32[16]{0:T(128)S(1)} copy-done((s32[16]{0:T(128)S(1)}, s32[16]{0:T(128)}, u32[]{:S(2)}) %copy-start.7) | copy-done | bytes 88
  3.8 0.0 copy-start.1
  3.8 0.6 %shard_map.86 = (f32[4,16,256]{2,1,0:T(8,128)S(1)}, f32[35,4,256]{2,1,0:T(4,128)S(1)}, f32[35,4,256]{2,1,0:T(4,128)S(1)}, f32[3,16,256]{2,1,0:T(8,128)S(1)}) custom-call(f32[32,16,256]{2,1,0:T(8,128)S(1)} %copy-done, f32[16,256]{1,0:T(8,128)S(1)} %copy-done.3, s32[16,256]{1,0:T(8,128)S(1)} %copy-done.4, s32[16]{0:T(128)S(1)} %copy-done.7), custom_call_target="tpu_custom_call" | custom-call | tf_op jit(solution)/shard_map/pallas_call | solution.py:20
  4.4 0.7 %collective-permute-start = (f32[4,16,256]{2,1,0:T(8,128)S(1)}, f32[4,16,256]{2,1,0:T(8,128)S(1)}, u32[]{:S(2)}, u32[]{:S(2)}) collective-permute-start(f32[4,16,256]{2,1,0:T(8,128)S(1)} %get-tuple-element.29), channel_id=1, source_target_pairs={{0,1},{1,0},{2,3},{3,2},{4,5},{5,4},{6,7},{7,6},{8,9},{9,8},{10,11... | collective-permute-start | bytes 196616 | tf_op jit(solution)/shard_map/ppermute | solution.py:364
  5.1 1.2 %collective-permute-start.3 = (f32[35,4,256]{2,1,0:T(4,128)S(1)}, f32[35,4,256]{2,1,0:T(4,128)S(1)}, u32[]{:S(2)}, u32[]{:S(2)}) collective-permute-start(f32[35,4,256]{2,1,0:T(4,128)S(1)} %get-tuple-element.41), channel_id=1, source_target_pairs={{0,2},{2,0},{4,6},{6,4},{8,10},{10,8},{12,14},{14,12},{16,18},{18,... | collective-permute-start | bytes 430088 | tf_op jit(solution)/shard_map/ppermute | solution.py:365
  6.3 0.0 collective-permute-done.zrecv
  6.4 3.6 %collective-permute-start.1 = (f32[39,4,256]{2,1,0:T(4,128)S(1)}, f32[39,4,256]{2,1,0:T(4,128)S(1)}, u32[]{:S(2)}, u32[]{:S(2)}) collective-permute-start(f32[39,4,256]{2,1,0:T(4,128)S(1)} %shard_map.87), channel_id=1, source_target_pairs={{2,4},{4,2},{6,8},{8,6},{10,12},{12,10},{14,16},{16,14},{18,20},{2... | collective-permute-start | bytes 479240 | tf_op jit(solution)/shard_map/ppermute | solution.py:367
  10.0 0.3 %collective-permute-done.3.xrecv = f32[35,4,256]{2,1,0:T(4,128)S(1)} collective-permute-done((f32[35,4,256]{2,1,0:T(4,128)S(1)}, f32[35,4,256]{2,1,0:T(4,128)S(1)}, u32[]{:S(2)}, u32[]{:S(2)}) %collective-permute-start.3) | collective-permute-done | bytes 143392 | tf_op jit(solution)/shard_map/ppermute | solution.py:365
  10.4 0.0 copy-start.2
  10.4 0.9 %collective-permute-start.4 = (f32[4,4,256]{2,1,0:T(4,128)S(1)}, f32[4,4,256]{2,1,0:T(4,128)S(1)}, u32[]{:S(2)}, u32[]{:S(2)}) collective-permute-start(f32[4,4,256]{2,1,0:T(4,128)S(1)} %slice.4), channel_id=1, source_target_pairs={{0,1},{1,0},{2,3},{3,2},{4,5},{5,4},{6,7},{7,6},{8,9},{9,8},{10,11... | collective-permute-start | bytes 49160 | tf_op jit(solution)/shard_map/ppermute | solution.py:368
  11.3 0.8 %collective-permute-done.4.xcorner = f32[4,4,256]{2,1,0:T(4,128)S(1)} collective-permute-done((f32[4,4,256]{2,1,0:T(4,128)S(1)}, f32[4,4,256]{2,1,0:T(4,128)S(1)}, u32[]{:S(2)}, u32[]{:S(2)}) %collective-permute-start.4) | collective-permute-done | bytes 16416 | tf_op jit(solution)/shard_map/ppermute | solution.py:368
  12.2 0.0 copy-done.1
  12.2 0.0 copy-done.2
  12.2 0.0 copy-done.6
  12.2 2.9 %shard_map.89 = (f32[36,24,256]{2,1,0:T(8,128)S(1)}, f32[34,16,256]{2,1,0:T(8,128)S(1)}, f32[34,16,256]{2,1,0:T(8,128)S(1)}, f32[34,16,256]{2,1,0:T(8,128)S(1)},...) custom-call(f32[32,16,256]{2,1,0:T(8,128)S(1)} %copy-done.1, ...), custom_call_target="tpu_custom_call" | custom-call | tf_op jit(solution)/shard_map/pallas_call | solution.py:20
  15.0 0.4 %collective-permute-start.5 = (f32[4,16,256]{2,1,0:T(8,128)S(1)}, f32[4,16,256]{2,1,0:T(8,128)S(1)}, u32[]{:S(2)}, u32[]{:S(2)}) collective-permute-start(f32[4,16,256]{2,1,0:T(8,128)S(1)} %get-tuple-element.50.refs_8_), channel_id=1, source_target_pairs={{0,1},{1,0},{2,3},{3,2},{4,5},{5,4},{6,7},{7,6},{8,9},{9,8},{10,11... | collective-permute-start | bytes 196616 | tf_op jit(solution)/shard_map/ppermute | solution.py:391
  15.5 0.0 collective-permute-done.1.lrecv
  15.5 2.4 %shard_map.88 = (f32[36,16,256]{2,1,0:T(8,128)S(1)}, f32[34,8,256]{2,1,0:T(8,128)S(1)}, f32[34,8,256]{2,1,0:T(8,128)S(1)}, f32[34,8,256]{2,1,0:T(8,128)S(1)}, f3...) custom-call(f32[32,16,256]{2,1,0:T(8,128)S(1)} %copy-done.1, ...), custom_call_target="tpu_custom_call" | custom-call | tf_op jit(solution)/shard_map/pallas_call | solution.py:20
  17.8 1.2 %collective-permute-start.2 = (f32[4,8,256]{2,1,0:T(8,128)S(1)}, f32[4,8,256]{2,1,0:T(8,128)S(1)}, u32[]{:S(2)}, u32[]{:S(2)}) collective-permute-start(f32[4,8,256]{2,1,0:T(8,128)S(1)} %get-tuple-element.39.refs_8_), channel_id=1, source_target_pairs={{0,1},{1,0},{2,3},{3,2},{4,5},{5,4},{6,7},{7,6},{8,9},{9,8},{10,11... | collective-permute-start | bytes 98312 | tf_op jit(solution)/shard_map/ppermute | solution.py:405
  19.0 0.0 collective-permute-done.5.refs_10_
  19.1 0.0 copy-start.5
  19.1 0.7 %copy-done.5 = f32[3,128]{1,0:T(4,128)S(1)} copy-done((f32[3,128]{1,0:T(4,128)S(1)}, f32[3,128]{1,0:T(4,128)}, u32[]{:S(2)}) %copy-start.5) | copy-done | bytes 1560
  19.7 2.5 %shard_map.90 = (f32[32,16,256]{2,1,0:T(8,128)S(1)}, f32[3,16,256]{2,1,0:T(8,128)S(1)}) custom-call(f32[36,24,256]{2,1,0:T(8,128)S(1)} %get-tuple-element.42.refs_0_, f32[34,16,256]{2,1,0:T(8,128)S(1)} %get-tuple-element.43.refs_1_, f32[34,16,256]{2,1,0:T(8,128)S(1)} %get-tuple-element.44.refs_2_, f32[34,16,256]{2,1,0:T(8,128)S(1)} %get-tuple-element.45.refs_3_, ...), custom_call_target="tpu_custom_call" | custom-call | tf_op jit(solution)/shard_map/pallas_call | solution.py:20
  22.2 0.0 collective-permute-done.2.refs_10_
  22.2 2.6 %shard_map.91 = (f32[3,8,256]{2,1,0:T(8,128)}, f32[32,16,256]{2,1,0:T(8,128)}) custom-call(f32[36,16,256]{2,1,0:T(8,128)S(1)} %get-tuple-element.31.refs_0_, f32[34,8,256]{2,1,0:T(8,128)S(1)} %get-tuple-element.32.refs_1_, f32[34,8,256]{2,1,0:T(8,128)S(1)} %get-tuple-element.33.refs_2_, f32[34,8,256]{2,1,0:T(8,128)S(1)} %get-tuple-element.34.refs_3_, ...), custom_call_target="tpu_custom_call" | custom-call | tf_op jit(solution)/shard_map/pallas_call | solution.py:20
  (3 shorter events, 0.0 us)
Async XLA Ops:
  0.6 1.0 %copy-start = (f32[32,16,256]{2,1,0:T(8,128)S(1)}, f32[32,16,256]{2,1,0:T(8,128)}, u32[]{:S(2)}) copy-start(f32[32,16,256]{2,1,0:T(8,128)} %dens.5) | copy-start | bytes 1572868
  1.7 0.7 %copy-start.3 = (f32[16,256]{1,0:T(8,128)S(1)}, f32[16,256]{1,0:T(8,128)}, u32[]{:S(2)}) copy-start(f32[16,256]{1,0:T(8,128)} %absorb.1) | copy-start | bytes 49156
  2.4 0.7 %copy-start.4 = (s32[16,256]{1,0:T(8,128)S(1)}, s32[16,256]{1,0:T(8,128)}, u32[]{:S(2)}) copy-start(s32[16,256]{1,0:T(8,128)} %ids.1) | copy-start | bytes 49156
  3.1 0.7 %copy-start.7 = (s32[16]{0:T(128)S(1)}, s32[16]{0:T(128)}, u32[]{:S(2)}) copy-start(s32[16]{0:T(128)} %view.1) | copy-start | bytes 196
  3.8 8.4 %copy-start.1 = (f32[32,16,256]{2,1,0:T(8,128)S(1)}, f32[32,16,256]{2,1,0:T(8,128)}, u32[]{:S(2)}) copy-start(f32[32,16,256]{2,1,0:T(8,128)} %dens.5) | copy-start | bytes 1572868
  4.4 2.0 %collective-permute-start = (f32[4,16,256]{2,1,0:T(8,128)S(1)}, f32[4,16,256]{2,1,0:T(8,128)S(1)}, u32[]{:S(2)}, u32[]{:S(2)}) collective-permute-start(f32[4,16,256]{2,1,0:T(8,128)S(1)} %get-tuple-element.29), channel_id=1, source_target_pairs={{0,1},{1,0},{2,3},{3,2},{4,5},{5,4},{6,7},{7,6},{8,9},{9,8},{10,11... | collective-permute-start | bytes 196616 | tf_op jit(solution)/shard_map/ppermute | solution.py:364
  5.1 5.2 %collective-permute-start.3 = (f32[35,4,256]{2,1,0:T(4,128)S(1)}, f32[35,4,256]{2,1,0:T(4,128)S(1)}, u32[]{:S(2)}, u32[]{:S(2)}) collective-permute-start(f32[35,4,256]{2,1,0:T(4,128)S(1)} %get-tuple-element.41), channel_id=1, source_target_pairs={{0,2},{2,0},{4,6},{6,4},{8,10},{10,8},{12,14},{14,12},{16,18},{18,... | collective-permute-start | bytes 430088 | tf_op jit(solution)/shard_map/ppermute | solution.py:365
  6.4 9.1 %collective-permute-start.1 = (f32[39,4,256]{2,1,0:T(4,128)S(1)}, f32[39,4,256]{2,1,0:T(4,128)S(1)}, u32[]{:S(2)}, u32[]{:S(2)}) collective-permute-start(f32[39,4,256]{2,1,0:T(4,128)S(1)} %shard_map.87), channel_id=1, source_target_pairs={{2,4},{4,2},{6,8},{8,6},{10,12},{12,10},{14,16},{16,14},{18,20},{2... | collective-permute-start | bytes 479240 | tf_op jit(solution)/shard_map/ppermute | solution.py:367
  10.4 1.8 %copy-start.2 = (f32[3,4]{1,0:T(4,128)S(1)}, f32[3,4]{1,0:T(4,128)}, u32[]{:S(2)}) copy-start(f32[3,4]{1,0:T(4,128)} %refs_13_.3) | copy-start | bytes 148
  10.4 1.8 %copy-start.6 = (f32[3]{0:T(128)S(1)}, f32[3]{0:T(128)}, u32[]{:S(2)}) copy-start(f32[3]{0:T(128)} %refs_12_.3) | copy-start | bytes 40
  10.4 1.8 %collective-permute-start.4 = (f32[4,4,256]{2,1,0:T(4,128)S(1)}, f32[4,4,256]{2,1,0:T(4,128)S(1)}, u32[]{:S(2)}, u32[]{:S(2)}) collective-permute-start(f32[4,4,256]{2,1,0:T(4,128)S(1)} %slice.4), channel_id=1, source_target_pairs={{0,1},{1,0},{2,3},{3,2},{4,5},{5,4},{6,7},{7,6},{8,9},{9,8},{10,11... | collective-permute-start | bytes 49160 | tf_op jit(solution)/shard_map/ppermute | solution.py:368
  15.0 4.0 %collective-permute-start.5 = (f32[4,16,256]{2,1,0:T(8,128)S(1)}, f32[4,16,256]{2,1,0:T(8,128)S(1)}, u32[]{:S(2)}, u32[]{:S(2)}) collective-permute-start(f32[4,16,256]{2,1,0:T(8,128)S(1)} %get-tuple-element.50.refs_8_), channel_id=1, source_target_pairs={{0,1},{1,0},{2,3},{3,2},{4,5},{5,4},{6,7},{7,6},{8,9},{9,8},{10,11... | collective-permute-start | bytes 196616 | tf_op jit(solution)/shard_map/ppermute | solution.py:391
  17.8 4.4 %collective-permute-start.2 = (f32[4,8,256]{2,1,0:T(8,128)S(1)}, f32[4,8,256]{2,1,0:T(8,128)S(1)}, u32[]{:S(2)}, u32[]{:S(2)}) collective-permute-start(f32[4,8,256]{2,1,0:T(8,128)S(1)} %get-tuple-element.39.refs_8_), channel_id=1, source_target_pairs={{0,1},{1,0},{2,3},{3,2},{4,5},{5,4},{6,7},{7,6},{8,9},{9,8},{10,11... | collective-permute-start | bytes 98312 | tf_op jit(solution)/shard_map/ppermute | solution.py:405
  19.1 0.7 %copy-start.5 = (f32[3,128]{1,0:T(4,128)S(1)}, f32[3,128]{1,0:T(4,128)}, u32[]{:S(2)}) copy-start(f32[3,128]{1,0:T(4,128)} %refs_11_.3) | copy-start | bytes 4612

commit v3 on v1

v3 whole, which is shorter than its diff:
```python
import jax
import jax.numpy as jnp
from jax import lax
from jax.experimental import pallas as pl
from jax.experimental.pallas import tpu as pltpu
from jax.sharding import PartitionSpec as P

F32 = jnp.float32
HALO = 4
PIX = 3
GROUP_MAIN = (16,16,16,16)
GROUP_FAR = (16,16,34,32)
LATE = True
VMEM = pl.BlockSpec(memory_space=pltpu.VMEM)
HBM = pl.BlockSpec(memory_space=pl.ANY)


def call(kernel, outs, args, specs, scratch=(), cost=None, out_specs=None):
    args = [pltpu.with_memory_space_constraint(a, pltpu.VMEM if s is VMEM else pltpu.HBM) for a, s in zip(args, specs)]
    return pl.pallas_call(
        kernel,
        out_shape=outs,
        in_specs=specs,
        out_specs=out_specs or jax.tree.map(lambda _: VMEM, outs),
        scratch_shapes=scratch,
        cost_estimate=cost,
        compiler_params=pltpu.CompilerParams(vmem_limit_bytes=8 << 20),
    )(*args)


def resident(*shape):
    return pltpu.VMEM(shape, F32)


def where_am_i():
    return lax.axis_index("depth"), lax.rem(lax.axis_index("tile"), 2)


def local_plane(core, nz, z):
    return jnp.where(core == 0, z, nz - 1 - z)


def in_groups(body, count, group, carry):
    full = count // group
    if full:
        carry = lax.fori_loop(0, full, lambda i, c: body(i * group, group, c), carry)
    if count % group:
        carry = body(full * group, count % group, carry)
    return carry


class Stores:
    def __init__(self):
        self.todo = []

    def put(self, ref, at, value):
        if LATE:
            self.todo.append((ref, at, value))
        else:
            ref[at] = value

    def flush(self):
        for ref, at, value in self.todo:
            ref[at] = value


def spread(par, i, rows, cols):
    t = par[i]
    t = jnp.concatenate([t] * (cols // t.shape[1]), axis=1)
    return jnp.concatenate([t] * (rows // t.shape[0]), axis=0)


def fetch_kernel(dens_h, absorb_h, ids_h, view_h, pal_h, coef_h, light_h, zmsg, dens, pix, pal, par, ids, view, coef, light, sem):
    nz, rows, cols = dens.shape
    core, odd = where_am_i()
    pairs = ((dens_h, dens), (view_h, view), (ids_h, ids), (absorb_h, pix.at[0]), (coef_h, coef), (light_h, light), (pal_h, pal))
    copies = [pltpu.make_async_copy(a, b, sem.at[i]) for i, (a, b) in enumerate(pairs)]
    for c in copies:
        c.start()
    for c in copies[1:]:
        c.wait()
    row = lax.broadcasted_iota(jnp.int32, (rows, cols), 0)
    seen = jnp.zeros((rows, cols), F32)
    for r in range(rows):
        seen = jnp.where(row == r, view[r].astype(F32), seen)
    pix[1] = ids[...].astype(F32)
    pix[2] = seen
    for i in range(3):
        for k in range(4):
            par[4 * i + k] = jnp.full(par.shape[1:], coef[i, k])
        value = light[i]
        if i == 0:
            value = jnp.where(core == 0, value, -value)
        par[12 + i] = jnp.full(par.shape[1:], value)
    copies[0].wait()
    for j in range(HALO):
        zmsg[j] = dens[local_plane(core, nz, nz - 1 - j)]


def edges_kernel(dens, pix, xmsg, lmsg):
    nz, rows, cols = dens.shape
    core, odd = where_am_i()

    def edges(plane, to):
        head, tail = plane[:HALO], plane[rows - HALO :]
        xmsg[to] = jnp.where(odd == 1, head, tail)
        lmsg[to] = jnp.where(odd == 1, tail, head)

    for j in range(PIX):
        edges(pix[j], nz + j)
    for j in range(nz):
        edges(dens[local_plane(core, nz, nz - 1 - j)], j)


def corner_kernel(zrecv, early, lmsg):
    rows = zrecv.shape[1]
    _, odd = where_am_i()
    lmsg[HALO:] = early[...]
    for j in range(HALO):
        plane = zrecv[HALO - 1 - j]
        lmsg[j] = jnp.where(odd == 1, plane[rows - HALO :], plane[:HALO])


def lookup(palette, ids):
    rows, cols = ids.shape
    entries = palette.shape[1]
    index = ids.astype(jnp.int32)
    parts = []
    for c in range(3):
        strips = []
        for r in range(0, rows, 8):
            strip = []
            for x in range(0, cols, entries):
                table = jnp.broadcast_to(palette[c : c + 1, :], (8, entries))
                strip.append(jnp.take_along_axis(table, index[r : r + 8, x : x + entries], axis=1))
            strips.append(jnp.concatenate(strip, axis=1))
        parts.append(jnp.concatenate(strips, axis=0))
    return parts


class Block:
    def __init__(self, band, shift, own, halo):
        self.band, self.shift, self.own, self.halo = band, shift, own, halo

    def plane(self, z):
        h = self.halo(z)
        return pltpu.roll(jnp.concatenate([self.own(z), h, h], axis=0), self.shift, axis=0)


def pixels(block, core, depth):
    a, ids, view = [block.plane(-1 - j)[: block.band] for j in range(PIX)]
    back = jnp.where(core == 0, view, 1.0 - view)
    return a, ids, back


def smooth_planes(block, first, n, signed, depth, smooth, taus, sig, total, lead=None):
    band, wide = block.band, block.band + 8
    out = Stores()
    zs = [first - 1 + i for i in range(n + 2)]
    planes = [lead if i == 0 and lead is not None else block.plane(z) for i, z in enumerate(zs)]
    for i in range(n):
        here = planes[i + 1]
        cols = here.shape[1]
        t = planes[i] + planes[i + 2] + 2.0 * here
        t = t + pltpu.roll(here, 1, axis=0) + pltpu.roll(here, wide - 1, axis=0)
        t = t + pltpu.roll(here, 1, axis=1) + pltpu.roll(here, cols - 1, axis=1)
        s = t * 0.125
        out.put(smooth, zs[i + 1] + 1, s)
        static = isinstance(first, int)
        if not static or first + i < depth + 2:
            soft = jnp.log(1.0 + jnp.exp(s[:band]))
            tau = signed * soft
            out.put(taus, zs[i + 1], tau)
            out.put(sig, zs[i + 1], 1.0 - jnp.exp(-soft))
            if not static or first + i < depth:
                total = total + tau
    out.flush()
    return total


def smooth_slab(block, core, depth, group, smooth, taus, sig, pixo):
    a, ids, back = pixels(block, core, depth)
    signed = a * (1.0 / (2 * depth)) * (1.0 - 2.0 * back)
    pixo[0], pixo[1], pixo[2] = a, ids, back
    face = block.plane(0)
    smooth[0] = face * 0.125
    zero = jnp.zeros_like(face)
    total = smooth_planes(block, 0, 1, signed, depth, smooth, taus, sig, jnp.zeros_like(a), lead=zero)

    def body(z, n, total):
        return smooth_planes(block, z + 1, n, signed, depth, smooth, taus, sig, total)

    return in_groups(body, depth - 2, group, total)


def smooth_seam(block, depth, smooth, taus, sig, pixo, total):
    a, back = pixo[0], pixo[2]
    signed = a * (1.0 / (2 * depth)) * (1.0 - 2.0 * back)
    return smooth_planes(block, depth - 1, 4, signed, depth, smooth, taus, sig, total)


def shade_slab(band, depth, group, total, par, smooth, taus, dxs, dys, rnorm, phis, edge, mid, pixo):
    wide, cols = band + 8, smooth.shape[2]
    back = pixo[2]
    sign = 1.0 - 2.0 * back
    lz, ly, lx = [spread(par, 12 + i, band, cols) for i in range(3)]
    start = jnp.where(back == 1.0, total, 0.0)
    opened = jnp.exp(start)
    edge[0] = opened

    def body(z0, n, carry):
        run, seen, m0, m1, m2, m3 = carry
        out = Stores()
        planes = [smooth[z0 + i] for i in range(n + 2)]
        absorbed = [taus[z0 + i] for i in range(n)]
        for i in range(n):
            here = planes[i + 1]
            s = here[:band]
            dz = planes[i + 2][:band] - planes[i][:band]
            dy = (pltpu.roll(here, wide - 1, axis=0) - pltpu.roll(here, 1, axis=0))[:band]
            dx = pltpu.roll(s, cols - 1, axis=1) - pltpu.roll(s, 1, axis=1)
            r = lax.rsqrt(4.0 + dz * dz + dy * dy + dx * dx)
            phi = (dz * lz + dy * ly + dx * lx) * r
            run = run - absorbed[i]
            nxt = jnp.exp(run)
            for ref, v in ((dxs, dx), (dys, dy), (rnorm, r), (phis, phi)):
                out.put(ref, z0 + i, v)
            out.put(edge, z0 + i + 1, nxt)
            b = (seen - nxt) * (1.0 + phi)
            m0 = m0 + b
            b = b * s
            m1 = m1 + b
            b = b * s
            m2 = m2 + b
            b = b * s
            m3 = m3 + b
            seen = nxt
        out.flush()
        return run, seen, m0, m1, m2, m3

    nil = jnp.zeros_like(back)
    carry = in_groups(body, depth, group, (start, opened, nil, nil, nil, nil))
    _, _, m0, m1, m2, m3 = carry
    half = 0.5 * sign
    mid[0] = sign * total
    for c in range(3):
        k0, k1, k2, k3 = [spread(par, 4 * c + k, band, cols) for k in range(4)]
        mid[1 + c] = half * (m0 * k0 + m1 * k1 + m2 * k2 + m3 * k3)
    body(depth, 2, carry)


def main_block(dens, pix, xrecv, zrecv=None, xcorner=None):
    nz, rows, _ = dens.shape
    core, odd = where_am_i()

    def own(z):
        if isinstance(z, int):
            if z < 0:
                return pix[-1 - z]
            if z >= nz:
                return zrecv[z - nz]
        return dens[local_plane(core, nz, z)]

    def halo(z):
        if isinstance(z, int):
            if z < 0:
                return xrecv[nz - 1 - z]
            if z >= nz:
                return xcorner[z - nz]
        return xrecv[nz - 1 - z]

    return Block(rows, jnp.where(odd == 1, 2, rows + 8 - 2), own, halo)


def far_forward_kernel(dens, pix, zrecv, lrecv, par, smooth, dxs, dys, rnorm, phis, edge, sig, taus, mid, pixo):
    nz, rows, cols = dens.shape
    core, odd = where_am_i()
    at = pl.multiple_of(odd * (rows - 8), 8)

    def own(z):
        if isinstance(z, int):
            if z < 0:
                return pix[-1 - z, pl.ds(at, 8)]
            if z >= nz:
                return zrecv[z - nz, pl.ds(at, 8)]
        return dens[local_plane(core, nz, z), pl.ds(at, 8)]

    def halo(z):
        return lrecv[nz + HALO - 1 - z]

    block = Block(8, jnp.where(odd == 1, 16 - 2, 2), own, halo)
    total = smooth_slab(block, core, nz, GROUP_FAR[0], smooth, taus, sig, pixo)
    total = smooth_seam(block, nz, smooth, taus, sig, pixo, total)
    shade_slab(8, nz, GROUP_FAR[1], total, par, smooth, taus, dxs, dys, rnorm, phis, edge, mid, pixo)


def main_forward_kernel(dens, pix, zrecv, xrecv, xcorner, par, smooth, dxs, dys, rnorm, phis, edge, sig, taus, mid, pixo):
    nz, rows, cols = dens.shape
    core, _ = where_am_i()
    block = main_block(dens, pix, xrecv, zrecv, xcorner)
    total = smooth_slab(block, core, nz, GROUP_MAIN[0], smooth, taus, sig, pixo)
    total = smooth_seam(block, nz, smooth, taus, sig, pixo, total)
    shade_slab(rows, nz, GROUP_MAIN[1], total, par, smooth, taus, dxs, dys, rnorm, phis, edge, mid, pixo)


def backward_block(band, depth, groups, res, theirs, palette, par, grads, image, emit):
    smooth, dxs, dys, rnorm, phis, edge, sig, taus, mid, pixo = res
    cols = smooth.shape[2]
    back = pixo[2] == 1.0
    sign = jnp.where(back, -1.0, 1.0)
    mine_total, their_total = mid[0], theirs[0]
    through_me, through_them = jnp.exp(-mine_total), jnp.exp(-their_total)
    target = lookup(palette, pixo[1])
    g, flow = [], jnp.zeros_like(sign)
    for c in range(3):
        mine, other = mid[1 + c], theirs[1 + c]
        pic = jnp.where(back, other + through_them * mine, mine + through_me * other)
        image[c] = pic
        err = (pic - target[c]) * (2.0 * depth)
        g.append(err)
        flow = flow + err * pic
    kappa = jnp.where(back, 0.5 * through_them, 0.5)
    gam = []
    for k in range(4):
        k0, k1, k2 = [spread(par, 4 * c + k, band, cols) for c in range(3)]
        gam.append(kappa * (g[0] * k0 + g[1] * k1 + g[2] * k2))
    gam2, gam3 = 2.0 * gam[2], 3.0 * gam[3]
    queue = jnp.where(back, 0.0, -flow)
    weight = pixo[0] * (1.0 / (2 * depth))
    lz, ly, lx = [spread(par, 12 + i, band, cols) for i in range(3)]

    def shade_back(z0, n, carry):
        run, part, last = carry
        out = Stores()
        planes = [smooth[z0 + i, pl.ds(0, band)] for i in range(n + 2)]
        edges = [edge[z0 + i] for i in range(n + 1)]
        rest = [(phis[z0 + i], rnorm[z0 + i], sig[z0 + i], dys[z0 + i], dxs[z0 + i]) for i in range(n)]
        for i in range(n):
            s = planes[i + 1]
            dz = planes[i + 2] - planes[i]
            phi, r, sg, dy, dx = rest[i]
            near, far = edges[i], edges[i + 1]
            shade = 1.0 + phi
            poly = gam[0] + s * (gam[1] + s * (gam[2] + s * gam[3]))
            slope = gam[1] + s * (gam2 + s * gam3)
            h = shade * poly
            lost = near - far
            w = sign * lost
            mine = (near * h + run) * (weight * sg) + (w * shade) * slope
            run = run + lost * h
            t1 = w * poly * r
            t3 = t1 * phi * r
            az = t1 * lz - t3 * dz
            ay = t1 * ly - t3 * dy
            ax = t1 * lx - t3 * dx
            out.put(grads, z0 + i, part - az)
            part = mine + last
            part = part + (pltpu.roll(ay, 1, axis=0) - pltpu.roll(ay, band - 1, axis=0))
            part = part + (pltpu.roll(ax, 1, axis=1) - pltpu.roll(ax, cols - 1, axis=1))
            last = az
        out.flush()
        return run, part, last

    nil = jnp.zeros_like(sign)
    in_groups(shade_back, depth + 2, groups[2], (queue, nil, nil))

    def smooth_back(z0, n, carry):
        planes = [grads[z0 + i] for i in range(n + 2)]
        done = []
        for i in range(n):
            here = planes[i + 1]
            t = planes[i] + planes[i + 2] + 2.0 * here
            t = t + pltpu.roll(here, 1, axis=0) + pltpu.roll(here, band - 1, axis=0)
            t = t + pltpu.roll(here, 1, axis=1) + pltpu.roll(here, cols - 1, axis=1)
            done.append(t * 0.125)
        emit(z0, done)
        return carry

    in_groups(smooth_back, depth, groups[3], 0)


def main_backward_kernel(*refs):
    res, (theirs, palette, par, out, image, grads) = refs[:10], refs[10:]
    nz, rows, cols = out.shape
    core, odd = where_am_i()
    shift = jnp.where(odd == 1, rows - 2, 2)

    def emit(z0, values):
        values = [pltpu.roll(v, shift, axis=0) for v in values]
        for i, v in enumerate(values):
            out[local_plane(core, nz, z0 + i)] = v

    backward_block(rows, nz, GROUP_MAIN, res, theirs, palette, par, grads, image, emit)


def far_backward_kernel(*refs):
    res = refs[:10]
    theirs, palette, par, near_grad, near_image, picture_h, out_h, image, grads, picture, out, sem = refs[10:]
    nz, rows, cols = out.shape
    size = GROUP_FAR[3]
    core, odd = where_am_i()
    shift = jnp.where(odd == 1, 2, rows - 2)
    unshift = jnp.where(odd == 1, rows - 2, 2)
    row = lax.broadcasted_iota(jnp.int32, (rows, cols), 0)
    low = odd * (rows - 4)
    mask = (row >= low) & (row < low + 4)

    def emit(z0, values):
        ats = [local_plane(core, nz, z0 + i) for i in range(len(values))]
        nears = [near_grad[at] for at in ats]
        both = [pltpu.roll(jnp.concatenate([v, v], axis=0), shift, axis=0) for v in values]
        both = [jnp.where(mask, b, v) for b, v in zip(both, nears)]
        for at, b in zip(ats, both):
            out[at] = b
        send(out, out_h, z0).start()

    def send(a, b, z0):
        at = pl.ds(jnp.where(core == 0, z0, nz - size - z0), size)
        return pltpu.make_async_copy(a.at[at], b.at[at], sem.at[z0 // size])

    backward_block(8, nz, GROUP_FAR, res, theirs, palette, par, grads, image, emit)
    low = odd * (rows - 2)
    mask2 = (row >= low) & (row < low + 2)
    for c in range(3):
        both = pltpu.roll(jnp.concatenate([image[c], image[c]], axis=0), shift, axis=0)
        whole = jnp.where(mask2, both, pltpu.roll(near_image[c], unshift, axis=0))
        picture[c] = jnp.where(core == 0, whole[:8], whole[8:])
    shown = pltpu.make_async_copy(picture, picture_h, sem.at[nz // size])
    shown.start()
    for z0 in range(0, nz, size):
        send(out, out_h, z0).wait()
    shown.wait()


def shards(density, absorption, view_dir, target_ids, palette, emission_coef, light):
    nz, rows, cols = density.shape
    tiles = lax.axis_size("tile")
    sds = resident

    zmsg, dens, pix, pal, par = call(
        fetch_kernel,
        (sds(HALO, rows, cols), sds(nz, rows, cols), sds(PIX, rows, cols), sds(*palette.shape), sds(15, 8, 128)),
        (density, absorption, target_ids, view_dir, palette, emission_coef, light),
        [HBM] * 7,
        scratch=[
            pltpu.VMEM((rows, cols), jnp.int32),
            pltpu.SMEM(view_dir.shape, jnp.int32),
            pltpu.SMEM(emission_coef.shape, F32),
            pltpu.SMEM(light.shape, F32),
            pltpu.SemaphoreType.DMA((7,)),
        ],
    )
    xmsg, lmsg = call(edges_kernel, (sds(nz + PIX, HALO, cols), sds(nz + PIX, HALO, cols)), (dens, pix), [VMEM] * 2)
    swap = [(0, 1), (1, 0)]
    near = [(i, i ^ 1) for i in range(tiles)]
    far = [(i, i + 1 if i % 2 else i - 1) for i in range(1, tiles - 1)]
    zrecv = lax.ppermute(zmsg, "depth", swap)
    xrecv = lax.ppermute(xmsg, "tile", near)
    lmsg = call(corner_kernel, sds(HALO + nz + PIX, HALO, cols), (zrecv, lmsg), [VMEM, VMEM])
    lrecv = lax.ppermute(lmsg, "tile", far)
    xcorner = lax.ppermute(xrecv[:HALO], "depth", swap)

    def residuals(band):
        planes = nz + 2
        return (
            sds(nz + 4, band + 8, cols),
            sds(planes, band, cols),
            sds(planes, band, cols),
            sds(planes, band, cols),
            sds(planes, band, cols),
            sds(planes + 1, band, cols),
            sds(planes, band, cols),
            sds(planes, band, cols),
            sds(4, band, cols),
            sds(PIX, band, cols),
        )

    main = call(main_forward_kernel, residuals(rows), (dens, pix, zrecv, xrecv, xcorner, par), [VMEM] * 6)
    theirs = lax.ppermute(main[8], "depth", swap)
    near_grad, near_image = call(
        main_backward_kernel,
        (sds(nz, rows, cols), sds(3, rows, cols)),
        (*main, theirs, pal, par),
        [VMEM] * 13,
        scratch=[pltpu.VMEM((nz + 2, rows, cols), F32)],
    )
    lrecv, near_image = lax.optimization_barrier((lrecv, near_image))
    edge = call(far_forward_kernel, residuals(8), (dens, pix, zrecv, lrecv, par), [VMEM] * 5)
    theirs = lax.ppermute(edge[8], "depth", swap)
    picture, grad = call(
        far_backward_kernel,
        (jax.ShapeDtypeStruct((3, 8, cols), F32), jax.ShapeDtypeStruct((nz, rows, cols), F32)),
        (*edge, theirs, pal, par, near_grad, near_image),
        [VMEM] * 15,
        scratch=[
            pltpu.VMEM((3, 8, cols), F32),
            pltpu.VMEM((nz + 2, 8, cols), F32),
            pltpu.VMEM((3, 8, cols), F32),
            pltpu.VMEM((nz, rows, cols), F32),
            pltpu.SemaphoreType.DMA((nz // GROUP_FAR[3] + 1,)),
        ],
        out_specs=(HBM, HBM),
    )
    return picture, grad


def solution(mesh):
    placed = (P("depth", "tile", None), P("tile", None), P("tile"), P("tile", None), P(), P(), P())
    return jax.shard_map(
        shards,
        mesh=mesh,
        in_specs=placed,
        out_specs=(P(None, ("tile", "depth"), None), P("depth", "tile", None)),
        check_vma=False,
    )
```

time: 42.1 us -> 18.7 us (0.44)
  the two profiles are of different devices: /device:TPU:0 before, /device:TPU:9 now
where the time goes in v3:
time: 18.7 us; the launch traced here: 18.6 us
  starting transfers between devices  7.42 us (40%)
  Pallas kernels  6.91 us (37%)
  waiting for transfers between devices  3.52 us (19%)
  between operations  0.71 us (4%)
    pallas_call x7, Pallas kernels, call(): pl.pallas_call(kernel, out_shape=outs, in_specs=specs, out_specs=out_spec...  6.91 us
    ppermute x1, starting transfers between devices, shards(): lrecv = lax.ppermute(lmsg, 'tile', far)  3 us
    ppermute x1, starting transfers between devices, shards(): xrecv = lax.ppermute(xmsg, 'tile', near)  1.28 us
    ppermute x1, starting transfers between devices, shards(): theirs = lax.ppermute(edge[8], 'depth', swap)  1.08 us
    ppermute x1, starting transfers between devices, shards(): zrecv = lax.ppermute(zmsg, 'depth', swap)  0.96 us
    ppermute x1, waiting for transfers between devices, shards(): theirs = lax.ppermute(main[8], 'depth', swap)  0.91 us
    ppermute x1, waiting for transfers between devices, shards(): zrecv = lax.ppermute(zmsg, 'depth', swap)  0.9 us
    ppermute x1, waiting for transfers between devices, shards(): theirs = lax.ppermute(edge[8], 'depth', swap)  0.86 us
  transfers between devices with their start and end apart: 6, of which 4 were waited for; matrix products, arithmetic and copies ran while one was open for 0% of the time, Pallas kernels for 18%

profile of v3, /device:TPU:9, one launch (start us, length us, event | category | flops | bytes accessed | tf_op | source)
XLA Modules:
  0.0 18.6 jit_solution(5563101065598079237)
XLA Ops:
  0.6 1.1 %shard_map.86 = (f32[4,16,256]{2,1,0:T(8,128)S(1)}, f32[32,16,256]{2,1,0:T(8,128)S(1)}, f32[3,16,256]{2,1,0:T(8,128)S(1)}, f32[3,128]{1,0:T(4,128)S(1)}, f32[15,8,128]{2,1,0:T(8,128)S(1)}) custom-call(f32[32,16,256]{2,1,0:T(8,128)} %dens_h.1, f32[16,256]{1,0:T(8,128)} %absorb_h.1, s32[16,256]{1,0:T(8,128)} %ids_h.1, s32[16]{0:T(128)} %view_h.1, ...), custom_call_target="tpu_custom_call" | custom-call | tf_op jit(solution)/shard_map/pallas_call | solution.py:20
  1.8 0.1 shard_map.87
  1.8 1.3 %collective-permute-start.2 = (f32[35,4,256]{2,1,0:T(4,128)S(1)}, f32[35,4,256]{2,1,0:T(4,128)S(1)}, u32[]{:S(2)}, u32[]{:S(2)}) collective-permute-start(f32[35,4,256]{2,1,0:T(4,128)S(1)} %get-tuple-element.37), channel_id=1, source_target_pairs={{0,2},{2,0},{4,6},{6,4},{8,10},{10,8},{12,14},{14,12},{16,18},{18,... | collective-permute-start | bytes 430088 | tf_op jit(solution)/shard_map/ppermute | solution.py:458
  3.1 1.0 %collective-permute-start = (f32[4,16,256]{2,1,0:T(8,128)S(1)}, f32[4,16,256]{2,1,0:T(8,128)S(1)}, u32[]{:S(2)}, u32[]{:S(2)}) collective-permute-start(f32[4,16,256]{2,1,0:T(8,128)S(1)} %get-tuple-element.35), channel_id=1, source_target_pairs={{0,1},{1,0},{2,3},{3,2},{4,5},{5,4},{6,7},{7,6},{8,9},{9,8},{10,11... | collective-permute-start | bytes 196616 | tf_op jit(solution)/shard_map/ppermute | solution.py:457
  4.1 0.9 %collective-permute-done.zrecv = f32[4,16,256]{2,1,0:T(8,128)S(1)} collective-permute-done((f32[4,16,256]{2,1,0:T(8,128)S(1)}, f32[4,16,256]{2,1,0:T(8,128)S(1)}, u32[]{:S(2)}, u32[]{:S(2)}) %collective-permute-start) | collective-permute-done | bytes 65568 | tf_op jit(solution)/shard_map/ppermute | solution.py:457
  5.0 3.0 %collective-permute-start.1 = (f32[39,4,256]{2,1,0:T(4,128)S(1)}, f32[39,4,256]{2,1,0:T(4,128)S(1)}, u32[]{:S(2)}, u32[]{:S(2)}) collective-permute-start(f32[39,4,256]{2,1,0:T(4,128)S(1)} %shard_map.88), channel_id=1, source_target_pairs={{2,4},{4,2},{6,8},{8,6},{10,12},{12,10},{14,16},{16,14},{18,20},{2... | collective-permute-start | bytes 479240 | tf_op jit(solution)/shard_map/ppermute | solution.py:460
  8.0 0.0 collective-permute-done.2.xrecv
  8.0 0.7 %collective-permute-start.3 = (f32[4,4,256]{2,1,0:T(4,128)S(1)}, f32[4,4,256]{2,1,0:T(4,128)S(1)}, u32[]{:S(2)}, u32[]{:S(2)}) collective-permute-start(f32[4,4,256]{2,1,0:T(4,128)S(1)} %slice.4), channel_id=1, source_target_pairs={{0,1},{1,0},{2,3},{3,2},{4,5},{5,4},{6,7},{7,6},{8,9},{9,8},{10,11... | collective-permute-start | bytes 49160 | tf_op jit(solution)/shard_map/ppermute | solution.py:461
  8.7 0.8 %collective-permute-done.3.xcorner = f32[4,4,256]{2,1,0:T(4,128)S(1)} collective-permute-done((f32[4,4,256]{2,1,0:T(4,128)S(1)}, f32[4,4,256]{2,1,0:T(4,128)S(1)}, u32[]{:S(2)}, u32[]{:S(2)}) %collective-permute-start.3) | collective-permute-done | bytes 16416 | tf_op jit(solution)/shard_map/ppermute | solution.py:461
  9.6 1.6 %shard_map.89 = (f32[36,24,256]{2,1,0:T(8,128)S(1)}, f32[34,16,256]{2,1,0:T(8,128)S(1)}, f32[34,16,256]{2,1,0:T(8,128)S(1)}, f32[34,16,256]{2,1,0:T(8,128)S(1)},...) custom-call(f32[32,16,256]{2,1,0:T(8,128)S(1)} %get-tuple-element.33, ...), custom_call_target="tpu_custom_call" | custom-call | tf_op jit(solution)/shard_map/pallas_call | solution.py:20
  11.2 0.4 %collective-permute-start.4 = (f32[4,16,256]{2,1,0:T(8,128)S(1)}, f32[4,16,256]{2,1,0:T(8,128)S(1)}, u32[]{:S(2)}, u32[]{:S(2)}) collective-permute-start(f32[4,16,256]{2,1,0:T(8,128)S(1)} %get-tuple-element.47.refs_8_), channel_id=1, source_target_pairs={{0,1},{1,0},{2,3},{3,2},{4,5},{5,4},{6,7},{7,6},{8,9},{9,8},{10,11... | collective-permute-start | bytes 196616 | tf_op jit(solution)/shard_map/ppermute | solution.py:479
  11.6 0.9 %collective-permute-done.4.refs_10_ = f32[4,16,256]{2,1,0:T(8,128)S(1)} collective-permute-done((f32[4,16,256]{2,1,0:T(8,128)S(1)}, f32[4,16,256]{2,1,0:T(8,128)S(1)}, u32[]{:S(2)}, u32[]{:S(2)}) %collective-permute-start.4) | collective-permute-done | bytes 65568 | tf_op jit(solution)/shard_map/ppermute | solution.py:479
  12.5 1.7 %shard_map.90 = (f32[32,16,256]{2,1,0:T(8,128)S(1)}, f32[3,16,256]{2,1,0:T(8,128)S(1)}) custom-call(f32[36,24,256]{2,1,0:T(8,128)S(1)} %get-tuple-element.39.refs_0_, f32[34,16,256]{2,1,0:T(8,128)S(1)} %get-tuple-element.40.refs_1_, f32[34,16,256]{2,1,0:T(8,128)S(1)} %get-tuple-element.41.refs_2_, f32[34,16,256]{2,1,0:T(8,128)S(1)} %get-tuple-element.42.refs_3_, ...), custom_call_target="tpu_custom_call" | custom-call | tf_op jit(solution)/shard_map/pallas_call | solution.py:20
  14.2 0.0 collective-permute-done.1.lrecv
  14.2 0.9 %shard_map.91 = (f32[36,16,256]{2,1,0:T(8,128)S(1)}, f32[34,8,256]{2,1,0:T(8,128)S(1)}, f32[34,8,256]{2,1,0:T(8,128)S(1)}, f32[34,8,256]{2,1,0:T(8,128)S(1)}, f3...) custom-call(f32[32,16,256]{2,1,0:T(8,128)S(1)} %get-tuple-element.33, ...), custom_call_target="tpu_custom_call" | custom-call | tf_op jit(solution)/shard_map/pallas_call | solution.py:20
  15.1 1.1 %collective-permute-start.5 = (f32[4,8,256]{2,1,0:T(8,128)S(1)}, f32[4,8,256]{2,1,0:T(8,128)S(1)}, u32[]{:S(2)}, u32[]{:S(2)}) collective-permute-start(f32[4,8,256]{2,1,0:T(8,128)S(1)} %get-tuple-element.60.refs_8_), channel_id=1, source_target_pairs={{0,1},{1,0},{2,3},{3,2},{4,5},{5,4},{6,7},{7,6},{8,9},{9,8},{10,11... | collective-permute-start | bytes 98312 | tf_op jit(solution)/shard_map/ppermute | solution.py:489
  16.2 0.9 %collective-permute-done.5.refs_10_ = f32[4,8,256]{2,1,0:T(8,128)S(1)} collective-permute-done((f32[4,8,256]{2,1,0:T(8,128)S(1)}, f32[4,8,256]{2,1,0:T(8,128)S(1)}, u32[]{:S(2)}, u32[]{:S(2)}) %collective-permute-start.5) | collective-permute-done | bytes 32800 | tf_op jit(solution)/shard_map/ppermute | solution.py:489
  17.0 1.5 %shard_map.92 = (f32[3,8,256]{2,1,0:T(8,128)}, f32[32,16,256]{2,1,0:T(8,128)}) custom-call(f32[36,16,256]{2,1,0:T(8,128)S(1)} %get-tuple-element.52.refs_0_, f32[34,8,256]{2,1,0:T(8,128)S(1)} %get-tuple-element.53.refs_1_, f32[34,8,256]{2,1,0:T(8,128)S(1)} %get-tuple-element.54.refs_2_, f32[34,8,256]{2,1,0:T(8,128)S(1)} %get-tuple-element.55.refs_3_, ...), custom_call_target="tpu_custom_call" | custom-call | tf_op jit(solution)/shard_map/pallas_call | solution.py:20
  (2 shorter events, 0.0 us)
Async XLA Ops:
  1.8 6.2 %collective-permute-start.2 = (f32[35,4,256]{2,1,0:T(4,128)S(1)}, f32[35,4,256]{2,1,0:T(4,128)S(1)}, u32[]{:S(2)}, u32[]{:S(2)}) collective-permute-start(f32[35,4,256]{2,1,0:T(4,128)S(1)} %get-tuple-element.37), channel_id=1, source_target_pairs={{0,2},{2,0},{4,6},{6,4},{8,10},{10,8},{12,14},{14,12},{16,18},{18,... | collective-permute-start | bytes 430088 | tf_op jit(solution)/shard_map/ppermute | solution.py:458
  3.1 1.9 %collective-permute-start = (f32[4,16,256]{2,1,0:T(8,128)S(1)}, f32[4,16,256]{2,1,0:T(8,128)S(1)}, u32[]{:S(2)}, u32[]{:S(2)}) collective-permute-start(f32[4,16,256]{2,1,0:T(8,128)S(1)} %get-tuple-element.35), channel_id=1, source_target_pairs={{0,1},{1,0},{2,3},{3,2},{4,5},{5,4},{6,7},{7,6},{8,9},{9,8},{10,11... | collective-permute-start | bytes 196616 | tf_op jit(solution)/shard_map/ppermute | solution.py:457
  5.0 9.2 %collective-permute-start.1 = (f32[39,4,256]{2,1,0:T(4,128)S(1)}, f32[39,4,256]{2,1,0:T(4,128)S(1)}, u32[]{:S(2)}, u32[]{:S(2)}) collective-permute-start(f32[39,4,256]{2,1,0:T(4,128)S(1)} %shard_map.88), channel_id=1, source_target_pairs={{2,4},{4,2},{6,8},{8,6},{10,12},{12,10},{14,16},{16,14},{18,20},{2... | collective-permute-start | bytes 479240 | tf_op jit(solution)/shard_map/ppermute | solution.py:460
  8.0 1.5 %collective-permute-start.3 = (f32[4,4,256]{2,1,0:T(4,128)S(1)}, f32[4,4,256]{2,1,0:T(4,128)S(1)}, u32[]{:S(2)}, u32[]{:S(2)}) collective-permute-start(f32[4,4,256]{2,1,0:T(4,128)S(1)} %slice.4), channel_id=1, source_target_pairs={{0,1},{1,0},{2,3},{3,2},{4,5},{5,4},{6,7},{7,6},{8,9},{9,8},{10,11... | collective-permute-start | bytes 49160 | tf_op jit(solution)/shard_map/ppermute | solution.py:461
  11.2 1.3 %collective-permute-start.4 = (f32[4,16,256]{2,1,0:T(8,128)S(1)}, f32[4,16,256]{2,1,0:T(8,128)S(1)}, u32[]{:S(2)}, u32[]{:S(2)}) collective-permute-start(f32[4,16,256]{2,1,0:T(8,128)S(1)} %get-tuple-element.47.refs_8_), channel_id=1, source_target_pairs={{0,1},{1,0},{2,3},{3,2},{4,5},{5,4},{6,7},{7,6},{8,9},{9,8},{10,11... | collective-permute-start | bytes 196616 | tf_op jit(solution)/shard_map/ppermute | solution.py:479
  15.1 1.9 %collective-permute-start.5 = (f32[4,8,256]{2,1,0:T(8,128)S(1)}, f32[4,8,256]{2,1,0:T(8,128)S(1)}, u32[]{:S(2)}, u32[]{:S(2)}) collective-permute-start(f32[4,8,256]{2,1,0:T(8,128)S(1)} %get-tuple-element.60.refs_8_), channel_id=1, source_target_pairs={{0,1},{1,0},{2,3},{3,2},{4,5},{5,4},{6,7},{7,6},{8,9},{9,8},{10,11... | collective-permute-start | bytes 98312 | tf_op jit(solution)/shard_map/ppermute | solution.py:489

commit v4 on v3

--- a/solution.py
+++ b/solution.py
@@ -5,11 +5,13 @@
 from jax.experimental.pallas import tpu as pltpu
 from jax.sharding import PartitionSpec as P
 
+
 F32 = jnp.float32
 HALO = 4
 PIX = 3
-GROUP_MAIN = (16,16,16,16)
-GROUP_FAR = (16,16,34,32)
+GROUP_MAIN = (8,16,17,16)
+GROUP_FAR = (30,32,34,32)
+CHUNK = 8
 LATE = True
 VMEM = pl.BlockSpec(memory_space=pltpu.VMEM)
 HBM = pl.BlockSpec(memory_space=pl.ANY)
@@ -42,11 +44,29 @@
 
 def in_groups(body, count, group, carry):
     full = count // group
-    if full:
-        carry = lax.fori_loop(0, full, lambda i, c: body(i * group, group, c), carry)
+    for i in range(full):
+        carry = body(i * group, group, carry)
     if count % group:
         carry = body(full * group, count % group, carry)
     return carry
+
+
+class Joined:
+    def __init__(self, head, tail, cut):
+        self.head, self.tail, self.cut = head, tail, cut
+        self.shape = (cut + tail.shape[0], *tail.shape[1:])
+
+    def find(self, key):
+        at, *rest = key if isinstance(key, tuple) else (key,)
+        return (self.head, (at, *rest)) if at < self.cut else (self.tail, (at - self.cut, *rest))
+
+    def __getitem__(self, key):
+        ref, at = self.find(key)
+        return ref[at]
+
+    def __setitem__(self, key, value):
+        ref, at = self.find(key)
+        ref[at] = value
 
 
 class Stores:
@@ -72,7 +92,7 @@
 
 def fetch_kernel(dens_h, absorb_h, ids_h, view_h, pal_h, coef_h, light_h, zmsg, dens, pix, pal, par, ids, view, coef, light, sem):
     nz, rows, cols = dens.shape
-    core, odd = where_am_i()
+    core, _ = where_am_i()
     pairs = ((dens_h, dens), (view_h, view), (ids_h, ids), (absorb_h, pix.at[0]), (coef_h, coef), (light_h, light), (pal_h, pal))
     copies = [pltpu.make_async_copy(a, b, sem.at[i]) for i, (a, b) in enumerate(pairs)]
     for c in copies:
@@ -98,7 +118,7 @@
 
 
 def edges_kernel(dens, pix, xmsg, lmsg):
-    nz, rows, cols = dens.shape
+    nz, rows, _ = dens.shape
     core, odd = where_am_i()
 
     def edges(plane, to):
@@ -147,7 +167,7 @@
         return pltpu.roll(jnp.concatenate([self.own(z), h, h], axis=0), self.shift, axis=0)
 
 
-def pixels(block, core, depth):
+def pixels(block, core):
     a, ids, view = [block.plane(-1 - j)[: block.band] for j in range(PIX)]
     back = jnp.where(core == 0, view, 1.0 - view)
     return a, ids, back
@@ -179,7 +199,7 @@
 
 
 def smooth_slab(block, core, depth, group, smooth, taus, sig, pixo):
-    a, ids, back = pixels(block, core, depth)
+    a, ids, back = pixels(block, core)
     signed = a * (1.0 / (2 * depth)) * (1.0 - 2.0 * back)
     pixo[0], pixo[1], pixo[2] = a, ids, back
     face = block.plane(0)
@@ -273,7 +293,7 @@
 
 
 def far_forward_kernel(dens, pix, zrecv, lrecv, par, smooth, dxs, dys, rnorm, phis, edge, sig, taus, mid, pixo):
-    nz, rows, cols = dens.shape
+    nz, rows, _ = dens.shape
     core, odd = where_am_i()
     at = pl.multiple_of(odd * (rows - 8), 8)
 
@@ -294,65 +314,94 @@
     shade_slab(8, nz, GROUP_FAR[1], total, par, smooth, taus, dxs, dys, rnorm, phis, edge, mid, pixo)
 
 
-def main_forward_kernel(dens, pix, zrecv, xrecv, xcorner, par, smooth, dxs, dys, rnorm, phis, edge, sig, taus, mid, pixo):
-    nz, rows, cols = dens.shape
+def main_smooth_kernel(dens, pix, xrecv, smooth, taus, sig, pixo, total):
     core, _ = where_am_i()
+    block = main_block(dens, pix, xrecv)
+    total[...] = smooth_slab(block, core, dens.shape[0], GROUP_MAIN[0], smooth, taus, sig, pixo)
+
+
+def joined(depth, refs):
+    smooth, taus, sig, smooth_tail, taus_tail, sig_tail = refs
+    return Joined(smooth, smooth_tail, depth), Joined(taus, taus_tail, depth - 1), Joined(sig, sig_tail, depth - 1)
+
+
+def main_shade_kernel(smooth, taus, sig, pixo, total, dens, pix, zrecv, xrecv, xcorner, par, smooth_tail, taus_tail, sig_tail, *rest):
+    nz, rows, _ = dens.shape
     block = main_block(dens, pix, xrecv, zrecv, xcorner)
-    total = smooth_slab(block, core, nz, GROUP_MAIN[0], smooth, taus, sig, pixo)
-    total = smooth_seam(block, nz, smooth, taus, sig, pixo, total)
-    shade_slab(rows, nz, GROUP_MAIN[1], total, par, smooth, taus, dxs, dys, rnorm, phis, edge, mid, pixo)
-
-
-def backward_block(band, depth, groups, res, theirs, palette, par, grads, image, emit):
-    smooth, dxs, dys, rnorm, phis, edge, sig, taus, mid, pixo = res
+    smooth, taus, sig = joined(nz, (smooth, taus, sig, smooth_tail, taus_tail, sig_tail))
+    whole = smooth_seam(block, nz, smooth, taus, sig, pixo, total[...])
+    shade_slab(rows, nz, GROUP_MAIN[1], whole, par, smooth, taus, *rest, pixo)
+
+
+def prepare_block(band, depth, group, smooth, dxs, dys, rnorm, phis, edge, sig, pixo, palette, par, bx, by, bz, gained, damped, targets):
     cols = smooth.shape[2]
-    back = pixo[2] == 1.0
-    sign = jnp.where(back, -1.0, 1.0)
-    mine_total, their_total = mid[0], theirs[0]
-    through_me, through_them = jnp.exp(-mine_total), jnp.exp(-their_total)
-    target = lookup(palette, pixo[1])
-    g, flow = [], jnp.zeros_like(sign)
-    for c in range(3):
-        mine, other = mid[1 + c], theirs[1 + c]
-        pic = jnp.where(back, other + through_them * mine, mine + through_me * other)
-        image[c] = pic
-        err = (pic - target[c]) * (2.0 * depth)
-        g.append(err)
-        flow = flow + err * pic
-    kappa = jnp.where(back, 0.5 * through_them, 0.5)
-    gam = []
-    for k in range(4):
-        k0, k1, k2 = [spread(par, 4 * c + k, band, cols) for c in range(3)]
-        gam.append(kappa * (g[0] * k0 + g[1] * k1 + g[2] * k2))
-    gam2, gam3 = 2.0 * gam[2], 3.0 * gam[3]
-    queue = jnp.where(back, 0.0, -flow)
+    sign = 1.0 - 2.0 * pixo[2]
     weight = pixo[0] * (1.0 / (2 * depth))
     lz, ly, lx = [spread(par, 12 + i, band, cols) for i in range(3)]
-
-    def shade_back(z0, n, carry):
-        run, part, last = carry
+    for c, t in enumerate(lookup(palette, pixo[1])):
+        targets[c] = t
+
+    def body(z0, n, carry):
         out = Stores()
         planes = [smooth[z0 + i, pl.ds(0, band)] for i in range(n + 2)]
         edges = [edge[z0 + i] for i in range(n + 1)]
         rest = [(phis[z0 + i], rnorm[z0 + i], sig[z0 + i], dys[z0 + i], dxs[z0 + i]) for i in range(n)]
         for i in range(n):
-            s = planes[i + 1]
+            phi, r, sg, dy, dx = rest[i]
             dz = planes[i + 2] - planes[i]
-            phi, r, sg, dy, dx = rest[i]
+            w = sign * (edges[i] - edges[i + 1])
+            p = w * r
+            q = p * (phi * r)
+            out.put(bx, z0 + i, p * lx - q * dx)
+            out.put(by, z0 + i, p * ly - q * dy)
+            out.put(bz, z0 + i, p * lz - q * dz)
+            out.put(gained, z0 + i, w * (1.0 + phi))
+            out.put(damped, z0 + i, weight * sg)
+        out.flush()
+        return carry
+
+    in_groups(body, depth + 2, group, 0)
+
+
+def backward_block(band, depth, group, smooth, phis, edge, bx, by, bz, gained, damped, targets, mid, pixo, theirs, par, image, grads):
+    cols = smooth.shape[2]
+    back = pixo[2] == 1.0
+    through_me, through_them = jnp.exp(-mid[0]), jnp.exp(-theirs[0])
+    g, flow = [], jnp.zeros_like(through_me)
+    for c in range(3):
+        mine, other = mid[1 + c], theirs[1 + c]
+        pic = jnp.where(back, other + through_them * mine, mine + through_me * other)
+        image[c] = pic
+        err = (pic - targets[c]) * (2.0 * depth)
+        g.append(err)
+        flow = flow + err * pic
+    kappa = jnp.where(back, 0.5 * through_them, 0.5)
+    g = [kappa * e for e in g]
+    gam = []
+    for k in range(4):
+        k0, k1, k2 = [spread(par, 4 * c + k, band, cols) for c in range(3)]
+        gam.append(g[0] * k0 + g[1] * k1 + g[2] * k2)
+    queue = jnp.where(back, 0.0, -flow)
+
+    def shade_back(z0, n, carry):
+        run, part, last = carry
+        out = Stores()
+        rest = [[ref[z0 + i] for ref in (phis, bx, by, bz, gained, damped)] for i in range(n)]
+        values = [smooth[z0 + i + 1, pl.ds(0, band)] for i in range(n)]
+        edges = [edge[z0 + i] for i in range(n + 1)]
+        for i in range(n):
+            s = values[i]
+            phi, dx, dy, dz, gain, damp = rest[i]
             near, far = edges[i], edges[i + 1]
-            shade = 1.0 + phi
-            poly = gam[0] + s * (gam[1] + s * (gam[2] + s * gam[3]))
-            slope = gam[1] + s * (gam2 + s * gam3)
-            h = shade * poly
-            lost = near - far
-            w = sign * lost
-            mine = (near * h + run) * (weight * sg) + (w * shade) * slope
-            run = run + lost * h
-            t1 = w * poly * r
-            t3 = t1 * phi * r
-            az = t1 * lz - t3 * dz
-            ay = t1 * ly - t3 * dy
-            ax = t1 * lx - t3 * dx
+            top = s * gam[3]
+            inner = gam[2] + top
+            outer = gam[1] + s * inner
+            poly = gam[0] + s * outer
+            slope = outer + s * (inner + top)
+            h = poly + phi * poly
+            mine = (near * h + run) * damp + gain * slope
+            run = run + (near - far) * h
+            az, ay, ax = dz * poly, dy * poly, dx * poly
             out.put(grads, z0 + i, part - az)
             part = mine + last
             part = part + (pltpu.roll(ay, 1, axis=0) - pltpu.roll(ay, band - 1, axis=0))
@@ -361,8 +410,12 @@
         out.flush()
         return run, part, last
 
-    nil = jnp.zeros_like(sign)
-    in_groups(shade_back, depth + 2, groups[2], (queue, nil, nil))
+    nil = jnp.zeros_like(through_me)
+    in_groups(shade_back, depth + 2, group, (queue, nil, nil))
+
+
+def smooth_transpose(band, depth, group, grads, emit):
+    cols = grads.shape[2]
 
     def smooth_back(z0, n, carry):
         planes = [grads[z0 + i] for i in range(n + 2)]
@@ -373,39 +426,61 @@
             t = t + pltpu.roll(here, 1, axis=0) + pltpu.roll(here, band - 1, axis=0)
             t = t + pltpu.roll(here, 1, axis=1) + pltpu.roll(here, cols - 1, axis=1)
             done.append(t * 0.125)
-        emit(z0, done)
+            if len(done) == CHUNK:
+                emit(z0 + i + 1 - CHUNK, done)
+                done = []
         return carry
 
-    in_groups(smooth_back, depth, groups[3], 0)
-
-
-def main_backward_kernel(*refs):
-    res, (theirs, palette, par, out, image, grads) = refs[:10], refs[10:]
-    nz, rows, cols = out.shape
+    in_groups(smooth_back, depth, group, 0)
+
+
+def main_prepare_kernel(*refs):
+    slab, (dxs, dys, rnorm, phis, edge, pixo, palette, par, *out) = refs[:6], refs[6:]
+    nz, rows = slab[0].shape[0], dxs.shape[1]
+    smooth, _, sig = joined(nz, slab)
+    prepare_block(rows, nz, GROUP_MAIN[2], smooth, dxs, dys, rnorm, phis, edge, sig, pixo, palette, par, *out)
+
+
+def main_backward_kernel(smooth, smooth_tail, *refs):
+    nz, rows = smooth.shape[0], refs[0].shape[1]
+    backward_block(rows, nz, GROUP_MAIN[2], Joined(smooth, smooth_tail, nz), *refs)
+
+
+def far_prepare_kernel(smooth, *refs):
+    prepare_block(8, smooth.shape[0] - HALO, GROUP_FAR[2], smooth, *refs)
+
+
+def main_result_kernel(grads, image, out, shown):
+    nz, rows, _ = out.shape
     core, odd = where_am_i()
     shift = jnp.where(odd == 1, rows - 2, 2)
+    for c in range(3):
+        shown[c] = pltpu.roll(image[c], shift, axis=0)
 
     def emit(z0, values):
         values = [pltpu.roll(v, shift, axis=0) for v in values]
         for i, v in enumerate(values):
             out[local_plane(core, nz, z0 + i)] = v
 
-    backward_block(rows, nz, GROUP_MAIN, res, theirs, palette, par, grads, image, emit)
+    smooth_transpose(rows, nz, GROUP_MAIN[3], grads, emit)
 
 
 def far_backward_kernel(*refs):
-    res = refs[:10]
-    theirs, palette, par, near_grad, near_image, picture_h, out_h, image, grads, picture, out, sem = refs[10:]
+    res = refs[:13]
+    near_grad, near_image, picture_h, out_h, image, grads, picture, out, sem = refs[13:]
     nz, rows, cols = out.shape
-    size = GROUP_FAR[3]
+    size = CHUNK
     core, odd = where_am_i()
     shift = jnp.where(odd == 1, 2, rows - 2)
-    unshift = jnp.where(odd == 1, rows - 2, 2)
     row = lax.broadcasted_iota(jnp.int32, (rows, cols), 0)
     low = odd * (rows - 4)
     mask = (row >= low) & (row < low + 4)
 
     def emit(z0, values):
+        for i in range(0, len(values), size):
+            emit_chunk(z0 + i, values[i : i + size])
+
+    def emit_chunk(z0, values):
         ats = [local_plane(core, nz, z0 + i) for i in range(len(values))]
         nears = [near_grad[at] for at in ats]
         both = [pltpu.roll(jnp.concatenate([v, v], axis=0), shift, axis=0) for v in values]
@@ -418,12 +493,13 @@
         at = pl.ds(jnp.where(core == 0, z0, nz - size - z0), size)
         return pltpu.make_async_copy(a.at[at], b.at[at], sem.at[z0 // size])
 
-    backward_block(8, nz, GROUP_FAR, res, theirs, palette, par, grads, image, emit)
+    backward_block(8, nz, GROUP_FAR[2], *res, image, grads)
+    smooth_transpose(8, nz, GROUP_FAR[3], grads, emit)
     low = odd * (rows - 2)
     mask2 = (row >= low) & (row < low + 2)
     for c in range(3):
         both = pltpu.roll(jnp.concatenate([image[c], image[c]], axis=0), shift, axis=0)
-        whole = jnp.where(mask2, both, pltpu.roll(near_image[c], unshift, axis=0))
+        whole = jnp.where(mask2, both, near_image[c])
         picture[c] = jnp.where(core == 0, whole[:8], whole[8:])
     shown = pltpu.make_async_copy(picture, picture_h, sem.at[nz // size])
     shown.start()
@@ -475,29 +551,61 @@
             sds(PIX, band, cols),
         )
 
-    main = call(main_forward_kernel, residuals(rows), (dens, pix, zrecv, xrecv, xcorner, par), [VMEM] * 6)
-    theirs = lax.ppermute(main[8], "depth", swap)
-    near_grad, near_image = call(
+    parts = residuals(rows)
+    smooth, taus, sig, pixo, total = call(
+        main_smooth_kernel,
+        (sds(nz, rows + 8, cols), sds(nz - 1, rows, cols), sds(nz - 1, rows, cols), parts[9], sds(rows, cols)),
+        (dens, pix, xrecv),
+        [VMEM] * 3,
+    )
+    xcorner, total = lax.optimization_barrier((xcorner, total))
+    *tails, dxs, dys, rnorm, phis, edge, mid = call(
+        main_shade_kernel,
+        (sds(4, rows + 8, cols), sds(3, rows, cols), sds(3, rows, cols), *parts[1:6], parts[8]),
+        (smooth, taus, sig, pixo, total, dens, pix, zrecv, xrecv, xcorner, par),
+        [VMEM] * 11,
+    )
+    theirs = lax.ppermute(mid, "depth", swap)
+
+    def prepared(band):
+        return (*[sds(nz + 2, band, cols)] * 5, sds(3, band, cols))
+
+    ready = call(
+        main_prepare_kernel,
+        prepared(rows),
+        (smooth, taus, sig, *tails, dxs, dys, rnorm, phis, edge, pixo, pal, par),
+        [VMEM] * 14,
+    )
+    near_image, grads = call(
         main_backward_kernel,
-        (sds(nz, rows, cols), sds(3, rows, cols)),
-        (*main, theirs, pal, par),
-        [VMEM] * 13,
-        scratch=[pltpu.VMEM((nz + 2, rows, cols), F32)],
+        (sds(3, rows, cols), sds(nz + 2, rows, cols)),
+        (smooth, tails[0], phis, edge, *ready, mid, pixo, theirs, par),
+        [VMEM] * 14,
     )
     lrecv, near_image = lax.optimization_barrier((lrecv, near_image))
-    edge = call(far_forward_kernel, residuals(8), (dens, pix, zrecv, lrecv, par), [VMEM] * 5)
-    theirs = lax.ppermute(edge[8], "depth", swap)
+    smooth, dxs, dys, rnorm, phis, edge, sig, taus, mid, pixo = call(
+        far_forward_kernel, residuals(8), (dens, pix, zrecv, lrecv, par), [VMEM] * 5
+    )
+    theirs = lax.ppermute(mid, "depth", swap)
+    near_image, pixo = lax.optimization_barrier((near_image, pixo))
+    near_grad, near_image = call(main_result_kernel, (sds(nz, rows, cols), sds(3, rows, cols)), (grads, near_image), [VMEM] * 2)
+    ready = call(
+        far_prepare_kernel,
+        prepared(8),
+        (smooth, dxs, dys, rnorm, phis, edge, sig, pixo, pal, par),
+        [VMEM] * 10,
+    )
     picture, grad = call(
         far_backward_kernel,
         (jax.ShapeDtypeStruct((3, 8, cols), F32), jax.ShapeDtypeStruct((nz, rows, cols), F32)),
-        (*edge, theirs, pal, par, near_grad, near_image),
+        (smooth, phis, edge, *ready, mid, pixo, theirs, par, near_grad, near_image),
         [VMEM] * 15,
         scratch=[
             pltpu.VMEM((3, 8, cols), F32),
             pltpu.VMEM((nz + 2, 8, cols), F32),
             pltpu.VMEM((3, 8, cols), F32),
             pltpu.VMEM((nz, rows, cols), F32),
-            pltpu.SemaphoreType.DMA((nz // GROUP_FAR[3] + 1,)),
+            pltpu.SemaphoreType.DMA((nz // CHUNK + 1,)),
         ],
         out_specs=(HBM, HBM),
     )

time: 18.7 us -> 18.6 us (level)
  waiting for transfers between devices: 3.52 us -> 3.29 us
    ppermute x1, waiting for transfers between devices: 0.01 us -> 1.5 us  [shards(): lrecv = lax.ppermute(lmsg, 'tile', far)]
    ppermute x2, waiting for transfers between devices: 1.77 us -> 0.77 us  [shards(): theirs = lax.ppermute(mid, 'depth', swap)]
    ppermute x1, waiting for transfers between devices: 0.84 us -> 0.11 us  [shards(): xcorner = lax.ppermute(xrecv[:HALO], 'depth', swap)]
    pallas_call x7 -> x11, Pallas kernels: 6.91 us -> 6.9 us  [call(): pl.pallas_call(kernel, out_shape=outs, in_specs=specs, out_specs=out_spec...]
  transfers between devices with their start and end apart: 6 -> 6, of which waited for: 4 -> 5; matrix products, arithmetic and copies ran while one was open for 0% -> 0% of each run, Pallas kernels for 18% -> 18%
where the time goes in v4:
time: 18.6 us; the launch traced here: 18.5 us
  starting transfers between devices  7.56 us (41%)
  Pallas kernels  6.9 us (37%)
  waiting for transfers between devices  3.29 us (18%)
  between operations  0.72 us (4%)
    pallas_call x11, Pallas kernels, call(): pl.pallas_call(kernel, out_shape=outs, in_specs=specs, out_specs=out_spec...  6.9 us
    ppermute x1, starting transfers between devices, shards(): lrecv = lax.ppermute(lmsg, 'tile', far)  3 us
    ppermute x2, starting transfers between devices, shards(): theirs = lax.ppermute(mid, 'depth', swap)  1.62 us
    ppermute x1, waiting for transfers between devices, shards(): lrecv = lax.ppermute(lmsg, 'tile', far)  1.5 us
    ppermute x1, starting transfers between devices, shards(): xrecv = lax.ppermute(xmsg, 'tile', near)  1.28 us
    ppermute x1, starting transfers between devices, shards(): zrecv = lax.ppermute(zmsg, 'depth', swap)  0.96 us
    ppermute x1, waiting for transfers between devices, shards(): zrecv = lax.ppermute(zmsg, 'depth', swap)  0.9 us
    ppermute x2, waiting for transfers between devices, shards(): theirs = lax.ppermute(mid, 'depth', swap)  0.77 us
  transfers between devices with their start and end apart: 6, of which 5 were waited for; matrix products, arithmetic and copies ran while one was open for 0% of the time, Pallas kernels for 18%

profile of v4, /device:TPU:9, one launch (start us, length us, event | category | flops | bytes accessed | tf_op | source)
XLA Modules:
  0.0 18.5 jit_solution(15048833535500561633)
XLA Ops:
  0.6 1.1 %shard_map.86 = (f32[4,16,256]{2,1,0:T(8,128)S(1)}, f32[32,16,256]{2,1,0:T(8,128)S(1)}, f32[3,16,256]{2,1,0:T(8,128)S(1)}, f32[3,128]{1,0:T(4,128)S(1)}, f32[15,8,128]{2,1,0:T(8,128)S(1)}) custom-call(f32[32,16,256]{2,1,0:T(8,128)} %dens_h.1, f32[16,256]{1,0:T(8,128)} %absorb_h.1, s32[16,256]{1,0:T(8,128)} %ids_h.1, s32[16]{0:T(128)} %view_h.1, ...), custom_call_target="tpu_custom_call" | custom-call | tf_op jit(solution)/shard_map/pallas_call | solution.py:22
  1.8 0.1 shard_map.87
  1.8 1.3 %collective-permute-start.2 = (f32[35,4,256]{2,1,0:T(4,128)S(1)}, f32[35,4,256]{2,1,0:T(4,128)S(1)}, u32[]{:S(2)}, u32[]{:S(2)}) collective-permute-start(f32[35,4,256]{2,1,0:T(4,128)S(1)} %get-tuple-element.58), channel_id=1, source_target_pairs={{0,2},{2,0},{4,6},{6,4},{8,10},{10,8},{12,14},{14,12},{16,18},{18,... | collective-permute-start | bytes 430088 | tf_op jit(solution)/shard_map/ppermute | solution.py:534
  3.1 1.0 %collective-permute-start = (f32[4,16,256]{2,1,0:T(8,128)S(1)}, f32[4,16,256]{2,1,0:T(8,128)S(1)}, u32[]{:S(2)}, u32[]{:S(2)}) collective-permute-start(f32[4,16,256]{2,1,0:T(8,128)S(1)} %get-tuple-element.56), channel_id=1, source_target_pairs={{0,1},{1,0},{2,3},{3,2},{4,5},{5,4},{6,7},{7,6},{8,9},{9,8},{10,11... | collective-permute-start | bytes 196616 | tf_op jit(solution)/shard_map/ppermute | solution.py:533
  4.1 0.9 %collective-permute-done.zrecv = f32[4,16,256]{2,1,0:T(8,128)S(1)} collective-permute-done((f32[4,16,256]{2,1,0:T(8,128)S(1)}, f32[4,16,256]{2,1,0:T(8,128)S(1)}, u32[]{:S(2)}, u32[]{:S(2)}) %collective-permute-start) | collective-permute-done | bytes 65568 | tf_op jit(solution)/shard_map/ppermute | solution.py:533
  5.0 3.0 %collective-permute-start.1 = (f32[39,4,256]{2,1,0:T(4,128)S(1)}, f32[39,4,256]{2,1,0:T(4,128)S(1)}, u32[]{:S(2)}, u32[]{:S(2)}) collective-permute-start(f32[39,4,256]{2,1,0:T(4,128)S(1)} %shard_map.88), channel_id=1, source_target_pairs={{2,4},{4,2},{6,8},{8,6},{10,12},{12,10},{14,16},{16,14},{18,20},{2... | collective-permute-start | bytes 479240 | tf_op jit(solution)/shard_map/ppermute | solution.py:536
  8.0 0.0 collective-permute-done.2.xrecv
  8.0 0.7 %collective-permute-start.3 = (f32[4,4,256]{2,1,0:T(4,128)S(1)}, f32[4,4,256]{2,1,0:T(4,128)S(1)}, u32[]{:S(2)}, u32[]{:S(2)}) collective-permute-start(f32[4,4,256]{2,1,0:T(4,128)S(1)} %slice.4), channel_id=1, source_target_pairs={{0,1},{1,0},{2,3},{3,2},{4,5},{5,4},{6,7},{7,6},{8,9},{9,8},{10,11... | collective-permute-start | bytes 49160 | tf_op jit(solution)/shard_map/ppermute | solution.py:537
  8.7 0.7 %shard_map.89 = (f32[32,24,256]{2,1,0:T(8,128)S(1)}, f32[31,16,256]{2,1,0:T(8,128)S(1)}, f32[31,16,256]{2,1,0:T(8,128)S(1)}, f32[3,16,256]{2,1,0:T(8,128)S(1)}, f32[16,256]{1,0:T(8,128)S(1)}) custom-call(f32[32,16,256]{2,1,0:T(8,128)S(1)} %get-tuple-element.54.dens, f32[3,16,256]{2,1,0:T(8,128)S(1)} %get-tuple-element.55.pix, ...), custom_call_target="tpu_custom_call" | custom-call | tf_op jit(solution)/shard_map/pallas_call | solution.py:22
  9.4 0.1 collective-permute-done.3.xcorner
  9.6 0.8 %shard_map.90 = (f32[4,24,256]{2,1,0:T(8,128)S(1)}, f32[3,16,256]{2,1,0:T(8,128)S(1)}, f32[3,16,256]{2,1,0:T(8,128)S(1)}, f32[34,16,256]{2,1,0:T(8,128)S(1)}, f3...) custom-call(f32[32,24,256]{2,1,0:T(8,128)S(1)} %get-tuple-element.59, ...), custom_call_target="tpu_custom_call" | custom-call | tf_op jit(solution)/shard_map/pallas_call | solution.py:22
  10.4 0.4 %collective-permute-start.4 = (f32[4,16,256]{2,1,0:T(8,128)S(1)}, f32[4,16,256]{2,1,0:T(8,128)S(1)}, u32[]{:S(2)}, u32[]{:S(2)}) collective-permute-start(f32[4,16,256]{2,1,0:T(8,128)S(1)} %get-tuple-element.82.refs_8_), channel_id=1, source_target_pairs={{0,1},{1,0},{2,3},{3,2},{4,5},{5,4},{6,7},{7,6},{8,9},{9,8},{10,11... | collective-permute-start | bytes 196616 | tf_op jit(solution)/shard_map/ppermute | solution.py:568
  10.8 0.4 %shard_map.91 = (f32[34,16,256]{2,1,0:T(8,128)S(1)}, f32[34,16,256]{2,1,0:T(8,128)S(1)}, f32[34,16,256]{2,1,0:T(8,128)S(1)}, f32[34,16,256]{2,1,0:T(8,128)S(1)},...) custom-call(f32[32,24,256]{2,1,0:T(8,128)S(1)} %get-tuple-element.59.smooth.refs_0_, ...), custom_call_target="tpu_custom_call" | custom-call | tf_op jit(solution)/shard_map/pallas_call | solution.py:22
  11.2 0.5 %collective-permute-done.4.refs_10_ = f32[4,16,256]{2,1,0:T(8,128)S(1)} collective-permute-done((f32[4,16,256]{2,1,0:T(8,128)S(1)}, f32[4,16,256]{2,1,0:T(8,128)S(1)}, u32[]{:S(2)}, u32[]{:S(2)}) %collective-permute-start.4) | collective-permute-done | bytes 65568 | tf_op jit(solution)/shard_map/ppermute | solution.py:568
  11.7 0.8 %shard_map.92 = (f32[3,16,256]{2,1,0:T(8,128)S(1)}, f32[34,16,256]{2,1,0:T(8,128)S(1)}) custom-call(f32[32,24,256]{2,1,0:T(8,128)S(1)} %get-tuple-element.59.smooth.refs_0_, f32[4,24,256]{2,1,0:T(8,128)S(1)} %get-tuple-element.67.refs_3_.smooth_tail, f32[34,16,256]{2,1,0:T(8,128)S(1)} %get-tuple-element.68.refs_9_.refs_0_, ...), custom_call_target="tpu_custom_call" | custom-call | tf_op jit(solution)/shard_map/pallas_call | solution.py:22
  12.5 1.5 %collective-permute-done.1.lrecv = f32[39,4,256]{2,1,0:T(4,128)S(1)} collective-permute-done((f32[39,4,256]{2,1,0:T(4,128)S(1)}, f32[39,4,256]{2,1,0:T(4,128)S(1)}, u32[]{:S(2)}, u32[]{:S(2)}) %collective-permute-start.1) | collective-permute-done | bytes 159776 | tf_op jit(solution)/shard_map/ppermute | solution.py:536
  14.0 1.2 %shard_map.93 = (f32[36,16,256]{2,1,0:T(8,128)S(1)}, f32[34,8,256]{2,1,0:T(8,128)S(1)}, f32[34,8,256]{2,1,0:T(8,128)S(1)}, f32[34,8,256]{2,1,0:T(8,128)S(1)}, f3...) custom-call(f32[32,16,256]{2,1,0:T(8,128)S(1)} %get-tuple-element.54, ...), custom_call_target="tpu_custom_call" | custom-call | tf_op jit(solution)/shard_map/pallas_call | solution.py:22
  15.2 1.2 %collective-permute-start.5 = (f32[4,8,256]{2,1,0:T(8,128)S(1)}, f32[4,8,256]{2,1,0:T(8,128)S(1)}, u32[]{:S(2)}, u32[]{:S(2)}) collective-permute-start(f32[4,8,256]{2,1,0:T(8,128)S(1)} %get-tuple-element.101.refs_9_), channel_id=1, source_target_pairs={{0,1},{1,0},{2,3},{3,2},{4,5},{5,4},{6,7},{7,6},{8,9},{9,8},{10,11... | collective-permute-start | bytes 98312 | tf_op jit(solution)/shard_map/ppermute | solution.py:589
  16.4 0.3 %shard_map.95 = (f32[32,16,256]{2,1,0:T(8,128)S(1)}, f32[3,16,256]{2,1,0:T(8,128)S(1)}) custom-call(f32[34,16,256]{2,1,0:T(8,128)S(1)} %get-tuple-element.102.grads, f32[3,16,256]{2,1,0:T(8,128)S(1)} %get-tuple-element.103.image), custom_call_target="tpu_custom_call" | custom-call | tf_op jit(solution)/shard_map/pallas_call | solution.py:22
  16.7 0.2 %shard_map.94 = (f32[34,8,256]{2,1,0:T(8,128)S(1)}, f32[34,8,256]{2,1,0:T(8,128)S(1)}, f32[34,8,256]{2,1,0:T(8,128)S(1)}, f32[34,8,256]{2,1,0:T(8,128)S(1)}, f32...) custom-call(f32[36,16,256]{2,1,0:T(8,128)S(1)} %get-tuple-element.85.smooth.refs_0_, ...), custom_call_target="tpu_custom_call" | custom-call | tf_op jit(solution)/shard_map/pallas_call | solution.py:22
  17.0 0.3 %collective-permute-done.5.refs_11_ = f32[4,8,256]{2,1,0:T(8,128)S(1)} collective-permute-done((f32[4,8,256]{2,1,0:T(8,128)S(1)}, f32[4,8,256]{2,1,0:T(8,128)S(1)}, u32[]{:S(2)}, u32[]{:S(2)}) %collective-permute-start.5) | collective-permute-done | bytes 32800 | tf_op jit(solution)/shard_map/ppermute | solution.py:589
  17.2 1.2 %shard_map.96 = (f32[3,8,256]{2,1,0:T(8,128)}, f32[32,16,256]{2,1,0:T(8,128)}) custom-call(f32[36,16,256]{2,1,0:T(8,128)S(1)} %get-tuple-element.85.smooth.refs_0_, f32[34,8,256]{2,1,0:T(8,128)S(1)} %get-tuple-element.86.refs_3_.refs_1_, f32[35,8,256]{2,1,0:T(8,128)S(1)} %get-tuple-element.87.refs_4_.refs_2_, f32[34,8,256]{2,1,0:T(8,128)S(1)} %get-tuple-element.95.refs_3_, ...), custom_call_target="tpu_custom_call" | custom-call | tf_op jit(solution)/shard_map/pallas_call | solution.py:22
  (2 shorter events, 0.0 us)
Async XLA Ops:
  1.8 6.2 %collective-permute-start.2 = (f32[35,4,256]{2,1,0:T(4,128)S(1)}, f32[35,4,256]{2,1,0:T(4,128)S(1)}, u32[]{:S(2)}, u32[]{:S(2)}) collective-permute-start(f32[35,4,256]{2,1,0:T(4,128)S(1)} %get-tuple-element.58), channel_id=1, source_target_pairs={{0,2},{2,0},{4,6},{6,4},{8,10},{10,8},{12,14},{14,12},{16,18},{18,... | collective-permute-start | bytes 430088 | tf_op jit(solution)/shard_map/ppermute | solution.py:534
  3.1 1.9 %collective-permute-start = (f32[4,16,256]{2,1,0:T(8,128)S(1)}, f32[4,16,256]{2,1,0:T(8,128)S(1)}, u32[]{:S(2)}, u32[]{:S(2)}) collective-permute-start(f32[4,16,256]{2,1,0:T(8,128)S(1)} %get-tuple-element.56), channel_id=1, source_target_pairs={{0,1},{1,0},{2,3},{3,2},{4,5},{5,4},{6,7},{7,6},{8,9},{9,8},{10,11... | collective-permute-start | bytes 196616 | tf_op jit(solution)/shard_map/ppermute | solution.py:533
  5.0 9.0 %collective-permute-start.1 = (f32[39,4,256]{2,1,0:T(4,128)S(1)}, f32[39,4,256]{2,1,0:T(4,128)S(1)}, u32[]{:S(2)}, u32[]{:S(2)}) collective-permute-start(f32[39,4,256]{2,1,0:T(4,128)S(1)} %shard_map.88), channel_id=1, source_target_pairs={{2,4},{4,2},{6,8},{8,6},{10,12},{12,10},{14,16},{16,14},{18,20},{2... | collective-permute-start | bytes 479240 | tf_op jit(solution)/shard_map/ppermute | solution.py:536
  8.0 1.5 %collective-permute-start.3 = (f32[4,4,256]{2,1,0:T(4,128)S(1)}, f32[4,4,256]{2,1,0:T(4,128)S(1)}, u32[]{:S(2)}, u32[]{:S(2)}) collective-permute-start(f32[4,4,256]{2,1,0:T(4,128)S(1)} %slice.4), channel_id=1, source_target_pairs={{0,1},{1,0},{2,3},{3,2},{4,5},{5,4},{6,7},{7,6},{8,9},{9,8},{10,11... | collective-permute-start | bytes 49160 | tf_op jit(solution)/shard_map/ppermute | solution.py:537
  10.4 1.3 %collective-permute-start.4 = (f32[4,16,256]{2,1,0:T(8,128)S(1)}, f32[4,16,256]{2,1,0:T(8,128)S(1)}, u32[]{:S(2)}, u32[]{:S(2)}) collective-permute-start(f32[4,16,256]{2,1,0:T(8,128)S(1)} %get-tuple-element.82.refs_8_), channel_id=1, source_target_pairs={{0,1},{1,0},{2,3},{3,2},{4,5},{5,4},{6,7},{7,6},{8,9},{9,8},{10,11... | collective-permute-start | bytes 196616 | tf_op jit(solution)/shard_map/ppermute | solution.py:568
  15.2 2.1 %collective-permute-start.5 = (f32[4,8,256]{2,1,0:T(8,128)S(1)}, f32[4,8,256]{2,1,0:T(8,128)S(1)}, u32[]{:S(2)}, u32[]{:S(2)}) collective-permute-start(f32[4,8,256]{2,1,0:T(8,128)S(1)} %get-tuple-element.101.refs_9_), channel_id=1, source_target_pairs={{0,1},{1,0},{2,3},{3,2},{4,5},{5,4},{6,7},{7,6},{8,9},{9,8},{10,11... | collective-permute-start | bytes 98312 | tf_op jit(solution)/shard_map/ppermute | solution.py:589

commit v5 on v4

--- a/solution.py
+++ b/solution.py
@@ -9,7 +9,7 @@
 F32 = jnp.float32
 HALO = 4
 PIX = 3
-GROUP_MAIN = (8,16,17,16)
+GROUP_MAIN = (10,16,17,16)
 GROUP_FAR = (30,32,34,32)
 CHUNK = 8
 LATE = True
@@ -42,9 +42,11 @@
     return jnp.where(core == 0, z, nz - 1 - z)
 
 
-def in_groups(body, count, group, carry):
+def in_groups(body, count, group, carry, loop=False):
     full = count // group
-    for i in range(full):
+    if loop:
+        carry = lax.fori_loop(0, full, lambda i, c: body(i * group, group, c), carry)
+    for i in range(0 if not loop else full, full):
         carry = body(i * group, group, carry)
     if count % group:
         carry = body(full * group, count % group, carry)
@@ -210,7 +212,7 @@
     def body(z, n, total):
         return smooth_planes(block, z + 1, n, signed, depth, smooth, taus, sig, total)
 
-    return in_groups(body, depth - 2, group, total)
+    return in_groups(body, depth - 2, group, total, loop=block.band > 8)
 
 
 def smooth_seam(block, depth, smooth, taus, sig, pixo, total):
@@ -292,7 +294,7 @@
     return Block(rows, jnp.where(odd == 1, 2, rows + 8 - 2), own, halo)
 
 
-def far_forward_kernel(dens, pix, zrecv, lrecv, par, smooth, dxs, dys, rnorm, phis, edge, sig, taus, mid, pixo):
+def far_forward_kernel(dens, pix, zrecv, lrecv, par, smooth, dxs, dys, rnorm, phis, edge, sig, mid, pixo, taus):
     nz, rows, _ = dens.shape
     core, odd = where_am_i()
     at = pl.multiple_of(odd * (rows - 8), 8)
@@ -320,17 +322,12 @@
     total[...] = smooth_slab(block, core, dens.shape[0], GROUP_MAIN[0], smooth, taus, sig, pixo)
 
 
-def joined(depth, refs):
-    smooth, taus, sig, smooth_tail, taus_tail, sig_tail = refs
-    return Joined(smooth, smooth_tail, depth), Joined(taus, taus_tail, depth - 1), Joined(sig, sig_tail, depth - 1)
-
-
-def main_shade_kernel(smooth, taus, sig, pixo, total, dens, pix, zrecv, xrecv, xcorner, par, smooth_tail, taus_tail, sig_tail, *rest):
+def main_shade_kernel(smooth, taus, sig, pixo, total, dens, pix, zrecv, xrecv, xcorner, par, smooth_tail, sig_tail, dxs, dys, rnorm, phis, edge, mid, taus_tail):
     nz, rows, _ = dens.shape
     block = main_block(dens, pix, xrecv, zrecv, xcorner)
-    smooth, taus, sig = joined(nz, (smooth, taus, sig, smooth_tail, taus_tail, sig_tail))
+    smooth, taus, sig = Joined(smooth, smooth_tail, nz), Joined(taus, taus_tail, nz - 1), Joined(sig, sig_tail, nz - 1)
     whole = smooth_seam(block, nz, smooth, taus, sig, pixo, total[...])
-    shade_slab(rows, nz, GROUP_MAIN[1], whole, par, smooth, taus, *rest, pixo)
+    shade_slab(rows, nz, GROUP_MAIN[1], whole, par, smooth, taus, dxs, dys, rnorm, phis, edge, mid, pixo)
 
 
 def prepare_block(band, depth, group, smooth, dxs, dys, rnorm, phis, edge, sig, pixo, palette, par, bx, by, bz, gained, damped, targets):
@@ -431,13 +428,13 @@
                 done = []
         return carry
 
-    in_groups(smooth_back, depth, group, 0)
-
-
-def main_prepare_kernel(*refs):
-    slab, (dxs, dys, rnorm, phis, edge, pixo, palette, par, *out) = refs[:6], refs[6:]
-    nz, rows = slab[0].shape[0], dxs.shape[1]
-    smooth, _, sig = joined(nz, slab)
+    in_groups(smooth_back, depth, group, 0, loop=band > 8)
+
+
+def main_prepare_kernel(smooth, sig, smooth_tail, sig_tail, dxs, dys, rnorm, phis, edge, pixo, palette, par, *out):
+    nz, rows, _ = dxs.shape
+    nz = nz - 2
+    smooth, sig = Joined(smooth, smooth_tail, nz), Joined(sig, sig_tail, nz - 1)
     prepare_block(rows, nz, GROUP_MAIN[2], smooth, dxs, dys, rnorm, phis, edge, sig, pixo, palette, par, *out)
 
 
@@ -540,12 +537,8 @@
         planes = nz + 2
         return (
             sds(nz + 4, band + 8, cols),
-            sds(planes, band, cols),
-            sds(planes, band, cols),
-            sds(planes, band, cols),
-            sds(planes, band, cols),
+            *[sds(planes, band, cols)] * 4,
             sds(planes + 1, band, cols),
-            sds(planes, band, cols),
             sds(planes, band, cols),
             sds(4, band, cols),
             sds(PIX, band, cols),
@@ -554,16 +547,17 @@
     parts = residuals(rows)
     smooth, taus, sig, pixo, total = call(
         main_smooth_kernel,
-        (sds(nz, rows + 8, cols), sds(nz - 1, rows, cols), sds(nz - 1, rows, cols), parts[9], sds(rows, cols)),
+        (sds(nz, rows + 8, cols), sds(nz - 1, rows, cols), sds(nz - 1, rows, cols), parts[8], sds(rows, cols)),
         (dens, pix, xrecv),
         [VMEM] * 3,
     )
     xcorner, total = lax.optimization_barrier((xcorner, total))
-    *tails, dxs, dys, rnorm, phis, edge, mid = call(
+    smooth_tail, sig_tail, dxs, dys, rnorm, phis, edge, mid = call(
         main_shade_kernel,
-        (sds(4, rows + 8, cols), sds(3, rows, cols), sds(3, rows, cols), *parts[1:6], parts[8]),
+        (sds(4, rows + 8, cols), sds(3, rows, cols), *parts[1:6], parts[7]),
         (smooth, taus, sig, pixo, total, dens, pix, zrecv, xrecv, xcorner, par),
         [VMEM] * 11,
+        scratch=[pltpu.VMEM((3, rows, cols), F32)],
     )
     theirs = lax.ppermute(mid, "depth", swap)
 
@@ -573,18 +567,22 @@
     ready = call(
         main_prepare_kernel,
         prepared(rows),
-        (smooth, taus, sig, *tails, dxs, dys, rnorm, phis, edge, pixo, pal, par),
-        [VMEM] * 14,
+        (smooth, sig, smooth_tail, sig_tail, dxs, dys, rnorm, phis, edge, pixo, pal, par),
+        [VMEM] * 12,
     )
     near_image, grads = call(
         main_backward_kernel,
         (sds(3, rows, cols), sds(nz + 2, rows, cols)),
-        (smooth, tails[0], phis, edge, *ready, mid, pixo, theirs, par),
+        (smooth, smooth_tail, phis, edge, *ready, mid, pixo, theirs, par),
         [VMEM] * 14,
     )
     lrecv, near_image = lax.optimization_barrier((lrecv, near_image))
-    smooth, dxs, dys, rnorm, phis, edge, sig, taus, mid, pixo = call(
-        far_forward_kernel, residuals(8), (dens, pix, zrecv, lrecv, par), [VMEM] * 5
+    smooth, dxs, dys, rnorm, phis, edge, sig, mid, pixo = call(
+        far_forward_kernel,
+        residuals(8),
+        (dens, pix, zrecv, lrecv, par),
+        [VMEM] * 5,
+        scratch=[pltpu.VMEM((nz + 2, 8, cols), F32)],
     )
     theirs = lax.ppermute(mid, "depth", swap)
     near_image, pixo = lax.optimization_barrier((near_image, pixo))

time: 18.6 us -> 18.3 us (0.984)
  Pallas kernels: 6.9 us -> 6.68 us
    pallas_call x11, Pallas kernels: 6.9 us -> 6.68 us  [call(): pl.pallas_call(kernel, out_shape=outs, in_specs=specs, out_specs=out_spec...]
  transfers between devices with their start and end apart: 6 -> 6, of which waited for: 5 -> 4; matrix products, arithmetic and copies ran while one was open for 0% -> 0% of each run, Pallas kernels for 18% -> 19%
where the time goes in v5:
time: 18.3 us; the launch traced here: 18.2 us
  starting transfers between devices  7.62 us (42%)
  Pallas kernels  6.68 us (37%)
  waiting for transfers between devices  3.14 us (17%)
  between operations  0.72 us (4%)
    pallas_call x11, Pallas kernels, call(): pl.pallas_call(kernel, out_shape=outs, in_specs=specs, out_specs=out_spec...  6.68 us
    ppermute x1, starting transfers between devices, shards(): lrecv = lax.ppermute(lmsg, 'tile', far)  3 us
    ppermute x2, starting transfers between devices, shards(): theirs = lax.ppermute(mid, 'depth', swap)  1.68 us
    ppermute x1, waiting for transfers between devices, shards(): lrecv = lax.ppermute(lmsg, 'tile', far)  1.51 us
    ppermute x1, starting transfers between devices, shards(): xrecv = lax.ppermute(xmsg, 'tile', near)  1.28 us
    ppermute x1, starting transfers between devices, shards(): zrecv = lax.ppermute(zmsg, 'depth', swap)  0.96 us
    ppermute x1, waiting for transfers between devices, shards(): zrecv = lax.ppermute(zmsg, 'depth', swap)  0.9 us
    ppermute x2, waiting for transfers between devices, shards(): theirs = lax.ppermute(mid, 'depth', swap)  0.7 us
  transfers between devices with their start and end apart: 6, of which 4 were waited for; matrix products, arithmetic and copies ran while one was open for 0% of the time, Pallas kernels for 19%

profile of v5, /device:TPU:9, one launch (start us, length us, event | category | flops | bytes accessed | tf_op | source)
XLA Modules:
  0.0 18.2 jit_solution(2966434549208945354)
XLA Ops:
  0.6 1.1 %shard_map.86 = (f32[4,16,256]{2,1,0:T(8,128)S(1)}, f32[32,16,256]{2,1,0:T(8,128)S(1)}, f32[3,16,256]{2,1,0:T(8,128)S(1)}, f32[3,128]{1,0:T(4,128)S(1)}, f32[15,8,128]{2,1,0:T(8,128)S(1)}) custom-call(f32[32,16,256]{2,1,0:T(8,128)} %dens_h.1, f32[16,256]{1,0:T(8,128)} %absorb_h.1, s32[16,256]{1,0:T(8,128)} %ids_h.1, s32[16]{0:T(128)} %view_h.1, ...), custom_call_target="tpu_custom_call" | custom-call | tf_op jit(solution)/shard_map/pallas_call | solution.py:22
  1.8 0.1 shard_map.87
  1.8 1.3 %collective-permute-start.2 = (f32[35,4,256]{2,1,0:T(4,128)S(1)}, f32[35,4,256]{2,1,0:T(4,128)S(1)}, u32[]{:S(2)}, u32[]{:S(2)}) collective-permute-start(f32[35,4,256]{2,1,0:T(4,128)S(1)} %get-tuple-element.57), channel_id=1, source_target_pairs={{0,2},{2,0},{4,6},{6,4},{8,10},{10,8},{12,14},{14,12},{16,18},{18,... | collective-permute-start | bytes 430088 | tf_op jit(solution)/shard_map/ppermute | solution.py:531
  3.1 1.0 %collective-permute-start = (f32[4,16,256]{2,1,0:T(8,128)S(1)}, f32[4,16,256]{2,1,0:T(8,128)S(1)}, u32[]{:S(2)}, u32[]{:S(2)}) collective-permute-start(f32[4,16,256]{2,1,0:T(8,128)S(1)} %get-tuple-element.55), channel_id=1, source_target_pairs={{0,1},{1,0},{2,3},{3,2},{4,5},{5,4},{6,7},{7,6},{8,9},{9,8},{10,11... | collective-permute-start | bytes 196616 | tf_op jit(solution)/shard_map/ppermute | solution.py:530
  4.1 0.9 %collective-permute-done.zrecv = f32[4,16,256]{2,1,0:T(8,128)S(1)} collective-permute-done((f32[4,16,256]{2,1,0:T(8,128)S(1)}, f32[4,16,256]{2,1,0:T(8,128)S(1)}, u32[]{:S(2)}, u32[]{:S(2)}) %collective-permute-start) | collective-permute-done | bytes 65568 | tf_op jit(solution)/shard_map/ppermute | solution.py:530
  5.0 3.0 %collective-permute-start.1 = (f32[39,4,256]{2,1,0:T(4,128)S(1)}, f32[39,4,256]{2,1,0:T(4,128)S(1)}, u32[]{:S(2)}, u32[]{:S(2)}) collective-permute-start(f32[39,4,256]{2,1,0:T(4,128)S(1)} %shard_map.88), channel_id=1, source_target_pairs={{2,4},{4,2},{6,8},{8,6},{10,12},{12,10},{14,16},{16,14},{18,20},{2... | collective-permute-start | bytes 479240 | tf_op jit(solution)/shard_map/ppermute | solution.py:533
  8.0 0.0 collective-permute-done.2.xrecv
  8.0 0.7 %collective-permute-start.3 = (f32[4,4,256]{2,1,0:T(4,128)S(1)}, f32[4,4,256]{2,1,0:T(4,128)S(1)}, u32[]{:S(2)}, u32[]{:S(2)}) collective-permute-start(f32[4,4,256]{2,1,0:T(4,128)S(1)} %slice.4), channel_id=1, source_target_pairs={{0,1},{1,0},{2,3},{3,2},{4,5},{5,4},{6,7},{7,6},{8,9},{9,8},{10,11... | collective-permute-start | bytes 49160 | tf_op jit(solution)/shard_map/ppermute | solution.py:534
  8.7 0.8 %shard_map.89 = (f32[32,24,256]{2,1,0:T(8,128)S(1)}, f32[31,16,256]{2,1,0:T(8,128)S(1)}, f32[31,16,256]{2,1,0:T(8,128)S(1)}, f32[3,16,256]{2,1,0:T(8,128)S(1)}, f32[16,256]{1,0:T(8,128)S(1)}) custom-call(f32[32,16,256]{2,1,0:T(8,128)S(1)} %get-tuple-element.53.dens, f32[3,16,256]{2,1,0:T(8,128)S(1)} %get-tuple-element.54.pix, ...), custom_call_target="tpu_custom_call" | custom-call | tf_op jit(solution)/shard_map/pallas_call | solution.py:22
  9.5 0.0 collective-permute-done.3.xcorner
  9.6 0.8 %shard_map.90 = (f32[4,24,256]{2,1,0:T(8,128)S(1)}, f32[3,16,256]{2,1,0:T(8,128)S(1)}, f32[34,16,256]{2,1,0:T(8,128)S(1)}, f32[34,16,256]{2,1,0:T(8,128)S(1)}, f...) custom-call(f32[32,24,256]{2,1,0:T(8,128)S(1)} %get-tuple-element.58, ...), custom_call_target="tpu_custom_call" | custom-call | tf_op jit(solution)/shard_map/pallas_call | solution.py:22
  10.4 0.4 %collective-permute-start.4 = (f32[4,16,256]{2,1,0:T(8,128)S(1)}, f32[4,16,256]{2,1,0:T(8,128)S(1)}, u32[]{:S(2)}, u32[]{:S(2)}) collective-permute-start(f32[4,16,256]{2,1,0:T(8,128)S(1)} %get-tuple-element.80.refs_8_), channel_id=1, source_target_pairs={{0,1},{1,0},{2,3},{3,2},{4,5},{5,4},{6,7},{7,6},{8,9},{9,8},{10,11... | collective-permute-start | bytes 196616 | tf_op jit(solution)/shard_map/ppermute | solution.py:562
  10.8 0.4 %shard_map.91 = (f32[34,16,256]{2,1,0:T(8,128)S(1)}, f32[34,16,256]{2,1,0:T(8,128)S(1)}, f32[34,16,256]{2,1,0:T(8,128)S(1)}, f32[34,16,256]{2,1,0:T(8,128)S(1)},...) custom-call(f32[32,24,256]{2,1,0:T(8,128)S(1)} %get-tuple-element.58.smooth, ...), custom_call_target="tpu_custom_call" | custom-call | tf_op jit(solution)/shard_map/pallas_call | solution.py:22
  11.2 0.5 %collective-permute-done.4.refs_10_ = f32[4,16,256]{2,1,0:T(8,128)S(1)} collective-permute-done((f32[4,16,256]{2,1,0:T(8,128)S(1)}, f32[4,16,256]{2,1,0:T(8,128)S(1)}, u32[]{:S(2)}, u32[]{:S(2)}) %collective-permute-start.4) | collective-permute-done | bytes 65568 | tf_op jit(solution)/shard_map/ppermute | solution.py:562
  11.7 0.8 %shard_map.92 = (f32[3,16,256]{2,1,0:T(8,128)S(1)}, f32[34,16,256]{2,1,0:T(8,128)S(1)}) custom-call(f32[32,24,256]{2,1,0:T(8,128)S(1)} %get-tuple-element.58.smooth, f32[4,24,256]{2,1,0:T(8,128)S(1)} %get-tuple-element.66.smooth_tail, f32[34,16,256]{2,1,0:T(8,128)S(1)} %get-tuple-element.67.phis.refs_0_, f32[35,16,256]{2,1,0:T(8,128)S(1)} %get-tuple-element.68.edge.refs_1_, ...), custom_call_target="tpu_custom_call" | custom-call | tf_op jit(solution)/shard_map/pallas_call | solution.py:22
  12.5 1.5 %collective-permute-done.1.lrecv = f32[39,4,256]{2,1,0:T(4,128)S(1)} collective-permute-done((f32[39,4,256]{2,1,0:T(4,128)S(1)}, f32[39,4,256]{2,1,0:T(4,128)S(1)}, u32[]{:S(2)}, u32[]{:S(2)}) %collective-permute-start.1) | collective-permute-done | bytes 159776 | tf_op jit(solution)/shard_map/ppermute | solution.py:533
  14.0 0.8 %shard_map.93 = (f32[36,16,256]{2,1,0:T(8,128)S(1)}, f32[34,8,256]{2,1,0:T(8,128)S(1)}, f32[34,8,256]{2,1,0:T(8,128)S(1)}, f32[34,8,256]{2,1,0:T(8,128)S(1)}, f3...) custom-call(f32[32,16,256]{2,1,0:T(8,128)S(1)} %get-tuple-element.53, ...), custom_call_target="tpu_custom_call" | custom-call | tf_op jit(solution)/shard_map/pallas_call | solution.py:22
  14.8 1.3 %collective-permute-start.5 = (f32[4,8,256]{2,1,0:T(8,128)S(1)}, f32[4,8,256]{2,1,0:T(8,128)S(1)}, u32[]{:S(2)}, u32[]{:S(2)}) collective-permute-start(f32[4,8,256]{2,1,0:T(8,128)S(1)} %get-tuple-element.99.refs_9_), channel_id=1, source_target_pairs={{0,1},{1,0},{2,3},{3,2},{4,5},{5,4},{6,7},{7,6},{8,9},{9,8},{10,11... | collective-permute-start | bytes 98312 | tf_op jit(solution)/shard_map/ppermute | solution.py:587
  16.1 0.4 %shard_map.95 = (f32[32,16,256]{2,1,0:T(8,128)S(1)}, f32[3,16,256]{2,1,0:T(8,128)S(1)}) custom-call(f32[34,16,256]{2,1,0:T(8,128)S(1)} %get-tuple-element.100.grads, f32[3,16,256]{2,1,0:T(8,128)S(1)} %get-tuple-element.101.image), custom_call_target="tpu_custom_call" | custom-call | tf_op jit(solution)/shard_map/pallas_call | solution.py:22
  16.5 0.2 %shard_map.94 = (f32[34,8,256]{2,1,0:T(8,128)S(1)}, f32[34,8,256]{2,1,0:T(8,128)S(1)}, f32[34,8,256]{2,1,0:T(8,128)S(1)}, f32[34,8,256]{2,1,0:T(8,128)S(1)}, f32...) custom-call(f32[36,16,256]{2,1,0:T(8,128)S(1)} %get-tuple-element.83.smooth.refs_0_, ...), custom_call_target="tpu_custom_call" | custom-call | tf_op jit(solution)/shard_map/pallas_call | solution.py:22
  16.7 0.2 %collective-permute-done.5.refs_11_ = f32[4,8,256]{2,1,0:T(8,128)S(1)} collective-permute-done((f32[4,8,256]{2,1,0:T(8,128)S(1)}, f32[4,8,256]{2,1,0:T(8,128)S(1)}, u32[]{:S(2)}, u32[]{:S(2)}) %collective-permute-start.5) | collective-permute-done | bytes 32800 | tf_op jit(solution)/shard_map/ppermute | solution.py:587
  16.9 1.2 %shard_map.96 = (f32[3,8,256]{2,1,0:T(8,128)}, f32[32,16,256]{2,1,0:T(8,128)}) custom-call(f32[36,16,256]{2,1,0:T(8,128)S(1)} %get-tuple-element.83.smooth.refs_0_, f32[34,8,256]{2,1,0:T(8,128)S(1)} %get-tuple-element.84.refs_3_.refs_1_, f32[35,8,256]{2,1,0:T(8,128)S(1)} %get-tuple-element.85.refs_4_.refs_2_, f32[34,8,256]{2,1,0:T(8,128)S(1)} %get-tuple-element.93.refs_3_, ...), custom_call_target="tpu_custom_call" | custom-call | tf_op jit(solution)/shard_map/pallas_call | solution.py:22
  (2 shorter events, 0.0 us)
Async XLA Ops:
  1.8 6.2 %collective-permute-start.2 = (f32[35,4,256]{2,1,0:T(4,128)S(1)}, f32[35,4,256]{2,1,0:T(4,128)S(1)}, u32[]{:S(2)}, u32[]{:S(2)}) collective-permute-start(f32[35,4,256]{2,1,0:T(4,128)S(1)} %get-tuple-element.57), channel_id=1, source_target_pairs={{0,2},{2,0},{4,6},{6,4},{8,10},{10,8},{12,14},{14,12},{16,18},{18,... | collective-permute-start | bytes 430088 | tf_op jit(solution)/shard_map/ppermute | solution.py:531
  3.1 1.9 %collective-permute-start = (f32[4,16,256]{2,1,0:T(8,128)S(1)}, f32[4,16,256]{2,1,0:T(8,128)S(1)}, u32[]{:S(2)}, u32[]{:S(2)}) collective-permute-start(f32[4,16,256]{2,1,0:T(8,128)S(1)} %get-tuple-element.55), channel_id=1, source_target_pairs={{0,1},{1,0},{2,3},{3,2},{4,5},{5,4},{6,7},{7,6},{8,9},{9,8},{10,11... | collective-permute-start | bytes 196616 | tf_op jit(solution)/shard_map/ppermute | solution.py:530
  5.0 9.0 %collective-permute-start.1 = (f32[39,4,256]{2,1,0:T(4,128)S(1)}, f32[39,4,256]{2,1,0:T(4,128)S(1)}, u32[]{:S(2)}, u32[]{:S(2)}) collective-permute-start(f32[39,4,256]{2,1,0:T(4,128)S(1)} %shard_map.88), channel_id=1, source_target_pairs={{2,4},{4,2},{6,8},{8,6},{10,12},{12,10},{14,16},{16,14},{18,20},{2... | collective-permute-start | bytes 479240 | tf_op jit(solution)/shard_map/ppermute | solution.py:533
  8.0 1.5 %collective-permute-start.3 = (f32[4,4,256]{2,1,0:T(4,128)S(1)}, f32[4,4,256]{2,1,0:T(4,128)S(1)}, u32[]{:S(2)}, u32[]{:S(2)}) collective-permute-start(f32[4,4,256]{2,1,0:T(4,128)S(1)} %slice.4), channel_id=1, source_target_pairs={{0,1},{1,0},{2,3},{3,2},{4,5},{5,4},{6,7},{7,6},{8,9},{9,8},{10,11... | collective-permute-start | bytes 49160 | tf_op jit(solution)/shard_map/ppermute | solution.py:534
  10.4 1.3 %collective-permute-start.4 = (f32[4,16,256]{2,1,0:T(8,128)S(1)}, f32[4,16,256]{2,1,0:T(8,128)S(1)}, u32[]{:S(2)}, u32[]{:S(2)}) collective-permute-start(f32[4,16,256]{2,1,0:T(8,128)S(1)} %get-tuple-element.80.refs_8_), channel_id=1, source_target_pairs={{0,1},{1,0},{2,3},{3,2},{4,5},{5,4},{6,7},{7,6},{8,9},{9,8},{10,11... | collective-permute-start | bytes 196616 | tf_op jit(solution)/shard_map/ppermute | solution.py:562
  14.8 2.1 %collective-permute-start.5 = (f32[4,8,256]{2,1,0:T(8,128)S(1)}, f32[4,8,256]{2,1,0:T(8,128)S(1)}, u32[]{:S(2)}, u32[]{:S(2)}) collective-permute-start(f32[4,8,256]{2,1,0:T(8,128)S(1)} %get-tuple-element.99.refs_9_), channel_id=1, source_target_pairs={{0,1},{1,0},{2,3},{3,2},{4,5},{5,4},{6,7},{7,6},{8,9},{9,8},{10,11... | collective-permute-start | bytes 98312 | tf_op jit(solution)/shard_map/ppermute | solution.py:587

commit v6 on v5

--- a/solution.py
+++ b/solution.py
@@ -123,24 +123,27 @@
     nz, rows, _ = dens.shape
     core, odd = where_am_i()
 
-    def edges(plane, to):
-        head, tail = plane[:HALO], plane[rows - HALO :]
+    def edges(head, tail, to):
         xmsg[to] = jnp.where(odd == 1, head, tail)
         lmsg[to] = jnp.where(odd == 1, tail, head)
 
-    for j in range(PIX):
-        edges(pix[j], nz + j)
+    a, ids, view = pix[0], pix[1], pix[2]
+    edges(jnp.concatenate([a[:2], ids[:2]], axis=0), jnp.concatenate([ids[rows - 2 :], a[rows - 2 :]], axis=0), nz)
+    edges(view[:HALO], view[rows - HALO :], nz + 1)
     for j in range(nz):
-        edges(dens[local_plane(core, nz, nz - 1 - j)], j)
+        plane = dens[local_plane(core, nz, nz - 1 - j)]
+        edges(plane[:HALO], plane[rows - HALO :], j)
 
 
 def corner_kernel(zrecv, early, lmsg):
     rows = zrecv.shape[1]
     _, odd = where_am_i()
-    lmsg[HALO:] = early[...]
-    for j in range(HALO):
-        plane = zrecv[HALO - 1 - j]
-        lmsg[j] = jnp.where(odd == 1, plane[rows - HALO :], plane[:HALO])
+    lmsg[2:] = early[...]
+    one, two, three = zrecv[0], zrecv[1], zrecv[2]
+    lmsg[1] = jnp.where(odd == 1, one[rows - HALO :], one[:HALO])
+    tail = jnp.concatenate([three[rows - 1 :], two[rows - HALO + 1 :]], axis=0)
+    head = jnp.concatenate([two[: HALO - 1], three[:1]], axis=0)
+    lmsg[0] = jnp.where(odd == 1, tail, head)
 
 
 def lookup(palette, ids):
@@ -158,6 +161,14 @@
             strips.append(jnp.concatenate(strip, axis=1))
         parts.append(jnp.concatenate(strips, axis=0))
     return parts
+
+
+def pixel_rows(planes, z):
+    if z == -1:
+        return planes[0]
+    if z == -2:
+        return jnp.concatenate([planes[0][2:], planes[0][:2]], axis=0)
+    return planes[1]
 
 
 class Block:
@@ -286,7 +297,7 @@
     def halo(z):
         if isinstance(z, int):
             if z < 0:
-                return xrecv[nz - 1 - z]
+                return pixel_rows((xrecv[nz], xrecv[nz + 1]), z)
             if z >= nz:
                 return xcorner[z - nz]
         return xrecv[nz - 1 - z]
@@ -308,7 +319,18 @@
         return dens[local_plane(core, nz, z), pl.ds(at, 8)]
 
     def halo(z):
-        return lrecv[nz + HALO - 1 - z]
+        if isinstance(z, int):
+            if z < 0:
+                return pixel_rows((lrecv[nz + 2], lrecv[nz + 3]), z)
+            if z == nz:
+                return lrecv[1]
+            if z > nz:
+                plane = lrecv[0]
+                if z != nz + 2:
+                    return plane
+                up = jnp.concatenate([plane[1:], plane[:1]], axis=0)
+                return jnp.where(odd == 1, jnp.concatenate([plane[HALO - 1 :], plane[: HALO - 1]], axis=0), up)
+        return lrecv[nz + 1 - z]
 
     block = Block(8, jnp.where(odd == 1, 16 - 2, 2), own, halo)
     total = smooth_slab(block, core, nz, GROUP_FAR[0], smooth, taus, sig, pixo)
@@ -523,13 +545,13 @@
             pltpu.SemaphoreType.DMA((7,)),
         ],
     )
-    xmsg, lmsg = call(edges_kernel, (sds(nz + PIX, HALO, cols), sds(nz + PIX, HALO, cols)), (dens, pix), [VMEM] * 2)
+    xmsg, lmsg = call(edges_kernel, (sds(nz + 2, HALO, cols), sds(nz + 2, HALO, cols)), (dens, pix), [VMEM] * 2)
     swap = [(0, 1), (1, 0)]
     near = [(i, i ^ 1) for i in range(tiles)]
     far = [(i, i + 1 if i % 2 else i - 1) for i in range(1, tiles - 1)]
     zrecv = lax.ppermute(zmsg, "depth", swap)
     xrecv = lax.ppermute(xmsg, "tile", near)
-    lmsg = call(corner_kernel, sds(HALO + nz + PIX, HALO, cols), (zrecv, lmsg), [VMEM, VMEM])
+    lmsg = call(corner_kernel, sds(nz + 4, HALO, cols), (zrecv, lmsg), [VMEM, VMEM])
     lrecv = lax.ppermute(lmsg, "tile", far)
     xcorner = lax.ppermute(xrecv[:HALO], "depth", swap)
 

time: 18.3 us -> 18.1 us (0.989)
  waiting for transfers between devices: 3.14 us -> 2.87 us
    ppermute x1, waiting for transfers between devices: 1.51 us -> 1.25 us  [shards(): lrecv = lax.ppermute(lmsg, 'tile', far)]
where the time goes in v6:
time: 18.1 us; the launch traced here: 17.9 us
  starting transfers between devices  7.62 us (42%)
  Pallas kernels  6.68 us (37%)
  waiting for transfers between devices  2.87 us (16%)
  between operations  0.72 us (4%)
    pallas_call x11, Pallas kernels, call(): pl.pallas_call(kernel, out_shape=outs, in_specs=specs, out_specs=out_spec...  6.68 us
    ppermute x1, starting transfers between devices, shards(): lrecv = lax.ppermute(lmsg, 'tile', far)  3 us
    ppermute x2, starting transfers between devices, shards(): theirs = lax.ppermute(mid, 'depth', swap)  1.69 us
    ppermute x1, starting transfers between devices, shards(): xrecv = lax.ppermute(xmsg, 'tile', near)  1.28 us
    ppermute x1, waiting for transfers between devices, shards(): lrecv = lax.ppermute(lmsg, 'tile', far)  1.25 us
    ppermute x1, starting transfers between devices, shards(): zrecv = lax.ppermute(zmsg, 'depth', swap)  0.96 us
    ppermute x1, waiting for transfers between devices, shards(): zrecv = lax.ppermute(zmsg, 'depth', swap)  0.9 us
    ppermute x1, starting transfers between devices, shards(): xcorner = lax.ppermute(xrecv[:HALO], 'depth', swap)  0.7 us
  transfers between devices with their start and end apart: 6, of which 4 were waited for; matrix products, arithmetic and copies ran while one was open for 0% of the time, Pallas kernels for 19%

profile of v6, /device:TPU:9, one launch (start us, length us, event | category | flops | bytes accessed | tf_op | source)
XLA Modules:
  0.0 17.9 jit_solution(73298004765437501)
XLA Ops:
  0.6 1.1 %shard_map.86 = (f32[4,16,256]{2,1,0:T(8,128)S(1)}, f32[32,16,256]{2,1,0:T(8,128)S(1)}, f32[3,16,256]{2,1,0:T(8,128)S(1)}, f32[3,128]{1,0:T(4,128)S(1)}, f32[15,8,128]{2,1,0:T(8,128)S(1)}) custom-call(f32[32,16,256]{2,1,0:T(8,128)} %dens_h.1, f32[16,256]{1,0:T(8,128)} %absorb_h.1, s32[16,256]{1,0:T(8,128)} %ids_h.1, s32[16]{0:T(128)} %view_h.1, ...), custom_call_target="tpu_custom_call" | custom-call | tf_op jit(solution)/shard_map/pallas_call | solution.py:22
  1.8 0.1 shard_map.87
  1.8 1.3 %collective-permute-start.2 = (f32[34,4,256]{2,1,0:T(4,128)S(1)}, f32[34,4,256]{2,1,0:T(4,128)S(1)}, u32[]{:S(2)}, u32[]{:S(2)}) collective-permute-start(f32[34,4,256]{2,1,0:T(4,128)S(1)} %get-tuple-element.57), channel_id=1, source_target_pairs={{0,2},{2,0},{4,6},{6,4},{8,10},{10,8},{12,14},{14,12},{16,18},{18,... | collective-permute-start | bytes 417800 | tf_op jit(solution)/shard_map/ppermute | solution.py:553
  3.1 1.0 %collective-permute-start = (f32[4,16,256]{2,1,0:T(8,128)S(1)}, f32[4,16,256]{2,1,0:T(8,128)S(1)}, u32[]{:S(2)}, u32[]{:S(2)}) collective-permute-start(f32[4,16,256]{2,1,0:T(8,128)S(1)} %get-tuple-element.55), channel_id=1, source_target_pairs={{0,1},{1,0},{2,3},{3,2},{4,5},{5,4},{6,7},{7,6},{8,9},{9,8},{10,11... | collective-permute-start | bytes 196616 | tf_op jit(solution)/shard_map/ppermute | solution.py:552
  4.1 0.9 %collective-permute-done.zrecv = f32[4,16,256]{2,1,0:T(8,128)S(1)} collective-permute-done((f32[4,16,256]{2,1,0:T(8,128)S(1)}, f32[4,16,256]{2,1,0:T(8,128)S(1)}, u32[]{:S(2)}, u32[]{:S(2)}) %collective-permute-start) | collective-permute-done | bytes 65568 | tf_op jit(solution)/shard_map/ppermute | solution.py:552
  5.0 3.0 %collective-permute-start.1 = (f32[36,4,256]{2,1,0:T(4,128)S(1)}, f32[36,4,256]{2,1,0:T(4,128)S(1)}, u32[]{:S(2)}, u32[]{:S(2)}) collective-permute-start(f32[36,4,256]{2,1,0:T(4,128)S(1)} %shard_map.88), channel_id=1, source_target_pairs={{2,4},{4,2},{6,8},{8,6},{10,12},{12,10},{14,16},{16,14},{18,20},{2... | collective-permute-start | bytes 442376 | tf_op jit(solution)/shard_map/ppermute | solution.py:555
  8.0 0.0 collective-permute-done.2.xrecv
  8.0 0.7 %collective-permute-start.3 = (f32[4,4,256]{2,1,0:T(4,128)S(1)}, f32[4,4,256]{2,1,0:T(4,128)S(1)}, u32[]{:S(2)}, u32[]{:S(2)}) collective-permute-start(f32[4,4,256]{2,1,0:T(4,128)S(1)} %slice.4), channel_id=1, source_target_pairs={{0,1},{1,0},{2,3},{3,2},{4,5},{5,4},{6,7},{7,6},{8,9},{9,8},{10,11... | collective-permute-start | bytes 49160 | tf_op jit(solution)/shard_map/ppermute | solution.py:556
  8.7 0.8 %shard_map.89 = (f32[32,24,256]{2,1,0:T(8,128)S(1)}, f32[31,16,256]{2,1,0:T(8,128)S(1)}, f32[31,16,256]{2,1,0:T(8,128)S(1)}, f32[3,16,256]{2,1,0:T(8,128)S(1)}, f32[16,256]{1,0:T(8,128)S(1)}) custom-call(f32[32,16,256]{2,1,0:T(8,128)S(1)} %get-tuple-element.53.dens, f32[3,16,256]{2,1,0:T(8,128)S(1)} %get-tuple-element.54.pix, ...), custom_call_target="tpu_custom_call" | custom-call | tf_op jit(solution)/shard_map/pallas_call | solution.py:22
  9.5 0.0 collective-permute-done.3.xcorner
  9.6 0.8 %shard_map.90 = (f32[4,24,256]{2,1,0:T(8,128)S(1)}, f32[3,16,256]{2,1,0:T(8,128)S(1)}, f32[34,16,256]{2,1,0:T(8,128)S(1)}, f32[34,16,256]{2,1,0:T(8,128)S(1)}, f...) custom-call(f32[32,24,256]{2,1,0:T(8,128)S(1)} %get-tuple-element.58, ...), custom_call_target="tpu_custom_call" | custom-call | tf_op jit(solution)/shard_map/pallas_call | solution.py:22
  10.4 0.4 %collective-permute-start.4 = (f32[4,16,256]{2,1,0:T(8,128)S(1)}, f32[4,16,256]{2,1,0:T(8,128)S(1)}, u32[]{:S(2)}, u32[]{:S(2)}) collective-permute-start(f32[4,16,256]{2,1,0:T(8,128)S(1)} %get-tuple-element.80.refs_8_), channel_id=1, source_target_pairs={{0,1},{1,0},{2,3},{3,2},{4,5},{5,4},{6,7},{7,6},{8,9},{9,8},{10,11... | collective-permute-start | bytes 196616 | tf_op jit(solution)/shard_map/ppermute | solution.py:584
  10.8 0.4 %shard_map.91 = (f32[34,16,256]{2,1,0:T(8,128)S(1)}, f32[34,16,256]{2,1,0:T(8,128)S(1)}, f32[34,16,256]{2,1,0:T(8,128)S(1)}, f32[34,16,256]{2,1,0:T(8,128)S(1)},...) custom-call(f32[32,24,256]{2,1,0:T(8,128)S(1)} %get-tuple-element.58.smooth, ...), custom_call_target="tpu_custom_call" | custom-call | tf_op jit(solution)/shard_map/pallas_call | solution.py:22
  11.2 0.5 %collective-permute-done.4.refs_10_ = f32[4,16,256]{2,1,0:T(8,128)S(1)} collective-permute-done((f32[4,16,256]{2,1,0:T(8,128)S(1)}, f32[4,16,256]{2,1,0:T(8,128)S(1)}, u32[]{:S(2)}, u32[]{:S(2)}) %collective-permute-start.4) | collective-permute-done | bytes 65568 | tf_op jit(solution)/shard_map/ppermute | solution.py:584
  11.7 0.8 %shard_map.92 = (f32[3,16,256]{2,1,0:T(8,128)S(1)}, f32[34,16,256]{2,1,0:T(8,128)S(1)}) custom-call(f32[32,24,256]{2,1,0:T(8,128)S(1)} %get-tuple-element.58.smooth, f32[4,24,256]{2,1,0:T(8,128)S(1)} %get-tuple-element.66.smooth_tail, f32[34,16,256]{2,1,0:T(8,128)S(1)} %get-tuple-element.67.phis.refs_0_, f32[35,16,256]{2,1,0:T(8,128)S(1)} %get-tuple-element.68.edge.refs_1_, ...), custom_call_target="tpu_custom_call" | custom-call | tf_op jit(solution)/shard_map/pallas_call | solution.py:22
  12.5 1.3 %collective-permute-done.1.lrecv = f32[36,4,256]{2,1,0:T(4,128)S(1)} collective-permute-done((f32[36,4,256]{2,1,0:T(4,128)S(1)}, f32[36,4,256]{2,1,0:T(4,128)S(1)}, u32[]{:S(2)}, u32[]{:S(2)}) %collective-permute-start.1) | collective-permute-done | bytes 147488 | tf_op jit(solution)/shard_map/ppermute | solution.py:555
  13.7 0.8 %shard_map.93 = (f32[36,16,256]{2,1,0:T(8,128)S(1)}, f32[34,8,256]{2,1,0:T(8,128)S(1)}, f32[34,8,256]{2,1,0:T(8,128)S(1)}, f32[34,8,256]{2,1,0:T(8,128)S(1)}, f3...) custom-call(f32[32,16,256]{2,1,0:T(8,128)S(1)} %get-tuple-element.53, ...), custom_call_target="tpu_custom_call" | custom-call | tf_op jit(solution)/shard_map/pallas_call | solution.py:22
  14.5 1.3 %collective-permute-start.5 = (f32[4,8,256]{2,1,0:T(8,128)S(1)}, f32[4,8,256]{2,1,0:T(8,128)S(1)}, u32[]{:S(2)}, u32[]{:S(2)}) collective-permute-start(f32[4,8,256]{2,1,0:T(8,128)S(1)} %get-tuple-element.99.refs_9_), channel_id=1, source_target_pairs={{0,1},{1,0},{2,3},{3,2},{4,5},{5,4},{6,7},{7,6},{8,9},{9,8},{10,11... | collective-permute-start | bytes 98312 | tf_op jit(solution)/shard_map/ppermute | solution.py:609
  15.8 0.4 %shard_map.95 = (f32[32,16,256]{2,1,0:T(8,128)S(1)}, f32[3,16,256]{2,1,0:T(8,128)S(1)}) custom-call(f32[34,16,256]{2,1,0:T(8,128)S(1)} %get-tuple-element.100.grads, f32[3,16,256]{2,1,0:T(8,128)S(1)} %get-tuple-element.101.image), custom_call_target="tpu_custom_call" | custom-call | tf_op jit(solution)/shard_map/pallas_call | solution.py:22
  16.2 0.2 %shard_map.94 = (f32[34,8,256]{2,1,0:T(8,128)S(1)}, f32[34,8,256]{2,1,0:T(8,128)S(1)}, f32[34,8,256]{2,1,0:T(8,128)S(1)}, f32[34,8,256]{2,1,0:T(8,128)S(1)}, f32...) custom-call(f32[36,16,256]{2,1,0:T(8,128)S(1)} %get-tuple-element.83.smooth.refs_0_, ...), custom_call_target="tpu_custom_call" | custom-call | tf_op jit(solution)/shard_map/pallas_call | solution.py:22
  16.5 0.2 %collective-permute-done.5.refs_11_ = f32[4,8,256]{2,1,0:T(8,128)S(1)} collective-permute-done((f32[4,8,256]{2,1,0:T(8,128)S(1)}, f32[4,8,256]{2,1,0:T(8,128)S(1)}, u32[]{:S(2)}, u32[]{:S(2)}) %collective-permute-start.5) | collective-permute-done | bytes 32800 | tf_op jit(solution)/shard_map/ppermute | solution.py:609
  16.7 1.2 %shard_map.96 = (f32[3,8,256]{2,1,0:T(8,128)}, f32[32,16,256]{2,1,0:T(8,128)}) custom-call(f32[36,16,256]{2,1,0:T(8,128)S(1)} %get-tuple-element.83.smooth.refs_0_, f32[34,8,256]{2,1,0:T(8,128)S(1)} %get-tuple-element.84.refs_3_.refs_1_, f32[35,8,256]{2,1,0:T(8,128)S(1)} %get-tuple-element.85.refs_4_.refs_2_, f32[34,8,256]{2,1,0:T(8,128)S(1)} %get-tuple-element.93.refs_3_, ...), custom_call_target="tpu_custom_call" | custom-call | tf_op jit(solution)/shard_map/pallas_call | solution.py:22
  (2 shorter events, 0.0 us)
Async XLA Ops:
  1.8 6.2 %collective-permute-start.2 = (f32[34,4,256]{2,1,0:T(4,128)S(1)}, f32[34,4,256]{2,1,0:T(4,128)S(1)}, u32[]{:S(2)}, u32[]{:S(2)}) collective-permute-start(f32[34,4,256]{2,1,0:T(4,128)S(1)} %get-tuple-element.57), channel_id=1, source_target_pairs={{0,2},{2,0},{4,6},{6,4},{8,10},{10,8},{12,14},{14,12},{16,18},{18,... | collective-permute-start | bytes 417800 | tf_op jit(solution)/shard_map/ppermute | solution.py:553
  3.1 1.9 %collective-permute-start = (f32[4,16,256]{2,1,0:T(8,128)S(1)}, f32[4,16,256]{2,1,0:T(8,128)S(1)}, u32[]{:S(2)}, u32[]{:S(2)}) collective-permute-start(f32[4,16,256]{2,1,0:T(8,128)S(1)} %get-tuple-element.55), channel_id=1, source_target_pairs={{0,1},{1,0},{2,3},{3,2},{4,5},{5,4},{6,7},{7,6},{8,9},{9,8},{10,11... | collective-permute-start | bytes 196616 | tf_op jit(solution)/shard_map/ppermute | solution.py:552
  5.0 8.7 %collective-permute-start.1 = (f32[36,4,256]{2,1,0:T(4,128)S(1)}, f32[36,4,256]{2,1,0:T(4,128)S(1)}, u32[]{:S(2)}, u32[]{:S(2)}) collective-permute-start(f32[36,4,256]{2,1,0:T(4,128)S(1)} %shard_map.88), channel_id=1, source_target_pairs={{2,4},{4,2},{6,8},{8,6},{10,12},{12,10},{14,16},{16,14},{18,20},{2... | collective-permute-start | bytes 442376 | tf_op jit(solution)/shard_map/ppermute | solution.py:555
  8.0 1.5 %collective-permute-start.3 = (f32[4,4,256]{2,1,0:T(4,128)S(1)}, f32[4,4,256]{2,1,0:T(4,128)S(1)}, u32[]{:S(2)}, u32[]{:S(2)}) collective-permute-start(f32[4,4,256]{2,1,0:T(4,128)S(1)} %slice.4), channel_id=1, source_target_pairs={{0,1},{1,0},{2,3},{3,2},{4,5},{5,4},{6,7},{7,6},{8,9},{9,8},{10,11... | collective-permute-start | bytes 49160 | tf_op jit(solution)/shard_map/ppermute | solution.py:556
  10.4 1.3 %collective-permute-start.4 = (f32[4,16,256]{2,1,0:T(8,128)S(1)}, f32[4,16,256]{2,1,0:T(8,128)S(1)}, u32[]{:S(2)}, u32[]{:S(2)}) collective-permute-start(f32[4,16,256]{2,1,0:T(8,128)S(1)} %get-tuple-element.80.refs_8_), channel_id=1, source_target_pairs={{0,1},{1,0},{2,3},{3,2},{4,5},{5,4},{6,7},{7,6},{8,9},{9,8},{10,11... | collective-permute-start | bytes 196616 | tf_op jit(solution)/shard_map/ppermute | solution.py:584
  14.5 2.1 %collective-permute-start.5 = (f32[4,8,256]{2,1,0:T(8,128)S(1)}, f32[4,8,256]{2,1,0:T(8,128)S(1)}, u32[]{:S(2)}, u32[]{:S(2)}) collective-permute-start(f32[4,8,256]{2,1,0:T(8,128)S(1)} %get-tuple-element.99.refs_9_), channel_id=1, source_target_pairs={{0,1},{1,0},{2,3},{3,2},{4,5},{5,4},{6,7},{7,6},{8,9},{9,8},{10,11... | collective-permute-start | bytes 98312 | tf_op jit(solution)/shard_map/ppermute | solution.py:609

commit v7 on v6

--- a/solution.py
+++ b/solution.py
@@ -382,8 +382,8 @@
     in_groups(body, depth + 2, group, 0)
 
 
-def backward_block(band, depth, group, smooth, phis, edge, bx, by, bz, gained, damped, targets, mid, pixo, theirs, par, image, grads):
-    cols = smooth.shape[2]
+def combine(band, depth, targets, mid, pixo, theirs, par, image):
+    cols = mid.shape[2]
     back = pixo[2] == 1.0
     through_me, through_them = jnp.exp(-mid[0]), jnp.exp(-theirs[0])
     g, flow = [], jnp.zeros_like(through_me)
@@ -401,6 +401,13 @@
         k0, k1, k2 = [spread(par, 4 * c + k, band, cols) for c in range(3)]
         gam.append(g[0] * k0 + g[1] * k1 + g[2] * k2)
     queue = jnp.where(back, 0.0, -flow)
+
+    nil = jnp.zeros_like(through_me)
+    return gam, (queue, nil, nil)
+
+
+def shade_transpose(band, first, count, group, gam, carry, smooth, phis, edge, bx, by, bz, gained, damped, grads):
+    cols = bx.shape[2]
 
     def shade_back(z0, n, carry):
         run, part, last = carry
@@ -429,8 +436,10 @@
         out.flush()
         return run, part, last
 
-    nil = jnp.zeros_like(through_me)
-    in_groups(shade_back, depth + 2, group, (queue, nil, nil))
+    def step(z0, n, carry):
+        return shade_back(first + z0, n, carry)
+
+    return in_groups(step, count, group, carry)
 
 
 def smooth_transpose(band, depth, group, grads, emit):
@@ -450,7 +459,7 @@
                 done = []
         return carry
 
-    in_groups(smooth_back, depth, group, 0, loop=band > 8)
+    in_groups(smooth_back, depth, group, 0)
 
 
 def main_prepare_kernel(smooth, sig, smooth_tail, sig_tail, dxs, dys, rnorm, phis, edge, pixo, palette, par, *out):
@@ -460,16 +469,20 @@
     prepare_block(rows, nz, GROUP_MAIN[2], smooth, dxs, dys, rnorm, phis, edge, sig, pixo, palette, par, *out)
 
 
-def main_backward_kernel(smooth, smooth_tail, *refs):
-    nz, rows = smooth.shape[0], refs[0].shape[1]
-    backward_block(rows, nz, GROUP_MAIN[2], Joined(smooth, smooth_tail, nz), *refs)
+def main_backward_kernel(smooth, phis, edge, bx, by, bz, gained, damped, targets, mid, pixo, theirs, par, image, grads, state):
+    rows = image.shape[1]
+    nz = phis.shape[0] - 2
+    gam, carry = combine(rows, nz, targets, mid, pixo, theirs, par, image)
+    carry = shade_transpose(rows, 0, grads.shape[0], grads.shape[0], gam, carry, smooth, phis, edge, bx, by, bz, gained, damped, grads)
+    for i, v in enumerate((*gam, *carry)):
+        state[i] = v
 
 
 def far_prepare_kernel(smooth, *refs):
     prepare_block(8, smooth.shape[0] - HALO, GROUP_FAR[2], smooth, *refs)
 
 
-def main_result_kernel(grads, image, out, shown):
+def main_result_kernel(state, early, smooth, smooth_tail, phis, edge, bx, by, bz, gained, damped, image, out, shown, late):
     nz, rows, _ = out.shape
     core, odd = where_am_i()
     shift = jnp.where(odd == 1, rows - 2, 2)
@@ -481,6 +494,11 @@
         for i, v in enumerate(values):
             out[local_plane(core, nz, z0 + i)] = v
 
+    first = early.shape[0]
+    smooth = Joined(smooth, smooth_tail, nz)
+    gam, carry = [state[i] for i in range(4)], tuple(state[4 + i] for i in range(3))
+    grads = Joined(early, late, first)
+    shade_transpose(rows, first, nz + 2 - first, nz + 2 - first, gam, carry, smooth, phis, edge, bx, by, bz, gained, damped, grads)
     smooth_transpose(rows, nz, GROUP_MAIN[3], grads, emit)
 
 
@@ -512,7 +530,9 @@
         at = pl.ds(jnp.where(core == 0, z0, nz - size - z0), size)
         return pltpu.make_async_copy(a.at[at], b.at[at], sem.at[z0 // size])
 
-    backward_block(8, nz, GROUP_FAR[2], *res, image, grads)
+    smooth, phis, edge, bx, by, bz, gained, damped, targets, mid, pixo, theirs, par = res
+    gam, carry = combine(8, nz, targets, mid, pixo, theirs, par, image)
+    shade_transpose(8, 0, nz + 2, GROUP_FAR[2], gam, carry, smooth, phis, edge, bx, by, bz, gained, damped, grads)
     smooth_transpose(8, nz, GROUP_FAR[3], grads, emit)
     low = odd * (rows - 2)
     mask2 = (row >= low) & (row < low + 2)
@@ -592,12 +612,14 @@
         (smooth, sig, smooth_tail, sig_tail, dxs, dys, rnorm, phis, edge, pixo, pal, par),
         [VMEM] * 12,
     )
-    near_image, grads = call(
+    half = nz // 2 + 1
+    near_image, early, state = call(
         main_backward_kernel,
-        (sds(3, rows, cols), sds(nz + 2, rows, cols)),
-        (smooth, smooth_tail, phis, edge, *ready, mid, pixo, theirs, par),
-        [VMEM] * 14,
-    )
+        (sds(3, rows, cols), sds(half, rows, cols), sds(7, rows, cols)),
+        (smooth, phis, edge, *ready, mid, pixo, theirs, par),
+        [VMEM] * 13,
+    )
+    main = (early, smooth, smooth_tail, phis, edge, *ready[:5])
     lrecv, near_image = lax.optimization_barrier((lrecv, near_image))
     smooth, dxs, dys, rnorm, phis, edge, sig, mid, pixo = call(
         far_forward_kernel,
@@ -607,8 +629,14 @@
         scratch=[pltpu.VMEM((nz + 2, 8, cols), F32)],
     )
     theirs = lax.ppermute(mid, "depth", swap)
-    near_image, pixo = lax.optimization_barrier((near_image, pixo))
-    near_grad, near_image = call(main_result_kernel, (sds(nz, rows, cols), sds(3, rows, cols)), (grads, near_image), [VMEM] * 2)
+    near_image, state, pixo = lax.optimization_barrier((near_image, state, pixo))
+    near_grad, near_image = call(
+        main_result_kernel,
+        (sds(nz, rows, cols), sds(3, rows, cols)),
+        (state, *main, near_image),
+        [VMEM] * 12,
+        scratch=[pltpu.VMEM((nz + 2 - half, rows, cols), F32)],
+    )
     ready = call(
         far_prepare_kernel,
         prepared(8),

time: 18.1 us -> 18.1 us (level)
  waiting for transfers between devices: 2.87 us -> 3.06 us
    ppermute x1, waiting for transfers between devices: 1.25 us -> 1.64 us  [shards(): lrecv = lax.ppermute(lmsg, 'tile', far)]
    ppermute x2, waiting for transfers between devices: 0.69 us -> 0.49 us  [shards(): theirs = lax.ppermute(mid, 'depth', swap)]
  transfers between devices with their start and end apart: 6 -> 6, of which waited for: 4 -> 3; matrix products, arithmetic and copies ran while one was open for 0% -> 0% of each run, Pallas kernels for 19% -> 18%
where the time goes in v7:
time: 18.1 us; the launch traced here: 18 us
  starting transfers between devices  7.62 us (42%)
  Pallas kernels  6.55 us (36%)
  waiting for transfers between devices  3.06 us (17%)
  between operations  0.72 us (4%)
    pallas_call x11, Pallas kernels, call(): pl.pallas_call(kernel, out_shape=outs, in_specs=specs, out_specs=out_spec...  6.55 us
    ppermute x1, starting transfers between devices, shards(): lrecv = lax.ppermute(lmsg, 'tile', far)  3 us
    ppermute x2, starting transfers between devices, shards(): theirs = lax.ppermute(mid, 'depth', swap)  1.69 us
    ppermute x1, waiting for transfers between devices, shards(): lrecv = lax.ppermute(lmsg, 'tile', far)  1.64 us
    ppermute x1, starting transfers between devices, shards(): xrecv = lax.ppermute(xmsg, 'tile', near)  1.28 us
    ppermute x1, starting transfers between devices, shards(): zrecv = lax.ppermute(zmsg, 'depth', swap)  0.96 us
    ppermute x1, waiting for transfers between devices, shards(): zrecv = lax.ppermute(zmsg, 'depth', swap)  0.9 us
    ppermute x1, starting transfers between devices, shards(): xcorner = lax.ppermute(xrecv[:HALO], 'depth', swap)  0.7 us
  transfers between devices with their start and end apart: 6, of which 3 were waited for; matrix products, arithmetic and copies ran while one was open for 0% of the time, Pallas kernels for 18%

profile of v7, /device:TPU:9, one launch (start us, length us, event | category | flops | bytes accessed | tf_op | source)
XLA Modules:
  0.0 18.0 jit_solution(7021288198391156800)
XLA Ops:
  0.6 1.1 %shard_map.86 = (f32[4,16,256]{2,1,0:T(8,128)S(1)}, f32[32,16,256]{2,1,0:T(8,128)S(1)}, f32[3,16,256]{2,1,0:T(8,128)S(1)}, f32[3,128]{1,0:T(4,128)S(1)}, f32[15,8,128]{2,1,0:T(8,128)S(1)}) custom-call(f32[32,16,256]{2,1,0:T(8,128)} %dens_h.1, f32[16,256]{1,0:T(8,128)} %absorb_h.1, s32[16,256]{1,0:T(8,128)} %ids_h.1, s32[16]{0:T(128)} %view_h.1, ...), custom_call_target="tpu_custom_call" | custom-call | tf_op jit(solution)/shard_map/pallas_call | solution.py:22
  1.8 0.1 shard_map.87
  1.8 1.3 %collective-permute-start.2 = (f32[34,4,256]{2,1,0:T(4,128)S(1)}, f32[34,4,256]{2,1,0:T(4,128)S(1)}, u32[]{:S(2)}, u32[]{:S(2)}) collective-permute-start(f32[34,4,256]{2,1,0:T(4,128)S(1)} %get-tuple-element.59), channel_id=1, source_target_pairs={{0,2},{2,0},{4,6},{6,4},{8,10},{10,8},{12,14},{14,12},{16,18},{18,... | collective-permute-start | bytes 417800 | tf_op jit(solution)/shard_map/ppermute | solution.py:573
  3.1 1.0 %collective-permute-start = (f32[4,16,256]{2,1,0:T(8,128)S(1)}, f32[4,16,256]{2,1,0:T(8,128)S(1)}, u32[]{:S(2)}, u32[]{:S(2)}) collective-permute-start(f32[4,16,256]{2,1,0:T(8,128)S(1)} %get-tuple-element.57), channel_id=1, source_target_pairs={{0,1},{1,0},{2,3},{3,2},{4,5},{5,4},{6,7},{7,6},{8,9},{9,8},{10,11... | collective-permute-start | bytes 196616 | tf_op jit(solution)/shard_map/ppermute | solution.py:572
  4.1 0.9 %collective-permute-done.zrecv = f32[4,16,256]{2,1,0:T(8,128)S(1)} collective-permute-done((f32[4,16,256]{2,1,0:T(8,128)S(1)}, f32[4,16,256]{2,1,0:T(8,128)S(1)}, u32[]{:S(2)}, u32[]{:S(2)}) %collective-permute-start) | collective-permute-done | bytes 65568 | tf_op jit(solution)/shard_map/ppermute | solution.py:572
  5.0 3.0 %collective-permute-start.1 = (f32[36,4,256]{2,1,0:T(4,128)S(1)}, f32[36,4,256]{2,1,0:T(4,128)S(1)}, u32[]{:S(2)}, u32[]{:S(2)}) collective-permute-start(f32[36,4,256]{2,1,0:T(4,128)S(1)} %shard_map.88), channel_id=1, source_target_pairs={{2,4},{4,2},{6,8},{8,6},{10,12},{12,10},{14,16},{16,14},{18,20},{2... | collective-permute-start | bytes 442376 | tf_op jit(solution)/shard_map/ppermute | solution.py:575
  8.0 0.0 collective-permute-done.2.xrecv
  8.0 0.7 %collective-permute-start.3 = (f32[4,4,256]{2,1,0:T(4,128)S(1)}, f32[4,4,256]{2,1,0:T(4,128)S(1)}, u32[]{:S(2)}, u32[]{:S(2)}) collective-permute-start(f32[4,4,256]{2,1,0:T(4,128)S(1)} %slice.4), channel_id=1, source_target_pairs={{0,1},{1,0},{2,3},{3,2},{4,5},{5,4},{6,7},{7,6},{8,9},{9,8},{10,11... | collective-permute-start | bytes 49160 | tf_op jit(solution)/shard_map/ppermute | solution.py:576
  8.7 0.8 %shard_map.89 = (f32[32,24,256]{2,1,0:T(8,128)S(1)}, f32[31,16,256]{2,1,0:T(8,128)S(1)}, f32[31,16,256]{2,1,0:T(8,128)S(1)}, f32[3,16,256]{2,1,0:T(8,128)S(1)}, f32[16,256]{1,0:T(8,128)S(1)}) custom-call(f32[32,16,256]{2,1,0:T(8,128)S(1)} %get-tuple-element.55.dens, f32[3,16,256]{2,1,0:T(8,128)S(1)} %get-tuple-element.56.pix, ...), custom_call_target="tpu_custom_call" | custom-call | tf_op jit(solution)/shard_map/pallas_call | solution.py:22
  9.5 0.0 collective-permute-done.3.xcorner
  9.6 0.8 %shard_map.90 = (f32[4,24,256]{2,1,0:T(8,128)S(1)}, f32[3,16,256]{2,1,0:T(8,128)S(1)}, f32[34,16,256]{2,1,0:T(8,128)S(1)}, f32[34,16,256]{2,1,0:T(8,128)S(1)}, f...) custom-call(f32[32,24,256]{2,1,0:T(8,128)S(1)} %get-tuple-element.60, ...), custom_call_target="tpu_custom_call" | custom-call | tf_op jit(solution)/shard_map/pallas_call | solution.py:22
  10.4 0.4 %collective-permute-start.4 = (f32[4,16,256]{2,1,0:T(8,128)S(1)}, f32[4,16,256]{2,1,0:T(8,128)S(1)}, u32[]{:S(2)}, u32[]{:S(2)}) collective-permute-start(f32[4,16,256]{2,1,0:T(8,128)S(1)} %get-tuple-element.82.mid), channel_id=1, source_target_pairs={{0,1},{1,0},{2,3},{3,2},{4,5},{5,4},{6,7},{7,6},{8,9},{9,8},{10,11... | collective-permute-start | bytes 196616 | tf_op jit(solution)/shard_map/ppermute | solution.py:604
  10.8 0.4 %shard_map.91 = (f32[34,16,256]{2,1,0:T(8,128)S(1)}, f32[34,16,256]{2,1,0:T(8,128)S(1)}, f32[34,16,256]{2,1,0:T(8,128)S(1)}, f32[34,16,256]{2,1,0:T(8,128)S(1)},...) custom-call(f32[32,24,256]{2,1,0:T(8,128)S(1)} %get-tuple-element.60.smooth, ...), custom_call_target="tpu_custom_call" | custom-call | tf_op jit(solution)/shard_map/pallas_call | solution.py:22
  11.2 0.5 %collective-permute-done.4.theirs = f32[4,16,256]{2,1,0:T(8,128)S(1)} collective-permute-done((f32[4,16,256]{2,1,0:T(8,128)S(1)}, f32[4,16,256]{2,1,0:T(8,128)S(1)}, u32[]{:S(2)}, u32[]{:S(2)}) %collective-permute-start.4) | collective-permute-done | bytes 65568 | tf_op jit(solution)/shard_map/ppermute | solution.py:604
  11.7 0.4 %shard_map.92 = (f32[3,16,256]{2,1,0:T(8,128)S(1)}, f32[17,16,256]{2,1,0:T(8,128)S(1)}, f32[7,16,256]{2,1,0:T(8,128)S(1)}) custom-call(f32[32,24,256]{2,1,0:T(8,128)S(1)} %get-tuple-element.60.smooth, f32[34,16,256]{2,1,0:T(8,128)S(1)} %get-tuple-element.68.phis, f32[35,16,256]{2,1,0:T(8,128)S(1)} %get-tuple-element.69.edge, ...), custom_call_target="tpu_custom_call" | custom-call | tf_op jit(solution)/shard_map/pallas_call | solution.py:22
  12.1 1.6 %collective-permute-done.1.lrecv = f32[36,4,256]{2,1,0:T(4,128)S(1)} collective-permute-done((f32[36,4,256]{2,1,0:T(4,128)S(1)}, f32[36,4,256]{2,1,0:T(4,128)S(1)}, u32[]{:S(2)}, u32[]{:S(2)}) %collective-permute-start.1) | collective-permute-done | bytes 147488 | tf_op jit(solution)/shard_map/ppermute | solution.py:575
  13.7 0.8 %shard_map.93 = (f32[36,16,256]{2,1,0:T(8,128)S(1)}, f32[34,8,256]{2,1,0:T(8,128)S(1)}, f32[34,8,256]{2,1,0:T(8,128)S(1)}, f32[34,8,256]{2,1,0:T(8,128)S(1)}, f3...) custom-call(f32[32,16,256]{2,1,0:T(8,128)S(1)} %get-tuple-element.55, ...), custom_call_target="tpu_custom_call" | custom-call | tf_op jit(solution)/shard_map/pallas_call | solution.py:22
  14.5 1.3 %collective-permute-start.5 = (f32[4,8,256]{2,1,0:T(8,128)S(1)}, f32[4,8,256]{2,1,0:T(8,128)S(1)}, u32[]{:S(2)}, u32[]{:S(2)}) collective-permute-start(f32[4,8,256]{2,1,0:T(8,128)S(1)} %get-tuple-element.102.refs_9_), channel_id=1, source_target_pairs={{0,1},{1,0},{2,3},{3,2},{4,5},{5,4},{6,7},{7,6},{8,9},{9,8},{10,11... | collective-permute-start | bytes 98312 | tf_op jit(solution)/shard_map/ppermute | solution.py:631
  15.8 0.7 %shard_map.95 = (f32[32,16,256]{2,1,0:T(8,128)S(1)}, f32[3,16,256]{2,1,0:T(8,128)S(1)}) custom-call(f32[7,16,256]{2,1,0:T(8,128)S(1)} %get-tuple-element.103.state, f32[17,16,256]{2,1,0:T(8,128)S(1)} %get-tuple-element.104.early, f32[32,24,256]{2,1,0:T(8,128)S(1)} %get-tuple-element.60.smooth, f32[4,24,256]{2,1,0:T(8,128)S(1)} %get-tuple-element.70.smooth_tail, ...), custom_call_target="tpu_custom_call" | custom-call | tf_op jit(solution)/shard_map/pallas_call | solution.py:22
  16.5 0.2 %shard_map.94 = (f32[34,8,256]{2,1,0:T(8,128)S(1)}, f32[34,8,256]{2,1,0:T(8,128)S(1)}, f32[34,8,256]{2,1,0:T(8,128)S(1)}, f32[34,8,256]{2,1,0:T(8,128)S(1)}, f32...) custom-call(f32[36,16,256]{2,1,0:T(8,128)S(1)} %get-tuple-element.85.smooth.refs_0_, ...), custom_call_target="tpu_custom_call" | custom-call | tf_op jit(solution)/shard_map/pallas_call | solution.py:22
  16.7 0.0 collective-permute-done.5.refs_11_
  16.7 1.2 %shard_map.96 = (f32[3,8,256]{2,1,0:T(8,128)}, f32[32,16,256]{2,1,0:T(8,128)}) custom-call(f32[36,16,256]{2,1,0:T(8,128)S(1)} %get-tuple-element.85.smooth.refs_0_, f32[34,8,256]{2,1,0:T(8,128)S(1)} %get-tuple-element.86.refs_3_.refs_1_, f32[35,8,256]{2,1,0:T(8,128)S(1)} %get-tuple-element.87.refs_4_.refs_2_, f32[34,8,256]{2,1,0:T(8,128)S(1)} %get-tuple-element.96.refs_3_, ...), custom_call_target="tpu_custom_call" | custom-call | tf_op jit(solution)/shard_map/pallas_call | solution.py:22
  (2 shorter events, 0.0 us)
Async XLA Ops:
  1.8 6.2 %collective-permute-start.2 = (f32[34,4,256]{2,1,0:T(4,128)S(1)}, f32[34,4,256]{2,1,0:T(4,128)S(1)}, u32[]{:S(2)}, u32[]{:S(2)}) collective-permute-start(f32[34,4,256]{2,1,0:T(4,128)S(1)} %get-tuple-element.59), channel_id=1, source_target_pairs={{0,2},{2,0},{4,6},{6,4},{8,10},{10,8},{12,14},{14,12},{16,18},{18,... | collective-permute-start | bytes 417800 | tf_op jit(solution)/shard_map/ppermute | solution.py:573
  3.1 1.9 %collective-permute-start = (f32[4,16,256]{2,1,0:T(8,128)S(1)}, f32[4,16,256]{2,1,0:T(8,128)S(1)}, u32[]{:S(2)}, u32[]{:S(2)}) collective-permute-start(f32[4,16,256]{2,1,0:T(8,128)S(1)} %get-tuple-element.57), channel_id=1, source_target_pairs={{0,1},{1,0},{2,3},{3,2},{4,5},{5,4},{6,7},{7,6},{8,9},{9,8},{10,11... | collective-permute-start | bytes 196616 | tf_op jit(solution)/shard_map/ppermute | solution.py:572
  5.0 8.7 %collective-permute-start.1 = (f32[36,4,256]{2,1,0:T(4,128)S(1)}, f32[36,4,256]{2,1,0:T(4,128)S(1)}, u32[]{:S(2)}, u32[]{:S(2)}) collective-permute-start(f32[36,4,256]{2,1,0:T(4,128)S(1)} %shard_map.88), channel_id=1, source_target_pairs={{2,4},{4,2},{6,8},{8,6},{10,12},{12,10},{14,16},{16,14},{18,20},{2... | collective-permute-start | bytes 442376 | tf_op jit(solution)/shard_map/ppermute | solution.py:575
  8.0 1.5 %collective-permute-start.3 = (f32[4,4,256]{2,1,0:T(4,128)S(1)}, f32[4,4,256]{2,1,0:T(4,128)S(1)}, u32[]{:S(2)}, u32[]{:S(2)}) collective-permute-start(f32[4,4,256]{2,1,0:T(4,128)S(1)} %slice.4), channel_id=1, source_target_pairs={{0,1},{1,0},{2,3},{3,2},{4,5},{5,4},{6,7},{7,6},{8,9},{9,8},{10,11... | collective-permute-start | bytes 49160 | tf_op jit(solution)/shard_map/ppermute | solution.py:576
  10.4 1.3 %collective-permute-start.4 = (f32[4,16,256]{2,1,0:T(8,128)S(1)}, f32[4,16,256]{2,1,0:T(8,128)S(1)}, u32[]{:S(2)}, u32[]{:S(2)}) collective-permute-start(f32[4,16,256]{2,1,0:T(8,128)S(1)} %get-tuple-element.82.mid), channel_id=1, source_target_pairs={{0,1},{1,0},{2,3},{3,2},{4,5},{5,4},{6,7},{7,6},{8,9},{9,8},{10,11... | collective-permute-start | bytes 196616 | tf_op jit(solution)/shard_map/ppermute | solution.py:604
  14.5 2.2 %collective-permute-start.5 = (f32[4,8,256]{2,1,0:T(8,128)S(1)}, f32[4,8,256]{2,1,0:T(8,128)S(1)}, u32[]{:S(2)}, u32[]{:S(2)}) collective-permute-start(f32[4,8,256]{2,1,0:T(8,128)S(1)} %get-tuple-element.102.refs_9_), channel_id=1, source_target_pairs={{0,1},{1,0},{2,3},{3,2},{4,5},{5,4},{6,7},{7,6},{8,9},{9,8},{10,11... | collective-permute-start | bytes 98312 | tf_op jit(solution)/shard_map/ppermute | solution.py:631

commit v8 on v6

--- a/solution.py
+++ b/solution.py
@@ -92,14 +92,15 @@
     return jnp.concatenate([t] * (rows // t.shape[0]), axis=0)
 
 
-def fetch_kernel(dens_h, absorb_h, ids_h, view_h, pal_h, coef_h, light_h, zmsg, dens, pix, pal, par, ids, view, coef, light, sem):
-    nz, rows, cols = dens.shape
+def fetch_kernel(dens_h, absorb_h, ids_h, view_h, pal_h, coef_h, light_h, zmsg, pix, pal, par, ids, view, coef, light, sem):
+    nz, rows, cols = dens_h.shape
     core, _ = where_am_i()
-    pairs = ((dens_h, dens), (view_h, view), (ids_h, ids), (absorb_h, pix.at[0]), (coef_h, coef), (light_h, light), (pal_h, pal))
+    seam = [(dens_h.at[local_plane(core, nz, nz - 1 - j)], zmsg.at[j]) for j in range(HALO)]
+    pairs = (*seam, (view_h, view), (ids_h, ids), (absorb_h, pix.at[0]), (coef_h, coef), (light_h, light), (pal_h, pal))
     copies = [pltpu.make_async_copy(a, b, sem.at[i]) for i, (a, b) in enumerate(pairs)]
     for c in copies:
         c.start()
-    for c in copies[1:]:
+    for c in copies[HALO:]:
         c.wait()
     row = lax.broadcasted_iota(jnp.int32, (rows, cols), 0)
     seen = jnp.zeros((rows, cols), F32)
@@ -114,9 +115,8 @@
         if i == 0:
             value = jnp.where(core == 0, value, -value)
         par[12 + i] = jnp.full(par.shape[1:], value)
-    copies[0].wait()
-    for j in range(HALO):
-        zmsg[j] = dens[local_plane(core, nz, nz - 1 - j)]
+    for c in copies[:HALO]:
+        c.wait()
 
 
 def edges_kernel(dens, pix, xmsg, lmsg):
@@ -531,10 +531,11 @@
     nz, rows, cols = density.shape
     tiles = lax.axis_size("tile")
     sds = resident
-
-    zmsg, dens, pix, pal, par = call(
+    dens = density
+
+    zmsg, pix, pal, par = call(
         fetch_kernel,
-        (sds(HALO, rows, cols), sds(nz, rows, cols), sds(PIX, rows, cols), sds(*palette.shape), sds(15, 8, 128)),
+        (sds(HALO, rows, cols), sds(PIX, rows, cols), sds(*palette.shape), sds(15, 8, 128)),
         (density, absorption, target_ids, view_dir, palette, emission_coef, light),
         [HBM] * 7,
         scratch=[
@@ -542,7 +543,7 @@
             pltpu.SMEM(view_dir.shape, jnp.int32),
             pltpu.SMEM(emission_coef.shape, F32),
             pltpu.SMEM(light.shape, F32),
-            pltpu.SemaphoreType.DMA((7,)),
+            pltpu.SemaphoreType.DMA((6 + HALO,)),
         ],
     )
     xmsg, lmsg = call(edges_kernel, (sds(nz + 2, HALO, cols), sds(nz + 2, HALO, cols)), (dens, pix), [VMEM] * 2)

time: 18.1 us -> 18.1 us (level)
  no operation moved by 1% of the time
where the time goes in v8:
time: 18.1 us; the launch traced here: 17.9 us
  starting transfers between devices  7.62 us (42%)
  Pallas kernels  6.55 us (36%)
  waiting for transfers between devices  2.87 us (16%)
  between operations  0.72 us (4%)
    pallas_call x11, Pallas kernels, call(): pl.pallas_call(kernel, out_shape=outs, in_specs=specs, out_specs=out_spec...  6.55 us
    ppermute x1, starting transfers between devices, shards(): lrecv = lax.ppermute(lmsg, 'tile', far)  3 us
    ppermute x2, starting transfers between devices, shards(): theirs = lax.ppermute(mid, 'depth', swap)  1.69 us
    ppermute x1, starting transfers between devices, shards(): xrecv = lax.ppermute(xmsg, 'tile', near)  1.28 us
    ppermute x1, waiting for transfers between devices, shards(): lrecv = lax.ppermute(lmsg, 'tile', far)  1.25 us
    ppermute x1, starting transfers between devices, shards(): zrecv = lax.ppermute(zmsg, 'depth', swap)  0.96 us
    ppermute x1, waiting for transfers between devices, shards(): zrecv = lax.ppermute(zmsg, 'depth', swap)  0.9 us
    ppermute x1, starting transfers between devices, shards(): xcorner = lax.ppermute(xrecv[:HALO], 'depth', swap)  0.7 us
  transfers between devices with their start and end apart: 6, of which 4 were waited for; matrix products, arithmetic and copies ran while one was open for 0% of the time, Pallas kernels for 19%

profile of v8, /device:TPU:9, one launch (start us, length us, event | category | flops | bytes accessed | tf_op | source)
XLA Modules:
  0.0 17.9 jit_solution(9479829007602459282)
XLA Ops:
  0.6 0.0 copy-start
  0.6 1.0 %shard_map.86 = (f32[4,16,256]{2,1,0:T(8,128)S(1)}, f32[3,16,256]{2,1,0:T(8,128)S(1)}, f32[3,128]{1,0:T(4,128)S(1)}, f32[15,8,128]{2,1,0:T(8,128)S(1)}) custom-call(f32[32,16,256]{2,1,0:T(8,128)} %dens.7, f32[16,256]{1,0:T(8,128)} %absorb_h.1, s32[16,256]{1,0:T(8,128)} %ids_h.1, s32[16]{0:T(128)} %view_h.1, f32[3,128]{1,0:T(4,128)} %pal_h.1, f32[3,4]{1,0:T(4,128)} %coef_h.1, ...), custom_call_target="tpu_custom_call" | custom-call | tf_op jit(solution)/shard_map/pallas_call | solution.py:22
  1.6 0.1 copy-done
  1.8 0.1 shard_map.87
  1.9 1.3 %collective-permute-start.2 = (f32[34,4,256]{2,1,0:T(4,128)S(1)}, f32[34,4,256]{2,1,0:T(4,128)S(1)}, u32[]{:S(2)}, u32[]{:S(2)}) collective-permute-start(f32[34,4,256]{2,1,0:T(4,128)S(1)} %get-tuple-element.55), channel_id=1, source_target_pairs={{0,2},{2,0},{4,6},{6,4},{8,10},{10,8},{12,14},{14,12},{16,18},{18,... | collective-permute-start | bytes 417800 | tf_op jit(solution)/shard_map/ppermute | solution.py:554
  3.1 1.0 %collective-permute-start = (f32[4,16,256]{2,1,0:T(8,128)S(1)}, f32[4,16,256]{2,1,0:T(8,128)S(1)}, u32[]{:S(2)}, u32[]{:S(2)}) collective-permute-start(f32[4,16,256]{2,1,0:T(8,128)S(1)} %get-tuple-element.53), channel_id=1, source_target_pairs={{0,1},{1,0},{2,3},{3,2},{4,5},{5,4},{6,7},{7,6},{8,9},{9,8},{10,11... | collective-permute-start | bytes 196616 | tf_op jit(solution)/shard_map/ppermute | solution.py:553
  4.1 0.9 %collective-permute-done.zrecv = f32[4,16,256]{2,1,0:T(8,128)S(1)} collective-permute-done((f32[4,16,256]{2,1,0:T(8,128)S(1)}, f32[4,16,256]{2,1,0:T(8,128)S(1)}, u32[]{:S(2)}, u32[]{:S(2)}) %collective-permute-start) | collective-permute-done | bytes 65568 | tf_op jit(solution)/shard_map/ppermute | solution.py:553
  5.0 3.0 %collective-permute-start.1 = (f32[36,4,256]{2,1,0:T(4,128)S(1)}, f32[36,4,256]{2,1,0:T(4,128)S(1)}, u32[]{:S(2)}, u32[]{:S(2)}) collective-permute-start(f32[36,4,256]{2,1,0:T(4,128)S(1)} %shard_map.88), channel_id=1, source_target_pairs={{2,4},{4,2},{6,8},{8,6},{10,12},{12,10},{14,16},{16,14},{18,20},{2... | collective-permute-start | bytes 442376 | tf_op jit(solution)/shard_map/ppermute | solution.py:556
  8.0 0.0 collective-permute-done.2.xrecv
  8.0 0.7 %collective-permute-start.3 = (f32[4,4,256]{2,1,0:T(4,128)S(1)}, f32[4,4,256]{2,1,0:T(4,128)S(1)}, u32[]{:S(2)}, u32[]{:S(2)}) collective-permute-start(f32[4,4,256]{2,1,0:T(4,128)S(1)} %slice.4), channel_id=1, source_target_pairs={{0,1},{1,0},{2,3},{3,2},{4,5},{5,4},{6,7},{7,6},{8,9},{9,8},{10,11... | collective-permute-start | bytes 49160 | tf_op jit(solution)/shard_map/ppermute | solution.py:557
  8.7 0.8 %shard_map.89 = (f32[32,24,256]{2,1,0:T(8,128)S(1)}, f32[31,16,256]{2,1,0:T(8,128)S(1)}, f32[31,16,256]{2,1,0:T(8,128)S(1)}, f32[3,16,256]{2,1,0:T(8,128)S(1)}, f32[16,256]{1,0:T(8,128)S(1)}) custom-call(f32[32,16,256]{2,1,0:T(8,128)S(1)} %copy-done, f32[3,16,256]{2,1,0:T(8,128)S(1)} %get-tuple-element.52.pix, f32[34,4,256]{2,1,0:T(4,128)S(1)} %collective-permute-done.2.xrecv), custom_call_target="tpu_custom_call" | custom-call | tf_op jit(solution)/shard_map/pallas_call | solution.py:22
  9.5 0.0 collective-permute-done.3.xcorner
  9.6 0.8 %shard_map.90 = (f32[4,24,256]{2,1,0:T(8,128)S(1)}, f32[3,16,256]{2,1,0:T(8,128)S(1)}, f32[34,16,256]{2,1,0:T(8,128)S(1)}, f32[34,16,256]{2,1,0:T(8,128)S(1)}, f...) custom-call(f32[32,24,256]{2,1,0:T(8,128)S(1)} %get-tuple-element.56, ...), custom_call_target="tpu_custom_call" | custom-call | tf_op jit(solution)/shard_map/pallas_call | solution.py:22
  10.4 0.4 %collective-permute-start.4 = (f32[4,16,256]{2,1,0:T(8,128)S(1)}, f32[4,16,256]{2,1,0:T(8,128)S(1)}, u32[]{:S(2)}, u32[]{:S(2)}) collective-permute-start(f32[4,16,256]{2,1,0:T(8,128)S(1)} %get-tuple-element.78.refs_8_), channel_id=1, source_target_pairs={{0,1},{1,0},{2,3},{3,2},{4,5},{5,4},{6,7},{7,6},{8,9},{9,8},{10,11... | collective-permute-start | bytes 196616 | tf_op jit(solution)/shard_map/ppermute | solution.py:585
  10.8 0.4 %shard_map.91 = (f32[34,16,256]{2,1,0:T(8,128)S(1)}, f32[34,16,256]{2,1,0:T(8,128)S(1)}, f32[34,16,256]{2,1,0:T(8,128)S(1)}, f32[34,16,256]{2,1,0:T(8,128)S(1)},...) custom-call(f32[32,24,256]{2,1,0:T(8,128)S(1)} %get-tuple-element.56.smooth, ...), custom_call_target="tpu_custom_call" | custom-call | tf_op jit(solution)/shard_map/pallas_call | solution.py:22
  11.2 0.5 %collective-permute-done.4.refs_10_ = f32[4,16,256]{2,1,0:T(8,128)S(1)} collective-permute-done((f32[4,16,256]{2,1,0:T(8,128)S(1)}, f32[4,16,256]{2,1,0:T(8,128)S(1)}, u32[]{:S(2)}, u32[]{:S(2)}) %collective-permute-start.4) | collective-permute-done | bytes 65568 | tf_op jit(solution)/shard_map/ppermute | solution.py:585
  11.7 0.8 %shard_map.92 = (f32[3,16,256]{2,1,0:T(8,128)S(1)}, f32[34,16,256]{2,1,0:T(8,128)S(1)}) custom-call(f32[32,24,256]{2,1,0:T(8,128)S(1)} %get-tuple-element.56.smooth, f32[4,24,256]{2,1,0:T(8,128)S(1)} %get-tuple-element.64.smooth_tail, f32[34,16,256]{2,1,0:T(8,128)S(1)} %get-tuple-element.65.phis.refs_0_, f32[35,16,256]{2,1,0:T(8,128)S(1)} %get-tuple-element.66.edge.refs_1_, ...), custom_call_target="tpu_custom_call" | custom-call | tf_op jit(solution)/shard_map/pallas_call | solution.py:22
  12.5 1.3 %collective-permute-done.1.lrecv = f32[36,4,256]{2,1,0:T(4,128)S(1)} collective-permute-done((f32[36,4,256]{2,1,0:T(4,128)S(1)}, f32[36,4,256]{2,1,0:T(4,128)S(1)}, u32[]{:S(2)}, u32[]{:S(2)}) %collective-permute-start.1) | collective-permute-done | bytes 147488 | tf_op jit(solution)/shard_map/ppermute | solution.py:556
  13.7 0.8 %shard_map.93 = (f32[36,16,256]{2,1,0:T(8,128)S(1)}, f32[34,8,256]{2,1,0:T(8,128)S(1)}, f32[34,8,256]{2,1,0:T(8,128)S(1)}, f32[34,8,256]{2,1,0:T(8,128)S(1)}, f3...) custom-call(f32[32,16,256]{2,1,0:T(8,128)S(1)} %copy-done, ...), custom_call_target="tpu_custom_call" | custom-call | tf_op jit(solution)/shard_map/pallas_call | solution.py:22
  14.6 1.3 %collective-permute-start.5 = (f32[4,8,256]{2,1,0:T(8,128)S(1)}, f32[4,8,256]{2,1,0:T(8,128)S(1)}, u32[]{:S(2)}, u32[]{:S(2)}) collective-permute-start(f32[4,8,256]{2,1,0:T(8,128)S(1)} %get-tuple-element.97.refs_9_), channel_id=1, source_target_pairs={{0,1},{1,0},{2,3},{3,2},{4,5},{5,4},{6,7},{7,6},{8,9},{9,8},{10,11... | collective-permute-start | bytes 98312 | tf_op jit(solution)/shard_map/ppermute | solution.py:610
  15.8 0.4 %shard_map.95 = (f32[32,16,256]{2,1,0:T(8,128)S(1)}, f32[3,16,256]{2,1,0:T(8,128)S(1)}) custom-call(f32[34,16,256]{2,1,0:T(8,128)S(1)} %get-tuple-element.98.grads, f32[3,16,256]{2,1,0:T(8,128)S(1)} %get-tuple-element.99.image), custom_call_target="tpu_custom_call" | custom-call | tf_op jit(solution)/shard_map/pallas_call | solution.py:22
  16.3 0.2 %shard_map.94 = (f32[34,8,256]{2,1,0:T(8,128)S(1)}, f32[34,8,256]{2,1,0:T(8,128)S(1)}, f32[34,8,256]{2,1,0:T(8,128)S(1)}, f32[34,8,256]{2,1,0:T(8,128)S(1)}, f32...) custom-call(f32[36,16,256]{2,1,0:T(8,128)S(1)} %get-tuple-element.81.smooth.refs_0_, ...), custom_call_target="tpu_custom_call" | custom-call | tf_op jit(solution)/shard_map/pallas_call | solution.py:22
  16.5 0.2 %collective-permute-done.5.refs_11_ = f32[4,8,256]{2,1,0:T(8,128)S(1)} collective-permute-done((f32[4,8,256]{2,1,0:T(8,128)S(1)}, f32[4,8,256]{2,1,0:T(8,128)S(1)}, u32[]{:S(2)}, u32[]{:S(2)}) %collective-permute-start.5) | collective-permute-done | bytes 32800 | tf_op jit(solution)/shard_map/ppermute | solution.py:610
  16.7 1.2 %shard_map.96 = (f32[3,8,256]{2,1,0:T(8,128)}, f32[32,16,256]{2,1,0:T(8,128)}) custom-call(f32[36,16,256]{2,1,0:T(8,128)S(1)} %get-tuple-element.81.smooth.refs_0_, f32[34,8,256]{2,1,0:T(8,128)S(1)} %get-tuple-element.82.refs_3_.refs_1_, f32[35,8,256]{2,1,0:T(8,128)S(1)} %get-tuple-element.83.refs_4_.refs_2_, f32[34,8,256]{2,1,0:T(8,128)S(1)} %get-tuple-element.91.refs_3_, ...), custom_call_target="tpu_custom_call" | custom-call | tf_op jit(solution)/shard_map/pallas_call | solution.py:22
  (2 shorter events, 0.0 us)
Async XLA Ops:
  0.6 1.2 %copy-start = (f32[32,16,256]{2,1,0:T(8,128)S(1)}, f32[32,16,256]{2,1,0:T(8,128)}, u32[]{:S(2)}) copy-start(f32[32,16,256]{2,1,0:T(8,128)} %dens.7) | copy-start | bytes 1572868
  1.9 6.2 %collective-permute-start.2 = (f32[34,4,256]{2,1,0:T(4,128)S(1)}, f32[34,4,256]{2,1,0:T(4,128)S(1)}, u32[]{:S(2)}, u32[]{:S(2)}) collective-permute-start(f32[34,4,256]{2,1,0:T(4,128)S(1)} %get-tuple-element.55), channel_id=1, source_target_pairs={{0,2},{2,0},{4,6},{6,4},{8,10},{10,8},{12,14},{14,12},{16,18},{18,... | collective-permute-start | bytes 417800 | tf_op jit(solution)/shard_map/ppermute | solution.py:554
  3.1 1.9 %collective-permute-start = (f32[4,16,256]{2,1,0:T(8,128)S(1)}, f32[4,16,256]{2,1,0:T(8,128)S(1)}, u32[]{:S(2)}, u32[]{:S(2)}) collective-permute-start(f32[4,16,256]{2,1,0:T(8,128)S(1)} %get-tuple-element.53), channel_id=1, source_target_pairs={{0,1},{1,0},{2,3},{3,2},{4,5},{5,4},{6,7},{7,6},{8,9},{9,8},{10,11... | collective-permute-start | bytes 196616 | tf_op jit(solution)/shard_map/ppermute | solution.py:553
  5.0 8.7 %collective-permute-start.1 = (f32[36,4,256]{2,1,0:T(4,128)S(1)}, f32[36,4,256]{2,1,0:T(4,128)S(1)}, u32[]{:S(2)}, u32[]{:S(2)}) collective-permute-start(f32[36,4,256]{2,1,0:T(4,128)S(1)} %shard_map.88), channel_id=1, source_target_pairs={{2,4},{4,2},{6,8},{8,6},{10,12},{12,10},{14,16},{16,14},{18,20},{2... | collective-permute-start | bytes 442376 | tf_op jit(solution)/shard_map/ppermute | solution.py:556
  8.0 1.5 %collective-permute-start.3 = (f32[4,4,256]{2,1,0:T(4,128)S(1)}, f32[4,4,256]{2,1,0:T(4,128)S(1)}, u32[]{:S(2)}, u32[]{:S(2)}) collective-permute-start(f32[4,4,256]{2,1,0:T(4,128)S(1)} %slice.4), channel_id=1, source_target_pairs={{0,1},{1,0},{2,3},{3,2},{4,5},{5,4},{6,7},{7,6},{8,9},{9,8},{10,11... | collective-permute-start | bytes 49160 | tf_op jit(solution)/shard_map/ppermute | solution.py:557
  10.4 1.3 %collective-permute-start.4 = (f32[4,16,256]{2,1,0:T(8,128)S(1)}, f32[4,16,256]{2,1,0:T(8,128)S(1)}, u32[]{:S(2)}, u32[]{:S(2)}) collective-permute-start(f32[4,16,256]{2,1,0:T(8,128)S(1)} %get-tuple-element.78.refs_8_), channel_id=1, source_target_pairs={{0,1},{1,0},{2,3},{3,2},{4,5},{5,4},{6,7},{7,6},{8,9},{9,8},{10,11... | collective-permute-start | bytes 196616 | tf_op jit(solution)/shard_map/ppermute | solution.py:585
  14.6 2.1 %collective-permute-start.5 = (f32[4,8,256]{2,1,0:T(8,128)S(1)}, f32[4,8,256]{2,1,0:T(8,128)S(1)}, u32[]{:S(2)}, u32[]{:S(2)}) collective-permute-start(f32[4,8,256]{2,1,0:T(8,128)S(1)} %get-tuple-element.97.refs_9_), channel_id=1, source_target_pairs={{0,1},{1,0},{2,3},{3,2},{4,5},{5,4},{6,7},{7,6},{8,9},{9,8},{10,11... | collective-permute-start | bytes 98312 | tf_op jit(solution)/shard_map/ppermute | solution.py:610

commit v9 on v8

--- a/solution.py
+++ b/solution.py
@@ -11,7 +11,7 @@
 PIX = 3
 GROUP_MAIN = (10,16,17,16)
 GROUP_FAR = (30,32,34,32)
-CHUNK = 8
+CHUNK = 4
 LATE = True
 VMEM = pl.BlockSpec(memory_space=pltpu.VMEM)
 HBM = pl.BlockSpec(memory_space=pl.ANY)
@@ -186,7 +186,7 @@
     return a, ids, back
 
 
-def smooth_planes(block, first, n, signed, depth, smooth, taus, sig, total, lead=None):
+def smooth_planes(block, first, n, signed, depth, smooth, taus, softs, total, lead=None):
     band, wide = block.band, block.band + 8
     out = Stores()
     zs = [first - 1 + i for i in range(n + 2)]
@@ -204,32 +204,32 @@
             soft = jnp.log(1.0 + jnp.exp(s[:band]))
             tau = signed * soft
             out.put(taus, zs[i + 1], tau)
-            out.put(sig, zs[i + 1], 1.0 - jnp.exp(-soft))
+            out.put(softs, zs[i + 1], soft)
             if not static or first + i < depth:
                 total = total + tau
     out.flush()
     return total
 
 
-def smooth_slab(block, core, depth, group, smooth, taus, sig, pixo):
+def smooth_slab(block, core, depth, group, smooth, taus, softs, pixo):
     a, ids, back = pixels(block, core)
     signed = a * (1.0 / (2 * depth)) * (1.0 - 2.0 * back)
     pixo[0], pixo[1], pixo[2] = a, ids, back
     face = block.plane(0)
     smooth[0] = face * 0.125
     zero = jnp.zeros_like(face)
-    total = smooth_planes(block, 0, 1, signed, depth, smooth, taus, sig, jnp.zeros_like(a), lead=zero)
+    total = smooth_planes(block, 0, 1, signed, depth, smooth, taus, softs, jnp.zeros_like(a), lead=zero)
 
     def body(z, n, total):
-        return smooth_planes(block, z + 1, n, signed, depth, smooth, taus, sig, total)
+        return smooth_planes(block, z + 1, n, signed, depth, smooth, taus, softs, total)
 
     return in_groups(body, depth - 2, group, total, loop=block.band > 8)
 
 
-def smooth_seam(block, depth, smooth, taus, sig, pixo, total):
+def smooth_seam(block, depth, smooth, taus, softs, pixo, total):
     a, back = pixo[0], pixo[2]
     signed = a * (1.0 / (2 * depth)) * (1.0 - 2.0 * back)
-    return smooth_planes(block, depth - 1, 4, signed, depth, smooth, taus, sig, total)
+    return smooth_planes(block, depth - 1, 4, signed, depth, smooth, taus, softs, total)
 
 
 def shade_slab(band, depth, group, total, par, smooth, taus, dxs, dys, rnorm, phis, edge, mid, pixo):
@@ -305,7 +305,7 @@
     return Block(rows, jnp.where(odd == 1, 2, rows + 8 - 2), own, halo)
 
 
-def far_forward_kernel(dens, pix, zrecv, lrecv, par, smooth, dxs, dys, rnorm, phis, edge, sig, mid, pixo, taus):
+def far_forward_kernel(dens, pix, zrecv, lrecv, par, smooth, dxs, dys, rnorm, phis, edge, softs, mid, pixo, taus):
     nz, rows, _ = dens.shape
     core, odd = where_am_i()
     at = pl.multiple_of(odd * (rows - 8), 8)
@@ -333,26 +333,26 @@
         return lrecv[nz + 1 - z]
 
     block = Block(8, jnp.where(odd == 1, 16 - 2, 2), own, halo)
-    total = smooth_slab(block, core, nz, GROUP_FAR[0], smooth, taus, sig, pixo)
-    total = smooth_seam(block, nz, smooth, taus, sig, pixo, total)
+    total = smooth_slab(block, core, nz, GROUP_FAR[0], smooth, taus, softs, pixo)
+    total = smooth_seam(block, nz, smooth, taus, softs, pixo, total)
     shade_slab(8, nz, GROUP_FAR[1], total, par, smooth, taus, dxs, dys, rnorm, phis, edge, mid, pixo)
 
 
-def main_smooth_kernel(dens, pix, xrecv, smooth, taus, sig, pixo, total):
+def main_smooth_kernel(dens, pix, xrecv, smooth, taus, softs, pixo, total):
     core, _ = where_am_i()
     block = main_block(dens, pix, xrecv)
-    total[...] = smooth_slab(block, core, dens.shape[0], GROUP_MAIN[0], smooth, taus, sig, pixo)
-
-
-def main_shade_kernel(smooth, taus, sig, pixo, total, dens, pix, zrecv, xrecv, xcorner, par, smooth_tail, sig_tail, dxs, dys, rnorm, phis, edge, mid, taus_tail):
+    total[...] = smooth_slab(block, core, dens.shape[0], GROUP_MAIN[0], smooth, taus, softs, pixo)
+
+
+def main_shade_kernel(smooth, taus, softs, pixo, total, dens, pix, zrecv, xrecv, xcorner, par, smooth_tail, softs_tail, dxs, dys, rnorm, phis, edge, mid, taus_tail):
     nz, rows, _ = dens.shape
     block = main_block(dens, pix, xrecv, zrecv, xcorner)
-    smooth, taus, sig = Joined(smooth, smooth_tail, nz), Joined(taus, taus_tail, nz - 1), Joined(sig, sig_tail, nz - 1)
-    whole = smooth_seam(block, nz, smooth, taus, sig, pixo, total[...])
+    smooth, taus, softs = Joined(smooth, smooth_tail, nz), Joined(taus, taus_tail, nz - 1), Joined(softs, softs_tail, nz - 1)
+    whole = smooth_seam(block, nz, smooth, taus, softs, pixo, total[...])
     shade_slab(rows, nz, GROUP_MAIN[1], whole, par, smooth, taus, dxs, dys, rnorm, phis, edge, mid, pixo)
 
 
-def prepare_block(band, depth, group, smooth, dxs, dys, rnorm, phis, edge, sig, pixo, palette, par, bx, by, bz, gained, damped, targets):
+def prepare_block(band, depth, group, smooth, dxs, dys, rnorm, phis, edge, softs, pixo, palette, par, bx, by, bz, gained, damped, targets):
     cols = smooth.shape[2]
     sign = 1.0 - 2.0 * pixo[2]
     weight = pixo[0] * (1.0 / (2 * depth))
@@ -364,7 +364,7 @@
         out = Stores()
         planes = [smooth[z0 + i, pl.ds(0, band)] for i in range(n + 2)]
         edges = [edge[z0 + i] for i in range(n + 1)]
-        rest = [(phis[z0 + i], rnorm[z0 + i], sig[z0 + i], dys[z0 + i], dxs[z0 + i]) for i in range(n)]
+        rest = [(phis[z0 + i], rnorm[z0 + i], softs[z0 + i], dys[z0 + i], dxs[z0 + i]) for i in range(n)]
         for i in range(n):
             phi, r, sg, dy, dx = rest[i]
             dz = planes[i + 2] - planes[i]
@@ -375,7 +375,7 @@
             out.put(by, z0 + i, p * ly - q * dy)
             out.put(bz, z0 + i, p * lz - q * dz)
             out.put(gained, z0 + i, w * (1.0 + phi))
-            out.put(damped, z0 + i, weight * sg)
+            out.put(damped, z0 + i, weight - weight * jnp.exp(-sg))
         out.flush()
         return carry
 
@@ -453,11 +453,11 @@
     in_groups(smooth_back, depth, group, 0, loop=band > 8)
 
 
-def main_prepare_kernel(smooth, sig, smooth_tail, sig_tail, dxs, dys, rnorm, phis, edge, pixo, palette, par, *out):
+def main_prepare_kernel(smooth, softs, smooth_tail, softs_tail, dxs, dys, rnorm, phis, edge, pixo, palette, par, *out):
     nz, rows, _ = dxs.shape
     nz = nz - 2
-    smooth, sig = Joined(smooth, smooth_tail, nz), Joined(sig, sig_tail, nz - 1)
-    prepare_block(rows, nz, GROUP_MAIN[2], smooth, dxs, dys, rnorm, phis, edge, sig, pixo, palette, par, *out)
+    smooth, softs = Joined(smooth, smooth_tail, nz), Joined(softs, softs_tail, nz - 1)
+    prepare_block(rows, nz, GROUP_MAIN[2], smooth, dxs, dys, rnorm, phis, edge, softs, pixo, palette, par, *out)
 
 
 def main_backward_kernel(smooth, smooth_tail, *refs):
@@ -568,17 +568,17 @@
         )
 
     parts = residuals(rows)
-    smooth, taus, sig, pixo, total = call(
+    smooth, taus, softs, pixo, total = call(
         main_smooth_kernel,
         (sds(nz, rows + 8, cols), sds(nz - 1, rows, cols), sds(nz - 1, rows, cols), parts[8], sds(rows, cols)),
         (dens, pix, xrecv),
         [VMEM] * 3,
     )
     xcorner, total = lax.optimization_barrier((xcorner, total))
-    smooth_tail, sig_tail, dxs, dys, rnorm, phis, edge, mid = call(
+    smooth_tail, softs_tail, dxs, dys, rnorm, phis, edge, mid = call(
         main_shade_kernel,
         (sds(4, rows + 8, cols), sds(3, rows, cols), *parts[1:6], parts[7]),
-        (smooth, taus, sig, pixo, total, dens, pix, zrecv, xrecv, xcorner, par),
+        (smooth, taus, softs, pixo, total, dens, pix, zrecv, xrecv, xcorner, par),
         [VMEM] * 11,
         scratch=[pltpu.VMEM((3, rows, cols), F32)],
     )
@@ -590,7 +590,7 @@
     ready = call(
         main_prepare_kernel,
         prepared(rows),
-        (smooth, sig, smooth_tail, sig_tail, dxs, dys, rnorm, phis, edge, pixo, pal, par),
+        (smooth, softs, smooth_tail, softs_tail, dxs, dys, rnorm, phis, edge, pixo, pal, par),
         [VMEM] * 12,
     )
     near_image, grads = call(
@@ -600,7 +600,7 @@
         [VMEM] * 14,
     )
     lrecv, near_image = lax.optimization_barrier((lrecv, near_image))
-    smooth, dxs, dys, rnorm, phis, edge, sig, mid, pixo = call(
+    smooth, dxs, dys, rnorm, phis, edge, softs, mid, pixo = call(
         far_forward_kernel,
         residuals(8),
         (dens, pix, zrecv, lrecv, par),
@@ -613,7 +613,7 @@
     ready = call(
         far_prepare_kernel,
         prepared(8),
-        (smooth, dxs, dys, rnorm, phis, edge, sig, pixo, pal, par),
+        (smooth, dxs, dys, rnorm, phis, edge, softs, pixo, pal, par),
         [VMEM] * 10,
     )
     picture, grad = call(

time: 18.1 us -> 18.1 us (level)
  transfers between devices with their start and end apart: 6 -> 6, of which waited for: 4 -> 5; matrix products, arithmetic and copies ran while one was open for 0% -> 0% of each run, Pallas kernels for 19% -> 20%
where the time goes in v9:
time: 18.1 us; the launch traced here: 17.9 us
  starting transfers between devices  7.62 us (42%)
  Pallas kernels  6.61 us (37%)
  waiting for transfers between devices  2.8 us (15%)
  between operations  0.72 us (4%)
    pallas_call x11, Pallas kernels, call(): pl.pallas_call(kernel, out_shape=outs, in_specs=specs, out_specs=out_spec...  6.61 us
    ppermute x1, starting transfers between devices, shards(): lrecv = lax.ppermute(lmsg, 'tile', far)  3 us
    ppermute x2, starting transfers between devices, shards(): theirs = lax.ppermute(mid, 'depth', swap)  1.69 us
    ppermute x1, starting transfers between devices, shards(): xrecv = lax.ppermute(xmsg, 'tile', near)  1.28 us
    ppermute x1, waiting for transfers between devices, shards(): lrecv = lax.ppermute(lmsg, 'tile', far)  1.26 us
    ppermute x1, starting transfers between devices, shards(): zrecv = lax.ppermute(zmsg, 'depth', swap)  0.96 us
    ppermute x1, waiting for transfers between devices, shards(): zrecv = lax.ppermute(zmsg, 'depth', swap)  0.9 us
    ppermute x1, starting transfers between devices, shards(): xcorner = lax.ppermute(xrecv[:HALO], 'depth', swap)  0.7 us
  transfers between devices with their start and end apart: 6, of which 5 were waited for; matrix products, arithmetic and copies ran while one was open for 0% of the time, Pallas kernels for 20%

profile of v9, /device:TPU:9, one launch (start us, length us, event | category | flops | bytes accessed | tf_op | source)
XLA Modules:
  0.0 17.9 jit_solution(17086253031927971680)
XLA Ops:
  0.6 0.0 copy-start
  0.6 1.0 %shard_map.86 = (f32[4,16,256]{2,1,0:T(8,128)S(1)}, f32[3,16,256]{2,1,0:T(8,128)S(1)}, f32[3,128]{1,0:T(4,128)S(1)}, f32[15,8,128]{2,1,0:T(8,128)S(1)}) custom-call(f32[32,16,256]{2,1,0:T(8,128)} %dens.7, f32[16,256]{1,0:T(8,128)} %absorb_h.1, s32[16,256]{1,0:T(8,128)} %ids_h.1, s32[16]{0:T(128)} %view_h.1, f32[3,128]{1,0:T(4,128)} %pal_h.1, f32[3,4]{1,0:T(4,128)} %coef_h.1, ...), custom_call_target="tpu_custom_call" | custom-call | tf_op jit(solution)/shard_map/pallas_call | solution.py:22
  1.6 0.1 copy-done
  1.8 0.1 shard_map.87
  1.9 1.3 %collective-permute-start.2 = (f32[34,4,256]{2,1,0:T(4,128)S(1)}, f32[34,4,256]{2,1,0:T(4,128)S(1)}, u32[]{:S(2)}, u32[]{:S(2)}) collective-permute-start(f32[34,4,256]{2,1,0:T(4,128)S(1)} %get-tuple-element.55), channel_id=1, source_target_pairs={{0,2},{2,0},{4,6},{6,4},{8,10},{10,8},{12,14},{14,12},{16,18},{18,... | collective-permute-start | bytes 417800 | tf_op jit(solution)/shard_map/ppermute | solution.py:554
  3.1 1.0 %collective-permute-start = (f32[4,16,256]{2,1,0:T(8,128)S(1)}, f32[4,16,256]{2,1,0:T(8,128)S(1)}, u32[]{:S(2)}, u32[]{:S(2)}) collective-permute-start(f32[4,16,256]{2,1,0:T(8,128)S(1)} %get-tuple-element.53), channel_id=1, source_target_pairs={{0,1},{1,0},{2,3},{3,2},{4,5},{5,4},{6,7},{7,6},{8,9},{9,8},{10,11... | collective-permute-start | bytes 196616 | tf_op jit(solution)/shard_map/ppermute | solution.py:553
  4.1 0.9 %collective-permute-done.zrecv = f32[4,16,256]{2,1,0:T(8,128)S(1)} collective-permute-done((f32[4,16,256]{2,1,0:T(8,128)S(1)}, f32[4,16,256]{2,1,0:T(8,128)S(1)}, u32[]{:S(2)}, u32[]{:S(2)}) %collective-permute-start) | collective-permute-done | bytes 65568 | tf_op jit(solution)/shard_map/ppermute | solution.py:553
  5.0 3.0 %collective-permute-start.1 = (f32[36,4,256]{2,1,0:T(4,128)S(1)}, f32[36,4,256]{2,1,0:T(4,128)S(1)}, u32[]{:S(2)}, u32[]{:S(2)}) collective-permute-start(f32[36,4,256]{2,1,0:T(4,128)S(1)} %shard_map.88), channel_id=1, source_target_pairs={{2,4},{4,2},{6,8},{8,6},{10,12},{12,10},{14,16},{16,14},{18,20},{2... | collective-permute-start | bytes 442376 | tf_op jit(solution)/shard_map/ppermute | solution.py:556
  8.0 0.0 collective-permute-done.2.xrecv
  8.0 0.7 %collective-permute-start.3 = (f32[4,4,256]{2,1,0:T(4,128)S(1)}, f32[4,4,256]{2,1,0:T(4,128)S(1)}, u32[]{:S(2)}, u32[]{:S(2)}) collective-permute-start(f32[4,4,256]{2,1,0:T(4,128)S(1)} %slice.4), channel_id=1, source_target_pairs={{0,1},{1,0},{2,3},{3,2},{4,5},{5,4},{6,7},{7,6},{8,9},{9,8},{10,11... | collective-permute-start | bytes 49160 | tf_op jit(solution)/shard_map/ppermute | solution.py:557
  8.7 0.7 %shard_map.89 = (f32[32,24,256]{2,1,0:T(8,128)S(1)}, f32[31,16,256]{2,1,0:T(8,128)S(1)}, f32[31,16,256]{2,1,0:T(8,128)S(1)}, f32[3,16,256]{2,1,0:T(8,128)S(1)}, f32[16,256]{1,0:T(8,128)S(1)}) custom-call(f32[32,16,256]{2,1,0:T(8,128)S(1)} %copy-done, f32[3,16,256]{2,1,0:T(8,128)S(1)} %get-tuple-element.52.pix, f32[34,4,256]{2,1,0:T(4,128)S(1)} %collective-permute-done.2.xrecv), custom_call_target="tpu_custom_call" | custom-call | tf_op jit(solution)/shard_map/pallas_call | solution.py:22
  9.5 0.1 collective-permute-done.3.xcorner
  9.6 0.8 %shard_map.90 = (f32[4,24,256]{2,1,0:T(8,128)S(1)}, f32[3,16,256]{2,1,0:T(8,128)S(1)}, f32[34,16,256]{2,1,0:T(8,128)S(1)}, f32[34,16,256]{2,1,0:T(8,128)S(1)}, f...) custom-call(f32[32,24,256]{2,1,0:T(8,128)S(1)} %get-tuple-element.56, ...), custom_call_target="tpu_custom_call" | custom-call | tf_op jit(solution)/shard_map/pallas_call | solution.py:22
  10.4 0.4 %collective-permute-start.4 = (f32[4,16,256]{2,1,0:T(8,128)S(1)}, f32[4,16,256]{2,1,0:T(8,128)S(1)}, u32[]{:S(2)}, u32[]{:S(2)}) collective-permute-start(f32[4,16,256]{2,1,0:T(8,128)S(1)} %get-tuple-element.78.refs_8_), channel_id=1, source_target_pairs={{0,1},{1,0},{2,3},{3,2},{4,5},{5,4},{6,7},{7,6},{8,9},{9,8},{10,11... | collective-permute-start | bytes 196616 | tf_op jit(solution)/shard_map/ppermute | solution.py:585
  10.8 0.5 %shard_map.91 = (f32[34,16,256]{2,1,0:T(8,128)S(1)}, f32[34,16,256]{2,1,0:T(8,128)S(1)}, f32[34,16,256]{2,1,0:T(8,128)S(1)}, f32[34,16,256]{2,1,0:T(8,128)S(1)},...) custom-call(f32[32,24,256]{2,1,0:T(8,128)S(1)} %get-tuple-element.56.smooth, ...), custom_call_target="tpu_custom_call" | custom-call | tf_op jit(solution)/shard_map/pallas_call | solution.py:22
  11.3 0.4 %collective-permute-done.4.refs_10_ = f32[4,16,256]{2,1,0:T(8,128)S(1)} collective-permute-done((f32[4,16,256]{2,1,0:T(8,128)S(1)}, f32[4,16,256]{2,1,0:T(8,128)S(1)}, u32[]{:S(2)}, u32[]{:S(2)}) %collective-permute-start.4) | collective-permute-done | bytes 65568 | tf_op jit(solution)/shard_map/ppermute | solution.py:585
  11.7 0.8 %shard_map.92 = (f32[3,16,256]{2,1,0:T(8,128)S(1)}, f32[34,16,256]{2,1,0:T(8,128)S(1)}) custom-call(f32[32,24,256]{2,1,0:T(8,128)S(1)} %get-tuple-element.56.smooth, f32[4,24,256]{2,1,0:T(8,128)S(1)} %get-tuple-element.64.smooth_tail, f32[34,16,256]{2,1,0:T(8,128)S(1)} %get-tuple-element.65.phis.refs_0_, f32[35,16,256]{2,1,0:T(8,128)S(1)} %get-tuple-element.66.edge.refs_1_, ...), custom_call_target="tpu_custom_call" | custom-call | tf_op jit(solution)/shard_map/pallas_call | solution.py:22
  12.5 1.3 %collective-permute-done.1.lrecv = f32[36,4,256]{2,1,0:T(4,128)S(1)} collective-permute-done((f32[36,4,256]{2,1,0:T(4,128)S(1)}, f32[36,4,256]{2,1,0:T(4,128)S(1)}, u32[]{:S(2)}, u32[]{:S(2)}) %collective-permute-start.1) | collective-permute-done | bytes 147488 | tf_op jit(solution)/shard_map/ppermute | solution.py:556
  13.7 0.8 %shard_map.93 = (f32[36,16,256]{2,1,0:T(8,128)S(1)}, f32[34,8,256]{2,1,0:T(8,128)S(1)}, f32[34,8,256]{2,1,0:T(8,128)S(1)}, f32[34,8,256]{2,1,0:T(8,128)S(1)}, f3...) custom-call(f32[32,16,256]{2,1,0:T(8,128)S(1)} %copy-done, ...), custom_call_target="tpu_custom_call" | custom-call | tf_op jit(solution)/shard_map/pallas_call | solution.py:22
  14.5 1.3 %collective-permute-start.5 = (f32[4,8,256]{2,1,0:T(8,128)S(1)}, f32[4,8,256]{2,1,0:T(8,128)S(1)}, u32[]{:S(2)}, u32[]{:S(2)}) collective-permute-start(f32[4,8,256]{2,1,0:T(8,128)S(1)} %get-tuple-element.97.refs_9_), channel_id=1, source_target_pairs={{0,1},{1,0},{2,3},{3,2},{4,5},{5,4},{6,7},{7,6},{8,9},{9,8},{10,11... | collective-permute-start | bytes 98312 | tf_op jit(solution)/shard_map/ppermute | solution.py:610
  15.8 0.4 %shard_map.95 = (f32[32,16,256]{2,1,0:T(8,128)S(1)}, f32[3,16,256]{2,1,0:T(8,128)S(1)}) custom-call(f32[34,16,256]{2,1,0:T(8,128)S(1)} %get-tuple-element.98.grads, f32[3,16,256]{2,1,0:T(8,128)S(1)} %get-tuple-element.99.image), custom_call_target="tpu_custom_call" | custom-call | tf_op jit(solution)/shard_map/pallas_call | solution.py:22
  16.2 0.3 %shard_map.94 = (f32[34,8,256]{2,1,0:T(8,128)S(1)}, f32[34,8,256]{2,1,0:T(8,128)S(1)}, f32[34,8,256]{2,1,0:T(8,128)S(1)}, f32[34,8,256]{2,1,0:T(8,128)S(1)}, f32...) custom-call(f32[36,16,256]{2,1,0:T(8,128)S(1)} %get-tuple-element.81.smooth.refs_0_, ...), custom_call_target="tpu_custom_call" | custom-call | tf_op jit(solution)/shard_map/pallas_call | solution.py:22
  16.5 0.2 collective-permute-done.5.refs_11_
  16.7 1.2 %shard_map.96 = (f32[3,8,256]{2,1,0:T(8,128)}, f32[32,16,256]{2,1,0:T(8,128)}) custom-call(f32[36,16,256]{2,1,0:T(8,128)S(1)} %get-tuple-element.81.smooth.refs_0_, f32[34,8,256]{2,1,0:T(8,128)S(1)} %get-tuple-element.82.refs_3_.refs_1_, f32[35,8,256]{2,1,0:T(8,128)S(1)} %get-tuple-element.83.refs_4_.refs_2_, f32[34,8,256]{2,1,0:T(8,128)S(1)} %get-tuple-element.91.refs_3_, ...), custom_call_target="tpu_custom_call" | custom-call | tf_op jit(solution)/shard_map/pallas_call | solution.py:22
  (2 shorter events, 0.0 us)
Async XLA Ops:
  0.6 1.2 %copy-start = (f32[32,16,256]{2,1,0:T(8,128)S(1)}, f32[32,16,256]{2,1,0:T(8,128)}, u32[]{:S(2)}) copy-start(f32[32,16,256]{2,1,0:T(8,128)} %dens.7) | copy-start | bytes 1572868
  1.9 6.2 %collective-permute-start.2 = (f32[34,4,256]{2,1,0:T(4,128)S(1)}, f32[34,4,256]{2,1,0:T(4,128)S(1)}, u32[]{:S(2)}, u32[]{:S(2)}) collective-permute-start(f32[34,4,256]{2,1,0:T(4,128)S(1)} %get-tuple-element.55), channel_id=1, source_target_pairs={{0,2},{2,0},{4,6},{6,4},{8,10},{10,8},{12,14},{14,12},{16,18},{18,... | collective-permute-start | bytes 417800 | tf_op jit(solution)/shard_map/ppermute | solution.py:554
  3.1 1.9 %collective-permute-start = (f32[4,16,256]{2,1,0:T(8,128)S(1)}, f32[4,16,256]{2,1,0:T(8,128)S(1)}, u32[]{:S(2)}, u32[]{:S(2)}) collective-permute-start(f32[4,16,256]{2,1,0:T(8,128)S(1)} %get-tuple-element.53), channel_id=1, source_target_pairs={{0,1},{1,0},{2,3},{3,2},{4,5},{5,4},{6,7},{7,6},{8,9},{9,8},{10,11... | collective-permute-start | bytes 196616 | tf_op jit(solution)/shard_map/ppermute | solution.py:553
  5.0 8.7 %collective-permute-start.1 = (f32[36,4,256]{2,1,0:T(4,128)S(1)}, f32[36,4,256]{2,1,0:T(4,128)S(1)}, u32[]{:S(2)}, u32[]{:S(2)}) collective-permute-start(f32[36,4,256]{2,1,0:T(4,128)S(1)} %shard_map.88), channel_id=1, source_target_pairs={{2,4},{4,2},{6,8},{8,6},{10,12},{12,10},{14,16},{16,14},{18,20},{2... | collective-permute-start | bytes 442376 | tf_op jit(solution)/shard_map/ppermute | solution.py:556
  8.0 1.5 %collective-permute-start.3 = (f32[4,4,256]{2,1,0:T(4,128)S(1)}, f32[4,4,256]{2,1,0:T(4,128)S(1)}, u32[]{:S(2)}, u32[]{:S(2)}) collective-permute-start(f32[4,4,256]{2,1,0:T(4,128)S(1)} %slice.4), channel_id=1, source_target_pairs={{0,1},{1,0},{2,3},{3,2},{4,5},{5,4},{6,7},{7,6},{8,9},{9,8},{10,11... | collective-permute-start | bytes 49160 | tf_op jit(solution)/shard_map/ppermute | solution.py:557
  10.4 1.3 %collective-permute-start.4 = (f32[4,16,256]{2,1,0:T(8,128)S(1)}, f32[4,16,256]{2,1,0:T(8,128)S(1)}, u32[]{:S(2)}, u32[]{:S(2)}) collective-permute-start(f32[4,16,256]{2,1,0:T(8,128)S(1)} %get-tuple-element.78.refs_8_), channel_id=1, source_target_pairs={{0,1},{1,0},{2,3},{3,2},{4,5},{5,4},{6,7},{7,6},{8,9},{9,8},{10,11... | collective-permute-start | bytes 196616 | tf_op jit(solution)/shard_map/ppermute | solution.py:585
  14.5 2.1 %collective-permute-start.5 = (f32[4,8,256]{2,1,0:T(8,128)S(1)}, f32[4,8,256]{2,1,0:T(8,128)S(1)}, u32[]{:S(2)}, u32[]{:S(2)}) collective-permute-start(f32[4,8,256]{2,1,0:T(8,128)S(1)} %get-tuple-element.97.refs_9_), channel_id=1, source_target_pairs={{0,1},{1,0},{2,3},{3,2},{4,5},{5,4},{6,7},{7,6},{8,9},{9,8},{10,11... | collective-permute-start | bytes 98312 | tf_op jit(solution)/shard_map/ppermute | solution.py:610

commit v10 on v7

--- a/solution.py
+++ b/solution.py
@@ -92,14 +92,15 @@
     return jnp.concatenate([t] * (rows // t.shape[0]), axis=0)
 
 
-def fetch_kernel(dens_h, absorb_h, ids_h, view_h, pal_h, coef_h, light_h, zmsg, dens, pix, pal, par, ids, view, coef, light, sem):
-    nz, rows, cols = dens.shape
+def fetch_kernel(dens_h, absorb_h, ids_h, view_h, pal_h, coef_h, light_h, zmsg, pix, pal, par, ids, view, coef, light, sem):
+    nz, rows, cols = dens_h.shape
     core, _ = where_am_i()
-    pairs = ((dens_h, dens), (view_h, view), (ids_h, ids), (absorb_h, pix.at[0]), (coef_h, coef), (light_h, light), (pal_h, pal))
+    seam = [(dens_h.at[local_plane(core, nz, nz - 1 - j)], zmsg.at[j]) for j in range(HALO)]
+    pairs = (*seam, (view_h, view), (ids_h, ids), (absorb_h, pix.at[0]), (coef_h, coef), (light_h, light), (pal_h, pal))
     copies = [pltpu.make_async_copy(a, b, sem.at[i]) for i, (a, b) in enumerate(pairs)]
     for c in copies:
         c.start()
-    for c in copies[1:]:
+    for c in copies[HALO:]:
         c.wait()
     row = lax.broadcasted_iota(jnp.int32, (rows, cols), 0)
     seen = jnp.zeros((rows, cols), F32)
@@ -114,9 +115,8 @@
         if i == 0:
             value = jnp.where(core == 0, value, -value)
         par[12 + i] = jnp.full(par.shape[1:], value)
-    copies[0].wait()
-    for j in range(HALO):
-        zmsg[j] = dens[local_plane(core, nz, nz - 1 - j)]
+    for c in copies[:HALO]:
+        c.wait()
 
 
 def edges_kernel(dens, pix, xmsg, lmsg):
@@ -551,10 +551,11 @@
     nz, rows, cols = density.shape
     tiles = lax.axis_size("tile")
     sds = resident
-
-    zmsg, dens, pix, pal, par = call(
+    dens = density
+
+    zmsg, pix, pal, par = call(
         fetch_kernel,
-        (sds(HALO, rows, cols), sds(nz, rows, cols), sds(PIX, rows, cols), sds(*palette.shape), sds(15, 8, 128)),
+        (sds(HALO, rows, cols), sds(PIX, rows, cols), sds(*palette.shape), sds(15, 8, 128)),
         (density, absorption, target_ids, view_dir, palette, emission_coef, light),
         [HBM] * 7,
         scratch=[
@@ -562,7 +563,7 @@
             pltpu.SMEM(view_dir.shape, jnp.int32),
             pltpu.SMEM(emission_coef.shape, F32),
             pltpu.SMEM(light.shape, F32),
-            pltpu.SemaphoreType.DMA((7,)),
+            pltpu.SemaphoreType.DMA((6 + HALO,)),
         ],
     )
     xmsg, lmsg = call(edges_kernel, (sds(nz + 2, HALO, cols), sds(nz + 2, HALO, cols)), (dens, pix), [VMEM] * 2)

time: 18.1 us -> 18.1 us (level)
  no operation moved by 1% of the time
where the time goes in v10:
time: 18.1 us; the launch traced here: 18 us
  starting transfers between devices  7.62 us (42%)
  Pallas kernels  6.42 us (35%)
  waiting for transfers between devices  3.06 us (17%)
  between operations  0.73 us (4%)
    pallas_call x11, Pallas kernels, call(): pl.pallas_call(kernel, out_shape=outs, in_specs=specs, out_specs=out_spec...  6.42 us
    ppermute x1, starting transfers between devices, shards(): lrecv = lax.ppermute(lmsg, 'tile', far)  3 us
    ppermute x2, starting transfers between devices, shards(): theirs = lax.ppermute(mid, 'depth', swap)  1.69 us
    ppermute x1, waiting for transfers between devices, shards(): lrecv = lax.ppermute(lmsg, 'tile', far)  1.64 us
    ppermute x1, starting transfers between devices, shards(): xrecv = lax.ppermute(xmsg, 'tile', near)  1.28 us
    ppermute x1, starting transfers between devices, shards(): zrecv = lax.ppermute(zmsg, 'depth', swap)  0.96 us
    ppermute x1, waiting for transfers between devices, shards(): zrecv = lax.ppermute(zmsg, 'depth', swap)  0.9 us
    ppermute x1, starting transfers between devices, shards(): xcorner = lax.ppermute(xrecv[:HALO], 'depth', swap)  0.7 us
  transfers between devices with their start and end apart: 6, of which 3 were waited for; matrix products, arithmetic and copies ran while one was open for 0% of the time, Pallas kernels for 18%

profile of v10, /device:TPU:9, one launch (start us, length us, event | category | flops | bytes accessed | tf_op | source)
XLA Modules:
  0.0 18.0 jit_solution(7920975655287424514)
XLA Ops:
  0.6 0.0 copy-start
  0.6 1.0 %shard_map.86 = (f32[4,16,256]{2,1,0:T(8,128)S(1)}, f32[3,16,256]{2,1,0:T(8,128)S(1)}, f32[3,128]{1,0:T(4,128)S(1)}, f32[15,8,128]{2,1,0:T(8,128)S(1)}) custom-call(f32[32,16,256]{2,1,0:T(8,128)} %dens.7, f32[16,256]{1,0:T(8,128)} %absorb_h.1, s32[16,256]{1,0:T(8,128)} %ids_h.1, s32[16]{0:T(128)} %view_h.1, f32[3,128]{1,0:T(4,128)} %pal_h.1, f32[3,4]{1,0:T(4,128)} %coef_h.1, ...), custom_call_target="tpu_custom_call" | custom-call | tf_op jit(solution)/shard_map/pallas_call | solution.py:22
  1.6 0.1 copy-done
  1.8 0.1 shard_map.87
  1.9 1.3 %collective-permute-start.2 = (f32[34,4,256]{2,1,0:T(4,128)S(1)}, f32[34,4,256]{2,1,0:T(4,128)S(1)}, u32[]{:S(2)}, u32[]{:S(2)}) collective-permute-start(f32[34,4,256]{2,1,0:T(4,128)S(1)} %get-tuple-element.57), channel_id=1, source_target_pairs={{0,2},{2,0},{4,6},{6,4},{8,10},{10,8},{12,14},{14,12},{16,18},{18,... | collective-permute-start | bytes 417800 | tf_op jit(solution)/shard_map/ppermute | solution.py:574
  3.1 1.0 %collective-permute-start = (f32[4,16,256]{2,1,0:T(8,128)S(1)}, f32[4,16,256]{2,1,0:T(8,128)S(1)}, u32[]{:S(2)}, u32[]{:S(2)}) collective-permute-start(f32[4,16,256]{2,1,0:T(8,128)S(1)} %get-tuple-element.55), channel_id=1, source_target_pairs={{0,1},{1,0},{2,3},{3,2},{4,5},{5,4},{6,7},{7,6},{8,9},{9,8},{10,11... | collective-permute-start | bytes 196616 | tf_op jit(solution)/shard_map/ppermute | solution.py:573
  4.1 0.9 %collective-permute-done.zrecv = f32[4,16,256]{2,1,0:T(8,128)S(1)} collective-permute-done((f32[4,16,256]{2,1,0:T(8,128)S(1)}, f32[4,16,256]{2,1,0:T(8,128)S(1)}, u32[]{:S(2)}, u32[]{:S(2)}) %collective-permute-start) | collective-permute-done | bytes 65568 | tf_op jit(solution)/shard_map/ppermute | solution.py:573
  5.0 3.0 %collective-permute-start.1 = (f32[36,4,256]{2,1,0:T(4,128)S(1)}, f32[36,4,256]{2,1,0:T(4,128)S(1)}, u32[]{:S(2)}, u32[]{:S(2)}) collective-permute-start(f32[36,4,256]{2,1,0:T(4,128)S(1)} %shard_map.88), channel_id=1, source_target_pairs={{2,4},{4,2},{6,8},{8,6},{10,12},{12,10},{14,16},{16,14},{18,20},{2... | collective-permute-start | bytes 442376 | tf_op jit(solution)/shard_map/ppermute | solution.py:576
  8.0 0.0 collective-permute-done.2.xrecv
  8.0 0.7 %collective-permute-start.3 = (f32[4,4,256]{2,1,0:T(4,128)S(1)}, f32[4,4,256]{2,1,0:T(4,128)S(1)}, u32[]{:S(2)}, u32[]{:S(2)}) collective-permute-start(f32[4,4,256]{2,1,0:T(4,128)S(1)} %slice.4), channel_id=1, source_target_pairs={{0,1},{1,0},{2,3},{3,2},{4,5},{5,4},{6,7},{7,6},{8,9},{9,8},{10,11... | collective-permute-start | bytes 49160 | tf_op jit(solution)/shard_map/ppermute | solution.py:577
  8.7 0.8 %shard_map.89 = (f32[32,24,256]{2,1,0:T(8,128)S(1)}, f32[31,16,256]{2,1,0:T(8,128)S(1)}, f32[31,16,256]{2,1,0:T(8,128)S(1)}, f32[3,16,256]{2,1,0:T(8,128)S(1)}, f32[16,256]{1,0:T(8,128)S(1)}) custom-call(f32[32,16,256]{2,1,0:T(8,128)S(1)} %copy-done, f32[3,16,256]{2,1,0:T(8,128)S(1)} %get-tuple-element.54.pix, f32[34,4,256]{2,1,0:T(4,128)S(1)} %collective-permute-done.2.xrecv), custom_call_target="tpu_custom_call" | custom-call | tf_op jit(solution)/shard_map/pallas_call | solution.py:22
  9.5 0.0 collective-permute-done.3.xcorner
  9.6 0.8 %shard_map.90 = (f32[4,24,256]{2,1,0:T(8,128)S(1)}, f32[3,16,256]{2,1,0:T(8,128)S(1)}, f32[34,16,256]{2,1,0:T(8,128)S(1)}, f32[34,16,256]{2,1,0:T(8,128)S(1)}, f...) custom-call(f32[32,24,256]{2,1,0:T(8,128)S(1)} %get-tuple-element.58, ...), custom_call_target="tpu_custom_call" | custom-call | tf_op jit(solution)/shard_map/pallas_call | solution.py:22
  10.4 0.4 %collective-permute-start.4 = (f32[4,16,256]{2,1,0:T(8,128)S(1)}, f32[4,16,256]{2,1,0:T(8,128)S(1)}, u32[]{:S(2)}, u32[]{:S(2)}) collective-permute-start(f32[4,16,256]{2,1,0:T(8,128)S(1)} %get-tuple-element.80.mid), channel_id=1, source_target_pairs={{0,1},{1,0},{2,3},{3,2},{4,5},{5,4},{6,7},{7,6},{8,9},{9,8},{10,11... | collective-permute-start | bytes 196616 | tf_op jit(solution)/shard_map/ppermute | solution.py:605
  10.8 0.4 %shard_map.91 = (f32[34,16,256]{2,1,0:T(8,128)S(1)}, f32[34,16,256]{2,1,0:T(8,128)S(1)}, f32[34,16,256]{2,1,0:T(8,128)S(1)}, f32[34,16,256]{2,1,0:T(8,128)S(1)},...) custom-call(f32[32,24,256]{2,1,0:T(8,128)S(1)} %get-tuple-element.58.smooth, ...), custom_call_target="tpu_custom_call" | custom-call | tf_op jit(solution)/shard_map/pallas_call | solution.py:22
  11.2 0.5 %collective-permute-done.4.theirs = f32[4,16,256]{2,1,0:T(8,128)S(1)} collective-permute-done((f32[4,16,256]{2,1,0:T(8,128)S(1)}, f32[4,16,256]{2,1,0:T(8,128)S(1)}, u32[]{:S(2)}, u32[]{:S(2)}) %collective-permute-start.4) | collective-permute-done | bytes 65568 | tf_op jit(solution)/shard_map/ppermute | solution.py:605
  11.7 0.4 %shard_map.92 = (f32[3,16,256]{2,1,0:T(8,128)S(1)}, f32[17,16,256]{2,1,0:T(8,128)S(1)}, f32[7,16,256]{2,1,0:T(8,128)S(1)}) custom-call(f32[32,24,256]{2,1,0:T(8,128)S(1)} %get-tuple-element.58.smooth, f32[34,16,256]{2,1,0:T(8,128)S(1)} %get-tuple-element.66.phis, f32[35,16,256]{2,1,0:T(8,128)S(1)} %get-tuple-element.67.edge, ...), custom_call_target="tpu_custom_call" | custom-call | tf_op jit(solution)/shard_map/pallas_call | solution.py:22
  12.1 1.6 %collective-permute-done.1.lrecv = f32[36,4,256]{2,1,0:T(4,128)S(1)} collective-permute-done((f32[36,4,256]{2,1,0:T(4,128)S(1)}, f32[36,4,256]{2,1,0:T(4,128)S(1)}, u32[]{:S(2)}, u32[]{:S(2)}) %collective-permute-start.1) | collective-permute-done | bytes 147488 | tf_op jit(solution)/shard_map/ppermute | solution.py:576
  13.7 0.8 %shard_map.93 = (f32[36,16,256]{2,1,0:T(8,128)S(1)}, f32[34,8,256]{2,1,0:T(8,128)S(1)}, f32[34,8,256]{2,1,0:T(8,128)S(1)}, f32[34,8,256]{2,1,0:T(8,128)S(1)}, f3...) custom-call(f32[32,16,256]{2,1,0:T(8,128)S(1)} %copy-done, ...), custom_call_target="tpu_custom_call" | custom-call | tf_op jit(solution)/shard_map/pallas_call | solution.py:22
  14.6 1.3 %collective-permute-start.5 = (f32[4,8,256]{2,1,0:T(8,128)S(1)}, f32[4,8,256]{2,1,0:T(8,128)S(1)}, u32[]{:S(2)}, u32[]{:S(2)}) collective-permute-start(f32[4,8,256]{2,1,0:T(8,128)S(1)} %get-tuple-element.100.refs_9_), channel_id=1, source_target_pairs={{0,1},{1,0},{2,3},{3,2},{4,5},{5,4},{6,7},{7,6},{8,9},{9,8},{10,11... | collective-permute-start | bytes 98312 | tf_op jit(solution)/shard_map/ppermute | solution.py:632
  15.8 0.7 %shard_map.95 = (f32[32,16,256]{2,1,0:T(8,128)S(1)}, f32[3,16,256]{2,1,0:T(8,128)S(1)}) custom-call(f32[7,16,256]{2,1,0:T(8,128)S(1)} %get-tuple-element.101.state, f32[17,16,256]{2,1,0:T(8,128)S(1)} %get-tuple-element.102.early, f32[32,24,256]{2,1,0:T(8,128)S(1)} %get-tuple-element.58.smooth, f32[4,24,256]{2,1,0:T(8,128)S(1)} %get-tuple-element.68.smooth_tail, ...), custom_call_target="tpu_custom_call" | custom-call | tf_op jit(solution)/shard_map/pallas_call | solution.py:22
  16.5 0.2 %shard_map.94 = (f32[34,8,256]{2,1,0:T(8,128)S(1)}, f32[34,8,256]{2,1,0:T(8,128)S(1)}, f32[34,8,256]{2,1,0:T(8,128)S(1)}, f32[34,8,256]{2,1,0:T(8,128)S(1)}, f32...) custom-call(f32[36,16,256]{2,1,0:T(8,128)S(1)} %get-tuple-element.83.smooth.refs_0_, ...), custom_call_target="tpu_custom_call" | custom-call | tf_op jit(solution)/shard_map/pallas_call | solution.py:22
  16.7 0.0 collective-permute-done.5.refs_11_
  16.7 1.2 %shard_map.96 = (f32[3,8,256]{2,1,0:T(8,128)}, f32[32,16,256]{2,1,0:T(8,128)}) custom-call(f32[36,16,256]{2,1,0:T(8,128)S(1)} %get-tuple-element.83.smooth.refs_0_, f32[34,8,256]{2,1,0:T(8,128)S(1)} %get-tuple-element.84.refs_3_.refs_1_, f32[35,8,256]{2,1,0:T(8,128)S(1)} %get-tuple-element.85.refs_4_.refs_2_, f32[34,8,256]{2,1,0:T(8,128)S(1)} %get-tuple-element.94.refs_3_, ...), custom_call_target="tpu_custom_call" | custom-call | tf_op jit(solution)/shard_map/pallas_call | solution.py:22
  (2 shorter events, 0.0 us)
Async XLA Ops:
  0.6 1.2 %copy-start = (f32[32,16,256]{2,1,0:T(8,128)S(1)}, f32[32,16,256]{2,1,0:T(8,128)}, u32[]{:S(2)}) copy-start(f32[32,16,256]{2,1,0:T(8,128)} %dens.7) | copy-start | bytes 1572868
  1.9 6.2 %collective-permute-start.2 = (f32[34,4,256]{2,1,0:T(4,128)S(1)}, f32[34,4,256]{2,1,0:T(4,128)S(1)}, u32[]{:S(2)}, u32[]{:S(2)}) collective-permute-start(f32[34,4,256]{2,1,0:T(4,128)S(1)} %get-tuple-element.57), channel_id=1, source_target_pairs={{0,2},{2,0},{4,6},{6,4},{8,10},{10,8},{12,14},{14,12},{16,18},{18,... | collective-permute-start | bytes 417800 | tf_op jit(solution)/shard_map/ppermute | solution.py:574
  3.1 1.9 %collective-permute-start = (f32[4,16,256]{2,1,0:T(8,128)S(1)}, f32[4,16,256]{2,1,0:T(8,128)S(1)}, u32[]{:S(2)}, u32[]{:S(2)}) collective-permute-start(f32[4,16,256]{2,1,0:T(8,128)S(1)} %get-tuple-element.55), channel_id=1, source_target_pairs={{0,1},{1,0},{2,3},{3,2},{4,5},{5,4},{6,7},{7,6},{8,9},{9,8},{10,11... | collective-permute-start | bytes 196616 | tf_op jit(solution)/shard_map/ppermute | solution.py:573
  5.0 8.7 %collective-permute-start.1 = (f32[36,4,256]{2,1,0:T(4,128)S(1)}, f32[36,4,256]{2,1,0:T(4,128)S(1)}, u32[]{:S(2)}, u32[]{:S(2)}) collective-permute-start(f32[36,4,256]{2,1,0:T(4,128)S(1)} %shard_map.88), channel_id=1, source_target_pairs={{2,4},{4,2},{6,8},{8,6},{10,12},{12,10},{14,16},{16,14},{18,20},{2... | collective-permute-start | bytes 442376 | tf_op jit(solution)/shard_map/ppermute | solution.py:576
  8.0 1.5 %collective-permute-start.3 = (f32[4,4,256]{2,1,0:T(4,128)S(1)}, f32[4,4,256]{2,1,0:T(4,128)S(1)}, u32[]{:S(2)}, u32[]{:S(2)}) collective-permute-start(f32[4,4,256]{2,1,0:T(4,128)S(1)} %slice.4), channel_id=1, source_target_pairs={{0,1},{1,0},{2,3},{3,2},{4,5},{5,4},{6,7},{7,6},{8,9},{9,8},{10,11... | collective-permute-start | bytes 49160 | tf_op jit(solution)/shard_map/ppermute | solution.py:577
  10.4 1.3 %collective-permute-start.4 = (f32[4,16,256]{2,1,0:T(8,128)S(1)}, f32[4,16,256]{2,1,0:T(8,128)S(1)}, u32[]{:S(2)}, u32[]{:S(2)}) collective-permute-start(f32[4,16,256]{2,1,0:T(8,128)S(1)} %get-tuple-element.80.mid), channel_id=1, source_target_pairs={{0,1},{1,0},{2,3},{3,2},{4,5},{5,4},{6,7},{7,6},{8,9},{9,8},{10,11... | collective-permute-start | bytes 196616 | tf_op jit(solution)/shard_map/ppermute | solution.py:605
  14.6 2.2 %collective-permute-start.5 = (f32[4,8,256]{2,1,0:T(8,128)S(1)}, f32[4,8,256]{2,1,0:T(8,128)S(1)}, u32[]{:S(2)}, u32[]{:S(2)}) collective-permute-start(f32[4,8,256]{2,1,0:T(8,128)S(1)} %get-tuple-element.100.refs_9_), channel_id=1, source_target_pairs={{0,1},{1,0},{2,3},{3,2},{4,5},{5,4},{6,7},{7,6},{8,9},{9,8},{10,11... | collective-permute-start | bytes 98312 | tf_op jit(solution)/shard_map/ppermute | solution.py:632
